TPU v7x, 32 devices: a whole 2x2x4 slice. The times are simulated.
32 devices in a mesh: rep: 4 (over y, x), shard: 8 (over z, core).
Axes of the slice: x: 2, y: 2, z: 4, core: 2. Of those that a mesh axis runs over, the one named last changes fastest.
Arguments:
- layer_input: bfloat16 [16384, 1024], P(('rep', 'shard')), may hold values from -6 to 6
- encoder_states: bfloat16 [2048, 1024], P(('rep', 'shard')), may hold values from -6 to 6
- out_grad: bfloat16 [16384, 1024], P(('rep', 'shard')), may hold values from -6 to 6
- placement: int32 [4, 8], P('rep'), may hold values from 0 to 7, each once within a row
- w_self_qkv: bfloat16 [1024, 3072], P('shard'), may hold values from -0.1875 to 0.1875
- w_self_out: bfloat16 [1024, 1024], P('shard'), may hold values from -0.75 to 0.75
- w_cross_q: bfloat16 [1024, 1024], P('shard'), may hold values from -0.1875 to 0.1875
- w_cross_kv: bfloat16 [1024, 2048], P('shard'), may hold values from -0.1875 to 0.1875
- w_cross_out: bfloat16 [1024, 1024], P('shard'), may hold values from -0.75 to 0.75
- w_fc1: bfloat16 [1024, 4096], P('shard'), may hold values from -0.1875 to 0.1875
- w_fc2: bfloat16 [4096, 1024], P('shard'), may hold values from -0.09375 to 0.09375
- proj_biases: float32 [7, 1024], replicated, may hold values from -1 to 1
- fc1_bias: float32 [4096], replicated, may hold values from -1 to 1
- norm_gains: float32 [3, 1024], replicated, may hold values from 0.5 to 1.5
- norm_shifts: float32 [3, 1024], replicated, may hold values from -1 to 1
Outputs:
- output: bfloat16 [16384, 1024], P(('rep', 'shard'))
- input_grad: float32 [16384, 1024], P(('rep', 'shard'))
- enc_grad: float32 [2048, 1024], P(('rep', 'shard'))
- grad_self_qkv: float32 [1024, 3072], P('shard')
- grad_self_out: float32 [1024, 1024], P('shard')
- grad_cross_q: float32 [1024, 1024], P('shard')
- grad_cross_kv: float32 [1024, 2048], P('shard')
- grad_cross_out: float32 [1024, 1024], P('shard')
- grad_fc1: float32 [1024, 4096], P('shard')
- grad_fc2: float32 [4096, 1024], P('shard')
- grad_proj_biases: float32 [7, 1024], replicated
- grad_fc1_bias: float32 [4096], replicated
- grad_norm_gains: float32 [3, 1024], replicated
- grad_norm_shifts: float32 [3, 1024], replicated
Inputs may be any that keep to these rules, and one draw needn't show every extreme that they name: `placement`: each row names each slot once.
All inputs are finite; a program needn't handle non-finite values.
Results may differ from a plain program's by a relative error of at most 0.028.
Values may be sent and summed in bfloat16 or wider, within the bound.
No kernel may reach another device: no remote copies, remote signals or barrier semaphores. Data moves between devices by JAX's collectives and lax.ppermute only.
A program may use at most 320 MiB of HBM per device.

v0:
```python
import jax
import jax.numpy as jnp
from jax import lax
from jax.sharding import PartitionSpec as P

HEADS = 16
HEAD_DIM = 64


masked_score = -1000000000.0
norm_epsilon = 1e-05


def norm_rows(values, gain_row, shift_row):
    row_mean = jnp.mean(values, -1, keepdims=True)
    centered = values - row_mean
    variance = jnp.mean(centered * centered, -1, keepdims=True)
    return centered * lax.rsqrt(variance + norm_epsilon) * gain_row + shift_row


def product(former, latter):
    return jnp.dot(former, latter, preferred_element_type=jnp.float32)


def product_left(former, latter):
    return lax.dot_general(
        former, latter, (((0,), (0,)), ((), ())), preferred_element_type=jnp.float32
    )


def product_right(former, latter):
    return lax.dot_general(
        former, latter, (((1,), (1,)), ((), ())), preferred_element_type=jnp.float32
    )


def split_heads(values):
    return values.reshape(values.shape[0], HEADS, HEAD_DIM).transpose(1, 0, 2)


def merge_heads(values):
    return values.transpose(1, 0, 2).reshape(values.shape[1], HEADS * HEAD_DIM)


def masked_scores(head_query, head_key, allowed):
    scores = product_right(head_query, head_key)
    if allowed is None:
        return scores
    return jnp.where(allowed, scores, masked_score)


def attend_forward(queries, key_rows, value_rows, allowed):

    def one_head(pieces):
        head_query, head_key, head_value = pieces
        scores = masked_scores(head_query, head_key, allowed)
        row_max = jnp.max(scores, 1, keepdims=True)
        exponent = jnp.exp(scores - row_max)
        row_total = jnp.sum(exponent, 1, keepdims=True)
        probabilities = (exponent / row_total).astype(jnp.bfloat16)
        return (product(probabilities, head_value), row_max[:, 0] + jnp.log(row_total[:, 0]))

    mixed_rows, log_total = lax.map(
        one_head, (split_heads(queries), split_heads(key_rows), split_heads(value_rows))
    )
    return (merge_heads(mixed_rows), log_total)


def attend_backward(queries, key_rows, value_rows, allowed, mixed_grad, log_total):

    def one_head(pieces):
        head_query, head_key, head_value, head_grad, head_total = pieces
        scores = masked_scores(head_query, head_key, allowed)
        probabilities = jnp.exp(scores - head_total[:, None])
        prob_grad = product_right(head_grad, head_value)
        row_delta = jnp.sum(probabilities * prob_grad, 1)
        score_grad = (probabilities * (prob_grad - row_delta[:, None])).astype(jnp.bfloat16)
        query_grad = product(score_grad, head_key)
        return (
            query_grad,
            row_delta,
            product_left(score_grad, head_query),
            product_left(probabilities.astype(jnp.bfloat16), head_grad),
        )

    results = lax.map(
        one_head,
        (
            split_heads(queries),
            split_heads(key_rows),
            split_heads(value_rows),
            split_heads(mixed_grad),
            log_total,
        ),
    )
    return (
        merge_heads(results[0]),
        results[1],
        jnp.concatenate([merge_heads(results[2]), merge_heads(results[3])], 1),
    )


def reduce_weight(former, latter):
    reduced = lax.psum_scatter(
        product_left(former, latter).astype(jnp.bfloat16), "shard", scatter_dimension=0, tiled=True
    )
    return lax.psum(reduced, "rep").astype(jnp.float32)


def column_sums(values):
    return jnp.sum(values.astype(jnp.float32), 0)


def local(
    layer_input,
    encoder_states,
    out_grad,
    placement,
    w_self_qkv,
    w_self_out,
    w_cross_q,
    w_cross_kv,
    w_cross_out,
    w_fc1,
    w_fc2,
    proj_biases,
    fc1_bias,
    norm_gains,
    norm_shifts,
):
    group_size = lax.axis_size("shard")
    half_group = group_size // 2
    member_index = lax.axis_index("shard")
    tok_rows = layer_input.shape[0]
    model_width = layer_input.shape[1]
    score_scale = HEAD_DIM ** (-0.5)
    slot_table = placement[0]
    device_ids = jnp.arange(group_size, dtype=jnp.int32)
    owners = jnp.sum(
        jnp.where(slot_table[None, :] == device_ids[:, None], device_ids[None, :], 0), 1
    )
    seq_of = jnp.where(slot_table < half_group, 0, slot_table - half_group + 1)
    start_of = jnp.where(slot_table < half_group, slot_table * tok_rows, half_group * tok_rows)
    my_seq = seq_of[member_index]
    my_start = start_of[member_index]
    gathered = (
        lax.all_gather(w_self_qkv, "shard", axis=0, tiled=True),
        lax.all_gather(w_self_out, "shard", axis=0, tiled=True),
        lax.all_gather(w_cross_q, "shard", axis=0, tiled=True),
        lax.all_gather(w_cross_kv, "shard", axis=0, tiled=True),
        lax.all_gather(w_cross_out, "shard", axis=0, tiled=True),
        lax.all_gather(w_fc1, "shard", axis=0, tiled=True),
        lax.all_gather(w_fc2, "shard", axis=0, tiled=True),
    )
    full_qkv, full_out, full_cross_q, full_cross_kv, full_cross_out, wfirst, wsecond = gathered
    inputs = layer_input.astype(jnp.float32)
    qkv_rows = product(layer_input, full_qkv)
    queries = ((qkv_rows[:, :model_width] + proj_biases[0]) * score_scale).astype(jnp.bfloat16)
    own_kv = jnp.concatenate(
        [
            qkv_rows[:, model_width : 2 * model_width],
            qkv_rows[:, 2 * model_width :] + proj_biases[1],
        ],
        1,
    ).astype(jnp.bfloat16)
    all_kv = lax.all_gather(own_kv, "shard", axis=0, tiled=True)
    prompt_kv = all_kv.reshape(group_size, tok_rows, 2 * model_width)[owners[:half_group]].reshape(
        half_group * tok_rows, 2 * model_width
    )
    key_value = jnp.concatenate([prompt_kv, own_kv], 0)
    self_keys = key_value[:, :model_width]
    self_values = key_value[:, model_width:]
    positions = jnp.arange(tok_rows, dtype=jnp.int32)
    prompt_pos = jnp.arange(half_group * tok_rows, dtype=jnp.int32)
    early_mask = (my_seq > 0) | (prompt_pos[None, :] <= (my_start + positions)[:, None])
    late_mask = (my_seq > 0) & (positions[None, :] <= positions[:, None])
    self_mask = jnp.concatenate([early_mask, late_mask], 1)
    self_mixed, self_total = attend_forward(queries, self_keys, self_values, self_mask)
    self_low = self_mixed.astype(jnp.bfloat16)
    first_sum = inputs + (product(self_low, full_out) + proj_biases[2])
    first_norm, norm1_back = jax.vjp(norm_rows, first_sum, norm_gains[0], norm_shifts[0])
    first_low = first_norm.astype(jnp.bfloat16)
    cross_queries = ((product(first_low, full_cross_q) + proj_biases[3]) * score_scale).astype(
        jnp.bfloat16
    )
    cross_pre = product(encoder_states, full_cross_kv)
    own_ckv = jnp.concatenate(
        [cross_pre[:, :model_width], cross_pre[:, model_width:] + proj_biases[4]], 1
    ).astype(jnp.bfloat16)
    cross_kv = lax.all_gather(own_ckv, "shard", axis=0, tiled=True)
    cross_keys = cross_kv[:, :model_width]
    cross_values = cross_kv[:, model_width:]
    cross_mixed, cross_total = attend_forward(cross_queries, cross_keys, cross_values, None)
    cross_low = cross_mixed.astype(jnp.bfloat16)
    second_sum = first_norm + (product(cross_low, full_cross_out) + proj_biases[5])
    second_norm, norm2_back = jax.vjp(norm_rows, second_sum, norm_gains[1], norm_shifts[1])
    second_low = second_norm.astype(jnp.bfloat16)
    pre_act = product(second_low, wfirst) + fc1_bias
    hidden, gelu_back = jax.vjp(lambda values: jax.nn.gelu(values, approximate=False), pre_act)
    hidden_low = hidden.astype(jnp.bfloat16)
    third_sum = second_norm + (product(hidden_low, wsecond) + proj_biases[6])
    result, norm3_back = jax.vjp(norm_rows, third_sum, norm_gains[2], norm_shifts[2])
    output = result.astype(jnp.bfloat16)
    third_grad, gain_three, shift_three = norm3_back(out_grad.astype(jnp.float32))
    feed_grad = third_grad.astype(jnp.bfloat16)
    grad_fc2 = reduce_weight(hidden_low, feed_grad)
    bias_fc2 = column_sums(feed_grad)
    pre_grad = gelu_back(product_right(feed_grad, wsecond))[0].astype(jnp.bfloat16)
    grad_fc1 = reduce_weight(second_low, pre_grad)
    bias_fc1 = column_sums(pre_grad)
    second_grad, gain_two, shift_two = norm2_back(third_grad + product_right(pre_grad, wfirst))
    cross_out_grad = second_grad.astype(jnp.bfloat16)
    grad_cross_out = reduce_weight(cross_low, cross_out_grad)
    bias_cross_out = column_sums(cross_out_grad)
    cross_mixed_grad = product_right(cross_out_grad, full_cross_out).astype(jnp.bfloat16)
    cross_query_grad, cross_delta, cross_terms = attend_backward(
        cross_queries, cross_keys, cross_values, None, cross_mixed_grad, cross_total
    )
    own_ckv_grad = lax.psum_scatter(
        cross_terms.astype(jnp.bfloat16), "shard", scatter_dimension=0, tiled=True
    )
    cross_q_grad = cross_query_grad.astype(jnp.bfloat16) * score_scale
    grad_cross_q = reduce_weight(first_low, cross_q_grad)
    bias_cross_q = column_sums(cross_q_grad)
    grad_cross_kv = reduce_weight(encoder_states, own_ckv_grad)
    bias_cross_v = column_sums(own_ckv_grad[:, model_width:])
    enc_grad = product_right(own_ckv_grad, full_cross_kv)
    first_grad, gain_one, shift_one = norm1_back(
        second_grad + product_right(cross_q_grad, full_cross_q)
    )
    self_out_grad = first_grad.astype(jnp.bfloat16)
    grad_self_out = reduce_weight(self_low, self_out_grad)
    bias_self_out = column_sums(self_out_grad)
    self_mixed_grad = product_right(self_out_grad, full_out).astype(jnp.bfloat16)
    self_query_grad, self_delta, key_terms = attend_backward(
        queries, self_keys, self_values, self_mask, self_mixed_grad, self_total
    )
    prompt_terms = key_terms[: half_group * tok_rows].reshape(half_group, tok_rows, 2 * model_width)
    spread_terms = (
        jnp.zeros((group_size, tok_rows, 2 * model_width), jnp.float32)
        .at[owners[:half_group]]
        .set(prompt_terms)
    )
    own_kv_grad = (
        lax.psum_scatter(
            spread_terms.reshape(group_size * tok_rows, 2 * model_width).astype(jnp.bfloat16),
            "shard",
            scatter_dimension=0,
            tiled=True,
        ).astype(jnp.float32)
        + key_terms[half_group * tok_rows :]
    )
    own_kv_low = own_kv_grad.astype(jnp.bfloat16)
    query_low = self_query_grad.astype(jnp.bfloat16) * score_scale
    qkv_grad = jnp.concatenate([query_low, own_kv_low], 1)
    grad_self_qkv = reduce_weight(layer_input, qkv_grad)
    bias_self_q = column_sums(query_low)
    bias_self_v = column_sums(own_kv_low[:, model_width:])
    input_grad = first_grad + product_right(qkv_grad, full_qkv)
    bias_rows = jnp.stack(
        [
            bias_self_q,
            bias_self_v,
            bias_self_out,
            bias_cross_q,
            bias_cross_v,
            bias_cross_out,
            bias_fc2,
        ],
        0,
    )
    gain_rows = jnp.stack([gain_one, gain_two, gain_three], 0)
    shift_rows = jnp.stack([shift_one, shift_two, shift_three], 0)
    grad_biases, grad_first_bias, grad_gains, grad_shifts = lax.psum(
        (bias_rows, bias_fc1, gain_rows, shift_rows), ("rep", "shard")
    )
    return (
        output,
        input_grad,
        enc_grad,
        grad_self_qkv,
        grad_self_out,
        grad_cross_q,
        grad_cross_kv,
        grad_cross_out,
        grad_fc1,
        grad_fc2,
        grad_biases,
        grad_first_bias,
        grad_gains,
        grad_shifts,
    )


def solution(mesh):
    placed = (
        P(("rep", "shard"), None),
        P(("rep", "shard"), None),
        P(("rep", "shard"), None),
        P("rep", None),
        P("shard", None),
        P("shard", None),
        P("shard", None),
        P("shard", None),
        P("shard", None),
        P("shard", None),
        P("shard", None),
        P(),
        P(),
        P(),
        P(),
    )
    return jax.shard_map(
        local,
        mesh=mesh,
        in_specs=placed,
        out_specs=(
            P(("rep", "shard"), None),
            P(("rep", "shard"), None),
            P(("rep", "shard"), None),
            P("shard", None),
            P("shard", None),
            P("shard", None),
            P("shard", None),
            P("shard", None),
            P("shard", None),
            P("shard", None),
            P(),
            P(),
            P(),
            P(),
        ),
        check_vma=False,
    )
```

profile of v0, /device:TPU:0, one launch (start us, length us, event | category | flops | bytes accessed | tf_op | source)
XLA Modules:
  0.0 1855.8 jit_solution(2037025577455184166)
XLA Ops:
  10.4 49.1 %all-gather.18.cloned.1.call-done = bf16[1024,2048]{1,0:T(8,128)(2,1)} async-done(((bf16[128,2048]{1,0:T(8,128)(2,1)}), bf16[1024,2048]{1,0:T(8,128)(2,1)}) %all-gather.18.cloned.1.call-update) | async-done | bytes 4194320 | tf_op jit(solution)/shard_map/all_gather | solution.py:150
  63.4 61.3 %all-gather.10.cloned.1.call-done = bf16[1024,3072]{1,0:T(8,128)(2,1)} async-done(((bf16[128,3072]{1,0:T(8,128)(2,1)}), bf16[1024,3072]{1,0:T(8,128)(2,1)}) %all-gather.10.cloned.1.call-update) | async-done | bytes 6291472 | tf_op jit(solution)/shard_map/all_gather | solution.py:147
  145.1 9.6 all-gather.20.cloned.1.call-done
  165.4 142.0 %all-gather.12.cloned.1.call-done = bf16[4096,2048]{1,0:T(8,128)(2,1)} async-done(((bf16[512,2048]{1,0:T(8,128)(2,1)}), bf16[4096,2048]{1,0:T(8,128)(2,1)}) %all-gather.12.cloned.1.call-update) | async-done | bytes 16777232 | tf_op jit(solution)/shard_map/all_gather | solution.py:166
  307.4 11.8 fusion.113
  340.3 12.5 copy.118
  360.9 10.2 copy.95
  371.1 10.3 copy.96
  381.5 86.0 %while.52 = (s32[]{:T(128)}, bf16[16,512,64]{1,2,0:T(8,128)(2,1)S(1)}, f32[16,512]{1,0:T(8,128)S(1)}, bf16[16,512,64]{2,1,0:T(8,128)(2,1)}, bf16[16,2560,64]{2,1...) while((s32[]{:T(128)}, ...), condition=%wide.region_4.5_spmd, body=%wide.region_1.4_spmd.sunk | while | flops 344718848 | bytes 18634856 | solution.py:63
  480.6 45.1 %while.53 = (s32[]{:T(128)}, bf16[16,512,64]{1,2,0:T(8,128)(2,1)S(1)}, f32[16,512]{1,0:T(8,128)S(1)}, bf16[16,512,64]{2,1,0:T(8,128)(2,1)}, bf16[16,512,64]{2,1,...) while((s32[]{:T(128)}, bf16[16,512,64]{1,2,0:T(8,128)(2,1)S(1)}, ...), condition=%wide.region_10.11_spmd, body=%wide.region_7.10_spmd.sunk | while | flops 68681216 | bytes 3692641 | solution.py:63
  531.0 28.4 %multiply_convert_fusion.2 = (bf16[512,4096]{1,0:T(8,128)(2,1)}, f32[512,4096]{1,0:T(8,128)}, f32[512,4096]{1,0:T(8,128)}) fusion(f32[4096]{0:T(1024)S(1)} %copy-done.72, bf16[1024,4096]{1,0:T(8,128)(2,1)} %all-gather.24.cloned.1.call-done, f32[512,1024]{1,0:T(8,128)} %copy-done.7, f32[1024]{0:T(1024)S(1)} %bitcast.369, f32[1024]{0:T(1024)S(1)} %bitcast.352, ...), kind=kOutput, calls=%fused_computation.109 | convolution fusion | flops 4436000768 | bytes 31485952 | tf_op jit(solution)/shard_map/dot_general | solution.py:22
  561.9 10.0 fusion.120
  576.4 15.7 convert_reduce_fusion
  592.1 9.6 multiply_reduce_fusion.2
  610.5 120.4 %while.54 = (s32[]{:T(128)}, bf16[16,512,64]{1,2,0:T(8,128)(2,1)S(1)}, bf16[16,512,64]{1,2,0:T(8,128)(2,1)}, bf16[16,512,64]{1,2,0:T(8,128)(2,1)}, bf16[16,512,6...) while((s32[]{:T(128)}, ...), condition=%wide.region_21.22_spmd, body=%wide.region_19.21_spmd.sunk | while | flops 169606656 | bytes 9059441 | solution.py:86
  749.5 190.3 %while.55 = (s32[]{:T(128)}, bf16[16,512,64]{1,2,0:T(8,128)(2,1)S(1)}, f32[16,2560,64]{1,2,0:T(8,128)}, f32[16,2560,64]{1,2,0:T(8,128)}, bf16[16,512,64]{2,1,0:T...) while((s32[]{:T(128)}, ...), condition=%wide.region_26.27_spmd, body=%wide.region_24.26_spmd.sunk | while | flops 849346048 | bytes 44448888 | solution.py:86
  939.8 11.4 copy.114
  951.2 11.4 copy.113
  962.6 11.7 fusion.74
  974.3 11.2 broadcast_in_dim.113
  985.6 23.4 %scatter_fusion = f32[8,512,2048]{2,1,0:T(8,128)} fusion(f32[8,512,2048]{2,1,0:T(8,128)} %broadcast_in_dim.113, s32[4]{0:T(128)S(1)} %copy-done.70, f32[4,512,2048]{2,1,0:T(8,128)} %bitcast.312), kind=kCustom, calls=%fused_computation.2 | custom fusion | bytes 50331664 | tf_op jit(solution)/shard_map/scatter | solution.py:242
  1009.0 17.5 convert_element_type.205
  1038.5 155.0 %reduce-scatter.16.cloned.1.call-done = bf16[512,2048]{1,0:T(8,128)(2,1)} async-done(((bf16[4096,2048]{1,0:T(8,128)(2,1)}), bf16[512,2048]{1,0:T(8,128)(2,1)}) %reduce-scatter.16.cloned.1.call-update) | async-done | bytes 2097168 | tf_op jit(solution)/shard_map/reduce_scatter | solution.py:245
  1226.3 9.3 convolution_convert_fusion.1
  1248.1 66.2 %reduce-scatter.30.cloned.1.call-done = bf16[128,3072]{1,0:T(8,128)(2,1)} async-done(((bf16[1024,3072]{1,0:T(8,128)(2,1)}), bf16[128,3072]{1,0:T(8,128)(2,1)}) %reduce-scatter.30.cloned.1.call-update) | async-done | bytes 786448
  1316.6 34.0 %reduce-scatter.22.cloned.1.call-done = bf16[128,1024]{1,0:T(8,128)(2,1)} async-done(((bf16[1024,1024]{1,0:T(8,128)(2,1)}), bf16[128,1024]{1,0:T(8,128)(2,1)}) %reduce-scatter.22.cloned.1.call-update) | async-done | bytes 262160 | tf_op jit(solution)/shard_map/reduce_scatter | solution.py:104
  1350.6 36.5 %reduce-scatter.20.cloned.1.call-done = bf16[128,1024]{1,0:T(8,128)(2,1)} async-done(((bf16[1024,1024]{1,0:T(8,128)(2,1)}), bf16[128,1024]{1,0:T(8,128)(2,1)}) %reduce-scatter.20.cloned.1.call-update) | async-done | bytes 262160 | tf_op jit(solution)/shard_map/reduce_scatter | solution.py:104
  1387.1 36.7 %reduce-scatter.18.cloned.1.call-done = bf16[128,1024]{1,0:T(8,128)(2,1)} async-done(((bf16[1024,1024]{1,0:T(8,128)(2,1)}), bf16[128,1024]{1,0:T(8,128)(2,1)}) %reduce-scatter.18.cloned.1.call-update) | async-done | bytes 262160 | tf_op jit(solution)/shard_map/reduce_scatter | solution.py:104
  1423.8 90.5 %reduce-scatter.24.cloned.1.call-done = bf16[128,4096]{1,0:T(8,128)(2,1)} async-done(((bf16[1024,4096]{1,0:T(8,128)(2,1)}), bf16[128,4096]{1,0:T(8,128)(2,1)}) %reduce-scatter.24.cloned.1.call-update) | async-done | bytes 1048592 | tf_op jit(solution)/shard_map/reduce_scatter | solution.py:104
  1514.3 90.1 %reduce-scatter.26.cloned.1.call-done = bf16[512,1024]{1,0:T(8,128)(2,1)} async-done(((bf16[4096,1024]{1,0:T(8,128)(2,1)}), bf16[512,1024]{1,0:T(8,128)(2,1)}) %reduce-scatter.26.cloned.1.call-update) | async-done | bytes 1048592 | tf_op jit(solution)/shard_map/reduce_scatter | solution.py:104
  1620.6 93.5 %all-reduce.7.cloned.1.call-done = (bf16[128,3072]{0,1:T(8,128)(2,1)}, bf16[128,2048]{0,1:T(8,128)(2,1)}, bf16[128,1024]{1,0:T(8,128)(2,1)}, bf16[128,1024]{1,0:...) async-done(((bf16[128,3072]{0,1:T(8,128)(2,1)}, bf16[128,2048]{0,1:T(8,128)(2,1)}, bf16[128,1024]{1,0:T(8,128)(2,1)}, ...) | async-done | bytes 4194320 | tf_op jit(solution)/shard_map/psum | solution.py:107
  1726.6 116.6 %all-reduce.5.cloned.1.call-done = (f32[7,1024]{1,0:T(8,128)}, f32[4096]{0:T(1024)}, f32[3,1024]{1,0:T(4,128)}, f32[3,1024]{1,0:T(4,128)}) async-done(((f32[7,1024]{1,0:T(8,128)}, f32[4096]{0:T(1024)}, f32[3,1024]{1,0:T(4,128)}, f32[3,1024]{1,0:T(4,128)}), (f32[7,1024]{1,0:T(8,128)}, f32[4096]{0:T(1024)}, f32[3,1024]{1,0:T(4,128)}, f32[3,1024]{1,0:T(4,128)})) %all-reduce.5.cloned.1.call-update) | async-done | bytes 69648 | tf_op jit(solution)/shard_map/psum | solution.py:274
  (692 shorter events, 651.1 us)
Async XLA Ops:
  7.2 52.3 %all-gather.18.cloned.1.call-start = ((), (), s32[]{:S(2)}) async-start(), calls=%async_computation.13 | async-start | bytes 4718592 | tf_op jit(solution)/shard_map/all_gather | solution.py:150
  7.9 116.8 %all-gather.10.cloned.1.call-start = ((), (), s32[]{:S(2)}) async-start(), calls=%async_computation.9 | async-start | bytes 7077888 | tf_op jit(solution)/shard_map/all_gather | solution.py:147
  8.7 146.0 %all-gather.20.cloned.1.call-start = ((), (), s32[]{:S(2)}) async-start(), calls=%async_computation.14 | async-start | bytes 2359296 | tf_op jit(solution)/shard_map/all_gather | solution.py:190
  63.4 244.0 %all-gather.12.cloned.1.call-start = ((), (), s32[]{:S(2)}) async-start(), calls=%async_computation.10 | async-start | bytes 18874368 | tf_op jit(solution)/shard_map/all_gather | solution.py:166
  133.5 334.0 %all-gather.14.cloned.1.call-start = ((), (), s32[]{:S(2)}) async-start(), calls=%async_computation.11 | async-start | bytes 2359296 | tf_op jit(solution)/shard_map/all_gather | solution.py:148
  134.1 339.2 %all-gather.16.cloned.1.call-start = ((), (), s32[]{:S(2)}) async-start(), calls=%async_computation.12 | async-start | bytes 2359296 | tf_op jit(solution)/shard_map/all_gather | solution.py:149
  134.7 391.1 %all-gather.22.cloned.1.call-start = ((), (), s32[]{:S(2)}) async-start(), calls=%async_computation.15 | async-start | bytes 2359296 | tf_op jit(solution)/shard_map/all_gather | solution.py:151
  135.5 395.5 %all-gather.24.cloned.1.call-start = ((), (), s32[]{:S(2)}) async-start(), calls=%async_computation.16 | async-start | bytes 9437184 | tf_op jit(solution)/shard_map/all_gather | solution.py:152
  136.2 425.7 %all-gather.26.cloned.1.call-start = ((), (), s32[]{:S(2)}) async-start(), calls=%async_computation.17 | async-start | bytes 9437184 | tf_op jit(solution)/shard_map/all_gather | solution.py:153
  136.9 889.7 %reduce-scatter.28.cloned.1.call-start = ((), (), s32[]{:S(2)}) async-start(), calls=%async_computation.24 | async-start | bytes 2359296
  140.2 461.6 %copy-start.47 = (f32[1,1024]{1,0:T(1,128)}, f32[1,1024]{1,0:T(1,128)S(1)}, u32[]{:S(2)}) copy-start(f32[1,1024]{1,0:T(1,128)S(1)} %get-tuple-element.480) | copy-start | bytes 12292
  140.2 604.1 %copy-start.49 = (f32[1,1024]{1,0:T(1,128)}, f32[1,1024]{1,0:T(1,128)S(1)}, u32[]{:S(2)}) copy-start(f32[1,1024]{1,0:T(1,128)S(1)} %get-tuple-element.479) | copy-start | bytes 12292
  472.1 272.2 %copy-start.3 = (f32[512,1024]{1,0:T(8,128)}, f32[512,1024]{1,0:T(8,128)S(1)}, u32[]{:S(2)}) copy-start(f32[512,1024]{1,0:T(8,128)S(1)} %get-tuple-element.487) | copy-start | bytes 6291460
  737.9 455.6 %reduce-scatter.16.cloned.1.call-start = ((), (), s32[]{:S(2)}) async-start(), calls=%async_computation.18 | async-start | bytes 18874368 | tf_op jit(solution)/shard_map/reduce_scatter | solution.py:245
  1026.6 219.5 %reduce-scatter.32.cloned.1.call-start = ((), (), s32[]{:S(2)}) async-start(), calls=%async_computation.26 | async-start | bytes 4718592
  1037.6 276.7 %reduce-scatter.30.cloned.1.call-start = ((), (), s32[]{:S(2)}) async-start(), calls=%async_computation.25 | async-start | bytes 7077888
  1212.8 137.8 %reduce-scatter.22.cloned.1.call-start = ((), (), s32[]{:S(2)}) async-start(), calls=%async_computation.21 | async-start | bytes 2359296 | tf_op jit(solution)/shard_map/reduce_scatter | solution.py:104
  1217.9 169.2 %reduce-scatter.20.cloned.1.call-start = ((), (), s32[]{:S(2)}) async-start(), calls=%async_computation.20 | async-start | bytes 2359296 | tf_op jit(solution)/shard_map/reduce_scatter | solution.py:104
  1222.2 201.6 %reduce-scatter.18.cloned.1.call-start = ((), (), s32[]{:S(2)}) async-start(), calls=%async_computation.19 | async-start | bytes 2359296 | tf_op jit(solution)/shard_map/reduce_scatter | solution.py:104
  1226.2 288.1 %reduce-scatter.24.cloned.1.call-start = ((), (), s32[]{:S(2)}) async-start(), calls=%async_computation.22 | async-start | bytes 9437184 | tf_op jit(solution)/shard_map/reduce_scatter | solution.py:104
  1235.7 368.8 %reduce-scatter.26.cloned.1.call-start = ((), (), s32[]{:S(2)}) async-start(), calls=%async_computation.23 | async-start | bytes 9437184 | tf_op jit(solution)/shard_map/reduce_scatter | solution.py:104
  1245.9 359.0 %copy-start.36 = (f32[16,64]{1,0:T(8,128)S(1)}, f32[16,64]{1,0:T(8,128)}, u32[]{:S(2)}) copy-start(f32[16,64]{1,0:T(8,128)} %get-tuple-element.440) | copy-start | bytes 12292
  1245.9 359.1 %copy-start.41 = (f32[1024]{0:T(1024)S(1)}, f32[1024]{0:T(1024)}, u32[]{:S(2)}) copy-start(f32[1024]{0:T(1024)} %get-tuple-element.354) | copy-start | bytes 12292
  1245.9 359.1 %copy-start.42 = (f32[1024]{0:T(1024)S(1)}, f32[1024]{0:T(1024)}, u32[]{:S(2)}) copy-start(f32[1024]{0:T(1024)} %get-tuple-element.358) | copy-start | bytes 12292
  1245.9 359.1 %copy-start.59 = (f32[1024]{0:T(1024)S(1)}, f32[1024]{0:T(1024)}, u32[]{:S(2)}) copy-start(f32[1024]{0:T(1024)} %get-tuple-element.352) | copy-start | bytes 12292
  1245.9 359.1 %copy-start.60 = (f32[1024]{0:T(1024)S(1)}, f32[1024]{0:T(1024)}, u32[]{:S(2)}) copy-start(f32[1024]{0:T(1024)} %get-tuple-element.357) | copy-start | bytes 12292
  1245.9 359.1 %copy-start.63 = (f32[1024]{0:T(1024)S(1)}, f32[1024]{0:T(1024)}, u32[]{:S(2)}) copy-start(f32[1024]{0:T(1024)} %get-tuple-element.350) | copy-start | bytes 12292
  1246.0 359.1 %copy-start.64 = (f32[1024]{0:T(1024)S(1)}, f32[1024]{0:T(1024)}, u32[]{:S(2)}) copy-start(f32[1024]{0:T(1024)} %get-tuple-element.356) | copy-start | bytes 12292
  1246.0 359.8 %slice-start = ((bf16[64,2048]{1,0:T(8,128)(2,1)}), bf16[64,1024]{1,0:T(8,128)(2,1)S(1)}, s32[]{:S(2)}) async-start(bf16[64,2048]{1,0:T(8,128)(2,1)} %reduce-scatter.28.cloned.1.call-done), calls=%async_computation.29 | async-start | bytes 262144 | tf_op jit(solution)/shard_map/slice | solution.py:226
  1246.0 360.1 %copy-start.20 = (bf16[64,2048]{1,0:T(8,128)(2,1)S(1)}, bf16[64,2048]{1,0:T(8,128)(2,1)}, u32[]{:S(2)}) copy-start(bf16[64,2048]{1,0:T(8,128)(2,1)} %reduce-scatter.28.cloned.1.call-done) | copy-start | bytes 786436
  1246.0 468.1 %all-reduce.7.cloned.1.call-start = ((), (), s32[]{:S(2)}) async-start(), calls=%async_computation.28 | async-start | bytes 8388608 | tf_op jit(solution)/shard_map/psum | solution.py:107
  1604.5 238.6 %all-reduce.5.cloned.1.call-start = ((), (), s32[]{:S(2)}) async-start(), calls=%async_computation.27 | async-start | bytes 163840 | tf_op jit(solution)/shard_map/psum | solution.py:274
  (63 other events, 1347.5 us)
Sparse Core Ops, SparseCore 0:
  9.6 49.8 all-gather.17
  61.2 63.5 all-gather.9
  126.9 27.7 all-gather.19
  156.7 150.5 all-gather.11
  308.8 27.3 all-gather.13
  337.6 28.5 all-gather.15
  367.9 28.5 all-gather.21
  398.1 81.5 all-gather.23
  481.3 80.5 all-gather.25
  738.1 34.4 reduce-scatter.27
  1026.7 166.7 reduce-scatter.15
  1195.7 48.3 reduce-scatter.31
  1246.3 67.9 reduce-scatter.29
  1316.5 34.1 reduce-scatter.21
  1352.8 34.2 reduce-scatter.19
  1389.2 34.5 reduce-scatter.17
  1425.9 88.3 reduce-scatter.23
  1516.5 87.9 reduce-scatter.25
  1609.5 104.5 all-reduce.6
  1721.7 121.3 all-reduce.4
where the time goes:
time: 1870 us; the launch traced here: 1860 us
  waiting for transfers between devices  989 us (53%)
  matrix products  541 us (29%)
  local copies, waits for them, and re-layouts  198 us (11%)
  other arithmetic  108 us (6%)
    reduce_scatter x5, waiting for transfers between devices, reduce_weight(): lax.psum_scatter(product_left(former, latter).astype(jnp.bfloat16), 'shar...  288 us
    dot_general x103, matrix products, product_right(): lax.dot_general(former, latter, (((1,), (1,)), ((), ())), preferred_eleme...  220 us
    dot_general x71, matrix products, product(): return jnp.dot(former, latter, preferred_element_type=jnp.float32)  164 us
    dot_general x71, matrix products, product_left(): lax.dot_general(former, latter, (((0,), (0,)), ((), ())), preferred_eleme...  158 us
    reduce_scatter x1, waiting for transfers between devices, local(): lax.psum_scatter(spread_terms.reshape(group_size * tok_rows, 2 * model_wi...  155 us
    all_gather x1, waiting for transfers between devices, local(): all_kv = lax.all_gather(own_kv, 'shard', axis=0, tiled=True)  142 us
    psum x1, waiting for transfers between devices, local(): lax.psum((bias_rows, bias_fc1, gain_rows, shift_rows), ('rep', 'shard'))  117 us
    psum x1, waiting for transfers between devices, reduce_weight(): return lax.psum(reduced, 'rep').astype(jnp.float32)  93.5 us
  transfers between devices with their start and end apart: 20, of which 14 were waited for; matrix products, arithmetic and copies ran while one was open for 36% of the time, Pallas kernels for 0%

commit v1 on v0

v1 whole, which is shorter than its diff:
```python
import functools

import jax
import jax.numpy as jnp
from jax import lax
from jax.experimental import pallas as pl
from jax.experimental.pallas import tpu as pltpu
from jax.sharding import PartitionSpec as P

HEADS = 16
HEAD_DIM = 64
LANES = 128

masked_score = -1000000000.0
norm_epsilon = 1e-05
low_type = jnp.bfloat16
MESH_AXES = ("rep", "shard")


def norm_rows(values, gain_row, shift_row):
    row_mean = jnp.mean(values, -1, keepdims=True)
    centered = values - row_mean
    variance = jnp.mean(centered * centered, -1, keepdims=True)
    return centered * lax.rsqrt(variance + norm_epsilon) * gain_row + shift_row


def product(former, latter):
    return jnp.dot(former, latter, preferred_element_type=jnp.float32)


def product_left(former, latter):
    return lax.dot_general(
        former, latter, (((0,), (0,)), ((), ())), preferred_element_type=jnp.float32
    )


def product_right(former, latter):
    return lax.dot_general(
        former, latter, (((1,), (1,)), ((), ())), preferred_element_type=jnp.float32
    )


def column_sums(values):
    return jnp.sum(values.astype(jnp.float32), 0)


def head_columns(index):
    return slice(index * HEAD_DIM, (index + 1) * HEAD_DIM)


def causal_rows(keys, queries):
    key_index = lax.broadcasted_iota(jnp.int32, (keys, queries), 0)
    query_index = lax.broadcasted_iota(jnp.int32, (keys, queries), 1)
    return key_index <= query_index


def self_forward_kernel(tok, width, half, owner, qkv, value_t, mixed, total):
    slot = pl.program_id(0)
    heads = width // HEAD_DIM
    base = pl.multiple_of(owner[slot] * tok, tok)
    query = qkv[pl.ds(base, tok), :width]

    def step(start, carry, causal):
        keys = qkv[pl.ds(start, tok), width : 2 * width]
        values = value_t[:, pl.ds(start, tok)]
        result = []
        for head in range(heads):
            top, weight, mix = carry[head]
            cols = head_columns(head)
            scores = product_right(keys[:, cols], query[:, cols])
            if causal:
                scores = jnp.where(causal_rows(tok, tok), scores, masked_score)
            new_top = jnp.maximum(top, jnp.max(scores, 0, keepdims=True))
            scale = jnp.exp(top - new_top)
            power = jnp.exp(scores - new_top)
            weight = weight * scale + jnp.sum(power, 0, keepdims=True)
            mix = mix * scale + product(values[cols], power.astype(low_type))
            result.append((new_top, weight, mix))
        return tuple(result)

    first = tuple(
        (
            jnp.full((1, tok), -1e30, jnp.float32),
            jnp.zeros((1, tok), jnp.float32),
            jnp.zeros((HEAD_DIM, tok), jnp.float32),
        )
        for _ in range(heads)
    )
    whole = jnp.minimum(slot, half)
    carry = lax.fori_loop(
        0, whole, lambda j, c: step(pl.multiple_of(owner[j] * tok, tok), c, False), first
    )
    carry = step(base, carry, True)
    mix = jnp.concatenate([part[2] / part[1] for part in carry], 0)
    mixed[pl.ds(base, tok), :] = jnp.transpose(mix).astype(low_type)
    for head in range(heads):
        total[head : head + 1, :] = carry[head][0] + jnp.log(carry[head][1])


def self_backward_kernel(
    tok, width, half, scale, owner, qkv, key_t, mixed_grad, mixed, total, out, key_sum, value_sum
):
    slot = pl.program_id(0)
    heads = width // HEAD_DIM
    base = pl.multiple_of(owner[slot] * tok, tok)

    @pl.when(slot == 0)
    def _():
        key_sum[...] = jnp.zeros_like(key_sum)
        value_sum[...] = jnp.zeros_like(value_sum)

    query = qkv[pl.ds(base, tok), :width]
    grad = mixed_grad[pl.ds(base, tok), :]
    both = grad.astype(jnp.float32) * mixed[pl.ds(base, tok), :].astype(jnp.float32)
    both = jnp.transpose(both)
    deltas = [jnp.sum(both[head_columns(h)], 0, keepdims=True) for h in range(heads)]
    totals = [total[h : h + 1, :] for h in range(heads)]

    def step(start, carry, causal):
        keys = qkv[pl.ds(start, tok), width : 2 * width]
        values = qkv[pl.ds(start, tok), 2 * width :]
        keys_t = key_t[:, pl.ds(start, tok)]
        result, key_parts, value_parts = [], [], []
        for head in range(heads):
            cols = head_columns(head)
            scores = product_right(keys[:, cols], query[:, cols])
            power = jnp.exp(scores - totals[head])
            if causal:
                power = jnp.where(causal_rows(tok, tok), power, 0.0)
            slope = product_right(values[:, cols], grad[:, cols])
            score_grad = (power * (slope - deltas[head])).astype(low_type)
            value_parts.append(product(power.astype(low_type), grad[:, cols]))
            key_parts.append(product(score_grad, query[:, cols]))
            result.append(carry[head] + product(keys_t[cols], score_grad))
        key_sum[pl.ds(start, tok), :] += jnp.concatenate(key_parts, 1)
        value_sum[pl.ds(start, tok), :] += jnp.concatenate(value_parts, 1)
        return tuple(result)

    first = tuple(jnp.zeros((HEAD_DIM, tok), jnp.float32) for _ in range(heads))
    whole = jnp.minimum(slot, half)
    carry = lax.fori_loop(
        0, whole, lambda j, c: step(pl.multiple_of(owner[j] * tok, tok), c, False), first
    )
    carry = step(base, carry, True)
    query_grad = jnp.transpose(jnp.concatenate(carry, 0)).astype(low_type)
    out[pl.ds(base, tok), :width] = query_grad * scale

    @pl.when(slot == pl.num_programs(0) - 1)
    def _():
        out[:, width : 2 * width] = key_sum[...].astype(low_type)
        out[:, 2 * width :] = value_sum[...].astype(low_type)


def cross_forward_kernel(width, query, pair, mixed, total):
    keys, values = pair[0], jnp.transpose(pair[1])
    mixes = []
    for head in range(width // HEAD_DIM):
        cols = head_columns(head)
        scores = product_right(keys[:, cols], query[:, cols])
        top = jnp.max(scores, 0, keepdims=True)
        power = jnp.exp(scores - top)
        weight = jnp.sum(power, 0, keepdims=True)
        mixes.append(product(values[cols], power.astype(low_type)) / weight)
        total[head : head + 1, :] = top + jnp.log(weight)
    mixed[...] = jnp.transpose(jnp.concatenate(mixes, 0)).astype(low_type)


def cross_backward_kernel(width, scale, query, pair, mixed_grad, mixed, total, out, pair_grad):
    heads = width // HEAD_DIM
    keys, values = pair[0], pair[1]
    keys_t = jnp.transpose(keys)
    grad = mixed_grad[...]
    both = jnp.transpose(grad.astype(jnp.float32) * mixed[...].astype(jnp.float32))
    query_parts, key_parts, value_parts = [], [], []
    for head in range(heads):
        cols = head_columns(head)
        scores = product_right(keys[:, cols], query[:, cols])
        power = jnp.exp(scores - total[head : head + 1, :])
        slope = product_right(values[:, cols], grad[:, cols])
        delta = jnp.sum(both[cols], 0, keepdims=True)
        score_grad = (power * (slope - delta)).astype(low_type)
        value_parts.append(product(power.astype(low_type), grad[:, cols]))
        key_parts.append(product(score_grad, query[:, cols]))
        query_parts.append(product(keys_t[cols], score_grad))
    query_grad = jnp.transpose(jnp.concatenate(query_parts, 0)).astype(low_type)
    out[...] = query_grad * scale
    pair_grad[0] = jnp.concatenate(key_parts, 1).astype(low_type)
    pair_grad[1] = jnp.concatenate(value_parts, 1).astype(low_type)


def kernel_options(megabytes):
    return pltpu.CompilerParams(
        dimension_semantics=("arbitrary",), vmem_limit_bytes=megabytes * 2**20
    )


def whole_block(shape):
    return pl.BlockSpec(shape, lambda *_: (0,) * len(shape), pipeline_mode=pl.Buffered(1))


def self_forward(owners, qkv, value_t, tok):
    rows, width = qkv.shape[0], qkv.shape[1] // 3
    group = rows // tok
    pairs = group * (group // 4 + 1)
    return pl.pallas_call(
        functools.partial(self_forward_kernel, tok, width, group // 2),
        out_shape=(
            jax.ShapeDtypeStruct((rows, width), low_type),
            jax.ShapeDtypeStruct((group, 8, tok), jnp.float32),
        ),
        grid_spec=pltpu.PrefetchScalarGridSpec(
            num_scalar_prefetch=1,
            grid=(group,),
            in_specs=[whole_block(qkv.shape), whole_block(value_t.shape)],
            out_specs=[
                pl.BlockSpec((rows, width), lambda *_: (0, 0)),
                pl.BlockSpec((None, 8, tok), lambda p, _: (p, 0, 0)),
            ],
        ),
        compiler_params=kernel_options(40),
        cost_estimate=pl.CostEstimate(
            flops=pairs * tok * tok * width * 12,
            transcendentals=pairs * tok * tok * (width // HEAD_DIM),
            bytes_accessed=rows * width * 10,
        ),
        name="self_forward",
    )(owners, qkv, value_t)


def self_backward(owners, qkv, key_t, mixed_grad, mixed, total, tok):
    rows, width = qkv.shape[0], qkv.shape[1] // 3
    group = rows // tok
    pairs = group * (group // 4 + 1)
    return pl.pallas_call(
        functools.partial(
            self_backward_kernel, tok, width, group // 2, HEAD_DIM ** (-0.5)
        ),
        out_shape=jax.ShapeDtypeStruct(qkv.shape, low_type),
        grid_spec=pltpu.PrefetchScalarGridSpec(
            num_scalar_prefetch=1,
            grid=(group,),
            in_specs=[
                whole_block(qkv.shape),
                whole_block(key_t.shape),
                whole_block(mixed_grad.shape),
                whole_block(mixed.shape),
                pl.BlockSpec((None, 8, tok), lambda p, _: (p, 0, 0)),
            ],
            out_specs=pl.BlockSpec(qkv.shape, lambda *_: (0, 0)),
            scratch_shapes=[
                pltpu.VMEM((rows, width), jnp.float32),
                pltpu.VMEM((rows, width), jnp.float32),
            ],
        ),
        compiler_params=kernel_options(48),
        cost_estimate=pl.CostEstimate(
            flops=pairs * tok * tok * width * 30,
            transcendentals=pairs * tok * tok * (width // HEAD_DIM),
            bytes_accessed=rows * width * 20,
        ),
        name="self_backward",
    )(owners, qkv, key_t, mixed_grad, mixed, total)


def split_columns(values, group):
    rows = values.shape[0]
    return values.reshape(rows, group, -1).transpose(1, 0, 2)


def join_columns(values):
    return values.transpose(1, 0, 2).reshape(values.shape[1], -1)


def by_head(values, group):
    rows, width = values.shape[0], values.shape[1] // group
    if width % LANES == 0:
        return values, pl.BlockSpec((rows, width), lambda g: (0, g))
    return split_columns(values, group), pl.BlockSpec((None, rows, width), lambda g: (g, 0, 0))


def of_heads(values, group):
    return values if values.ndim == 2 else join_columns(values)


def cross_forward(queries, pairs):
    group, _, states, width = pairs.shape
    rows = queries.shape[0]
    queries, query_spec = by_head(queries, group)
    mixed, total = pl.pallas_call(
        functools.partial(cross_forward_kernel, width),
        out_shape=(
            jax.ShapeDtypeStruct(queries.shape, low_type),
            jax.ShapeDtypeStruct((group, 8, rows), jnp.float32),
        ),
        grid=(group,),
        in_specs=[query_spec, pl.BlockSpec((None, 2, states, width), lambda g: (g, 0, 0, 0))],
        out_specs=[query_spec, pl.BlockSpec((None, 8, rows), lambda g: (g, 0, 0))],
        compiler_params=kernel_options(32),
        cost_estimate=pl.CostEstimate(
            flops=rows * states * group * width * 12,
            transcendentals=rows * states * HEADS,
            bytes_accessed=group * width * (rows * 4 + states * 4),
        ),
        name="cross_forward",
    )(queries, pairs)
    return of_heads(mixed, group), total


def cross_backward(queries, pairs, mixed_grad, mixed, total):
    group, _, states, width = pairs.shape
    rows = queries.shape[0]
    queries, spec = by_head(queries, group)
    mixed_grad, mixed = by_head(mixed_grad, group)[0], by_head(mixed, group)[0]
    pair_spec = pl.BlockSpec((None, 2, states, width), lambda g: (g, 0, 0, 0))
    query_grad, pair_grad = pl.pallas_call(
        functools.partial(cross_backward_kernel, width, HEAD_DIM ** (-0.5)),
        out_shape=(
            jax.ShapeDtypeStruct(queries.shape, low_type),
            jax.ShapeDtypeStruct(pairs.shape, low_type),
        ),
        grid=(group,),
        in_specs=[spec, pair_spec, spec, spec, pl.BlockSpec((None, 8, rows), lambda g: (g, 0, 0))],
        out_specs=[spec, pair_spec],
        compiler_params=kernel_options(32),
        cost_estimate=pl.CostEstimate(
            flops=rows * states * group * width * 30,
            transcendentals=rows * states * HEADS,
            bytes_accessed=group * width * (rows * 8 + states * 8),
        ),
        name="cross_backward",
    )(queries, pairs, mixed_grad, mixed, total)
    return of_heads(query_grad, group), pair_grad


def flip(values, axis_bit):
    axis, bit = axis_bit
    size = lax.axis_size(axis)
    return lax.ppermute(values, axis, [(i, i ^ bit) for i in range(size)])


def bits_of(axis):
    size = lax.axis_size(axis)
    return [(axis, 1 << i) for i in range(size.bit_length() - 1)]


def sum_over(values, bits):
    for bit in bits:
        values = (
            values.astype(jnp.float32) + flip(values, bit).astype(jnp.float32)
        ).astype(values.dtype)
    return values


def sum_over_rep(values):
    bits = bits_of("rep")
    middle = values.shape[0] // 2
    return jnp.concatenate(
        [sum_over(values[:middle], bits), sum_over(values[middle:], bits[::-1])], 0
    )


def gather_rows(values):
    return lax.all_gather(values, "shard", axis=0, tiled=True)


def exchange(values):
    return lax.all_to_all(values, "shard", split_axis=0, concat_axis=0, tiled=True)


def reduce_weight(former, latter):
    reduced = lax.psum_scatter(
        product_left(former, latter).astype(low_type), "shard", scatter_dimension=0, tiled=True
    )
    return sum_over_rep(reduced).astype(jnp.float32)


def local(
    layer_input,
    encoder_states,
    out_grad,
    placement,
    w_self_qkv,
    w_self_out,
    w_cross_q,
    w_cross_kv,
    w_cross_out,
    w_fc1,
    w_fc2,
    proj_biases,
    fc1_bias,
    norm_gains,
    norm_shifts,
):
    group = lax.axis_size("shard")
    member = lax.axis_index("shard")
    tok, model = layer_input.shape
    weight_rows = w_self_qkv.shape[0]
    width = model // group
    score_scale = HEAD_DIM ** (-0.5)
    slot_table = placement[0]
    device_ids = jnp.arange(group, dtype=jnp.int32)
    owners = jnp.sum(
        jnp.where(slot_table[None, :] == device_ids[:, None], device_ids[None, :], 0), 1
    )

    def own_columns(row):
        return lax.dynamic_slice(row, (member * width,), (width,))

    def in_columns(row):
        return lax.dynamic_update_slice(jnp.zeros((model,), jnp.float32), row, (member * width,))

    slices = jnp.concatenate(
        [
            w_self_qkv.reshape(weight_rows, 3, group, width),
            w_cross_kv.reshape(weight_rows, 2, group, width),
        ],
        1,
    )
    slices = slices.transpose(2, 0, 1, 3).reshape(group, weight_rows, 5 * width)
    slices = exchange(slices).reshape(model, 5 * width)
    head_qkv, head_ckv = slices[:, : 3 * width], slices[:, 3 * width :]
    all_inputs = gather_rows(layer_input)
    all_states = gather_rows(encoder_states)
    full_out = gather_rows(w_self_out)
    full_cross_q = gather_rows(w_cross_q)
    full_cross_out = gather_rows(w_cross_out)
    wfirst = gather_rows(w_fc1)
    wsecond = gather_rows(w_fc2)

    inputs = layer_input.astype(jnp.float32)
    zeros = jnp.zeros((width,), jnp.float32)
    head_bias = jnp.concatenate([own_columns(proj_biases[0]), zeros, own_columns(proj_biases[1])])
    head_scale = jnp.concatenate([jnp.full((width,), score_scale), jnp.ones((2 * width,))])
    qkv = ((product(all_inputs, head_qkv) + head_bias) * head_scale).astype(low_type)
    key_t, value_t = jnp.transpose(qkv[:, width : 2 * width]), jnp.transpose(qkv[:, 2 * width :])
    head_mixed, self_total = self_forward(owners, qkv, value_t, tok)
    self_low = join_columns(exchange(head_mixed.reshape(group, tok, width)))

    cross_bias = jnp.concatenate([zeros, own_columns(proj_biases[4])])
    head_pair = (product(all_states, head_ckv) + cross_bias).astype(low_type)
    states = all_states.shape[0]
    head_pair = split_columns(head_pair, 2)
    pairs = lax.all_gather(head_pair, "shard", axis=0, tiled=False)

    first_sum = inputs + (product(self_low, full_out) + proj_biases[2])
    first_norm, norm1_back = jax.vjp(norm_rows, first_sum, norm_gains[0], norm_shifts[0])
    first_low = first_norm.astype(low_type)
    cross_queries = ((product(first_low, full_cross_q) + proj_biases[3]) * score_scale).astype(
        low_type
    )
    cross_low, cross_total = cross_forward(cross_queries, pairs)
    second_sum = first_norm + (product(cross_low, full_cross_out) + proj_biases[5])
    second_norm, norm2_back = jax.vjp(norm_rows, second_sum, norm_gains[1], norm_shifts[1])
    second_low = second_norm.astype(low_type)
    pre_act = product(second_low, wfirst) + fc1_bias
    hidden, gelu_back = jax.vjp(lambda values: jax.nn.gelu(values, approximate=False), pre_act)
    hidden_low = hidden.astype(low_type)
    third_sum = second_norm + (product(hidden_low, wsecond) + proj_biases[6])
    result, norm3_back = jax.vjp(norm_rows, third_sum, norm_gains[2], norm_shifts[2])
    output = result.astype(low_type)

    third_grad, gain_three, shift_three = norm3_back(out_grad.astype(jnp.float32))
    feed_grad = third_grad.astype(low_type)
    grad_fc2 = reduce_weight(hidden_low, feed_grad)
    bias_fc2 = column_sums(feed_grad)
    pre_grad = gelu_back(product_right(feed_grad, wsecond))[0].astype(low_type)
    grad_fc1 = reduce_weight(second_low, pre_grad)
    bias_fc1 = column_sums(pre_grad)
    second_grad, gain_two, shift_two = norm2_back(third_grad + product_right(pre_grad, wfirst))
    cross_out_grad = second_grad.astype(low_type)
    grad_cross_out = reduce_weight(cross_low, cross_out_grad)
    bias_cross_out = column_sums(cross_out_grad)
    cross_mixed_grad = product_right(cross_out_grad, full_cross_out).astype(low_type)
    cross_q_grad, pair_grad = cross_backward(
        cross_queries, pairs, cross_mixed_grad, cross_low, cross_total
    )
    own_pair_grad = join_columns(
        lax.psum_scatter(pair_grad, "shard", scatter_dimension=0, tiled=False)
    )
    grad_cross_q = reduce_weight(first_low, cross_q_grad)
    bias_cross_q = column_sums(cross_q_grad)
    bias_cross_v = in_columns(column_sums(own_pair_grad[:, width:]))
    enc_grad = lax.psum_scatter(
        product_right(own_pair_grad, head_ckv).astype(low_type),
        "shard",
        scatter_dimension=0,
        tiled=True,
    ).astype(jnp.float32)
    first_grad, gain_one, shift_one = norm1_back(
        second_grad + product_right(cross_q_grad, full_cross_q)
    )
    self_out_grad = first_grad.astype(low_type)
    grad_self_out = reduce_weight(self_low, self_out_grad)
    bias_self_out = column_sums(self_out_grad)
    self_mixed_grad = product_right(self_out_grad, full_out).astype(low_type)
    head_grad = exchange(split_columns(self_mixed_grad, group)).reshape(group * tok, width)
    qkv_grad = self_backward(owners, qkv, key_t, head_grad, head_mixed, self_total, tok)
    input_part = lax.psum_scatter(
        product_right(qkv_grad, head_qkv).astype(low_type),
        "shard",
        scatter_dimension=0,
        tiled=True,
    )
    input_grad = first_grad + input_part.astype(jnp.float32)
    slice_grad = jnp.concatenate(
        [product_left(all_inputs, qkv_grad), product_left(all_states, own_pair_grad)], 1
    ).astype(low_type)
    slice_grad = sum_over_rep(slice_grad).reshape(group, weight_rows, 5 * width)
    slice_grad = exchange(slice_grad).astype(jnp.float32)
    slice_grad = slice_grad.reshape(group, weight_rows, 5, width).transpose(1, 2, 0, 3)
    slice_grad = slice_grad.reshape(weight_rows, 5 * model)
    grad_self_qkv, grad_cross_kv = slice_grad[:, : 3 * model], slice_grad[:, 3 * model :]
    bias_self_q = in_columns(column_sums(qkv_grad[:, :width]))
    bias_self_v = in_columns(column_sums(qkv_grad[:, 2 * width :]))
    everywhere = bits_of("rep") + bits_of("shard")
    small = jnp.concatenate(
        [
            jnp.stack(
                [
                    bias_self_q,
                    bias_self_v,
                    bias_self_out,
                    bias_cross_q,
                    bias_cross_v,
                    bias_cross_out,
                    bias_fc2,
                    gain_one,
                    gain_two,
                    gain_three,
                    shift_one,
                    shift_two,
                    shift_three,
                ],
                0,
            ),
            bias_fc1.reshape(-1, model),
        ],
        0,
    )
    small = sum_over(small, everywhere)
    return (
        output,
        input_grad,
        enc_grad,
        grad_self_qkv,
        grad_self_out,
        grad_cross_q,
        grad_cross_kv,
        grad_cross_out,
        grad_fc1,
        grad_fc2,
        small[:7],
        small[13:].reshape(-1),
        small[7:10],
        small[10:13],
    )


def solution(mesh):
    rows, cut = P(("rep", "shard"), None), P("shard", None)
    return jax.shard_map(
        local,
        mesh=mesh,
        in_specs=(rows,) * 3 + (P("rep", None),) + (cut,) * 7 + (P(),) * 4,
        out_specs=(rows,) * 3 + (cut,) * 7 + (P(),) * 4,
        check_vma=False,
    )
```

time: 1870 us -> 1000 us (0.53)
  waiting for transfers between devices: 989 us -> 558 us
  matrix products: 541 us -> 140 us
  local copies, waits for them, and re-layouts: 198 us -> 50.2 us
  Pallas kernels: 0 us -> 111 us
  other arithmetic: 108 us -> 33.3 us
  starting transfers between devices: 1.35 us -> 46.3 us
  blocking collectives: 0 us -> 37.4 us
    reduce_scatter x6 -> x8, waiting for transfers between devices: 443 us -> 216 us  [the longest x5 131 us: reduce_weight(): lax.psum_scatter(product_left(former, latter).astype(low_type), 'shard',...]
    psum x2 -> x0, waiting for transfers between devices: 210 us -> none  [the longest x1 117 us: local(): lax.psum((bias_rows, bias_fc1, gain_rows, shift_rows), ('rep', 'shard'))]
    dot_general x103 -> x7, matrix products: 220 us -> 45 us  [product_right(): lax.dot_general(former, latter, (((1,), (1,)), ((), ())), preferred_eleme...]
    dot_general x71 -> x7, matrix products: 158 us -> 35.7 us  [product_left(): lax.dot_general(former, latter, (((0,), (0,)), ((), ())), preferred_eleme...]
    pallas_call x0 -> x4, Pallas kernels: none -> 111 us  [the longest x1 50.3 us: self_backward(): pl.pallas_call(functools.partial(self_backward_kernel, tok, width, group...]
    dot_general x71 -> x7, matrix products: 164 us -> 59.8 us  [product(): return jnp.dot(former, latter, preferred_element_type=jnp.float32)]
    all_to_all x0 -> x3, waiting for transfers between devices: none -> 86.2 us  [exchange(): lax.all_to_all(values, 'shard', split_axis=0, concat_axis=0, tiled=True)]
    unnamed x23 -> x16, waiting for transfers between devices: 70.9 us -> 4.64 us
  transfers between devices with their start and end apart: 20 -> 48, of which waited for: 14 -> 26; matrix products, arithmetic and copies ran while one was open for 36% -> 17% of each run, Pallas kernels for 0% -> 10%
where the time goes in v1:
time: 1000 us; the launch traced here: 992 us
  waiting for transfers between devices  558 us (56%)
  matrix products  140 us (14%)
  Pallas kernels  111 us (11%)
  local copies, waits for them, and re-layouts  50.2 us (5%)
  starting transfers between devices  46.3 us (5%)
  blocking collectives  37.4 us (4%)
  other arithmetic  33.3 us (3%)
  between operations  15.2 us (2%)
    all_gather x7, waiting for transfers between devices, gather_rows(): return lax.all_gather(values, 'shard', axis=0, tiled=True)  202 us
    reduce_scatter x5, waiting for transfers between devices, reduce_weight(): lax.psum_scatter(product_left(former, latter).astype(low_type), 'shard',...  131 us
    all_to_all x3, waiting for transfers between devices, exchange(): lax.all_to_all(values, 'shard', split_axis=0, concat_axis=0, tiled=True)  86.2 us
    dot_general x7, matrix products, product(): return jnp.dot(former, latter, preferred_element_type=jnp.float32)  59.8 us
    pallas_call x1, Pallas kernels, self_backward(): pl.pallas_call(functools.partial(self_backward_kernel, tok, width, group...  50.3 us
    ppermute x29, waiting for transfers between devices, flip(): return lax.ppermute(values, axis, [(i, i ^ bit) for i in range(size)])  48.7 us
    reduce_scatter x1, waiting for transfers between devices, local(): lax.psum_scatter(product_right(qkv_grad, head_qkv).astype(low_type), 'sha...  46.3 us
    dot_general x7, matrix products, product_right(): lax.dot_general(former, latter, (((1,), (1,)), ((), ())), preferred_eleme...  45 us
  transfers between devices with their start and end apart: 48, of which 26 were waited for; matrix products, arithmetic and copies ran while one was open for 17% of the time, Pallas kernels for 10%

profile of v1, /device:TPU:0, one launch (start us, length us, event | category | flops | bytes accessed | tf_op | source)
XLA Modules:
  0.0 992.0 jit_solution(13002636807737513900)
XLA Ops:
  13.0 6.3 all-to-all-start
  19.4 44.7 %all-to-all-done = bf16[8,128,640]{1,2,0:T(8,128)(2,1)S(1)} async-done(((bf16[8,128,640]{1,2,0:T(8,128)(2,1)}), bf16[8,128,640]{1,2,0:T(8,128)(2,1)S(1)}, u32[]{:S(2)}, u32[]{:S(2)}) %all-to-all-start) | async-done | bytes 1310752 | tf_op jit(solution)/shard_map/all_to_all | solution.py:367
  70.2 59.3 %all-gather.10.cloned.1.call-done = bf16[4096,1024]{1,0:T(8,128)(2,1)} async-done(((bf16[512,1024]{1,0:T(8,128)(2,1)}), bf16[4096,1024]{1,0:T(8,128)(2,1)}) %all-gather.10.cloned.1.call-update) | async-done | bytes 8388624 | tf_op jit(solution)/shard_map/all_gather | solution.py:363
  129.5 8.9 fusion.6
  145.8 36.4 %self_forward.1 = (bf16[4096,128]{1,0:T(8,128)(2,1)S(1)}, f32[8,8,512]{2,1,0:T(8,128)S(1)}) custom-call(s32[8]{0:T(128)S(1)} %select_reduce_fusion.owner, bf16[4096,384]{1,0:T(8,128)(2,1)S(1)} %copy.68.qkv, bf16[128,4096]{1,0:T(8,128)(2,1)S(1)} %get-tuple-element.54.value_t), custom_call_target="tpu_custom_call" | custom-call | flops 9663676416 | bytes 5242880 | tf_op jit(solution)/shard_map/self_forward/pallas_call | solution.py:205
  189.5 41.5 %all-to-all-done.1 = bf16[8,512,128]{1,2,0:T(8,128)(2,1)S(1)} async-done(((bf16[8,512,128]{1,2,0:T(8,128)(2,1)}), bf16[8,512,128]{1,2,0:T(8,128)(2,1)S(1)}, u32[]{:S(2)}, u32[]{:S(2)}) %all-to-all-start.1) | async-done | bytes 1048608 | tf_op jit(solution)/shard_map/all_to_all | solution.py:367
  240.6 10.9 %cross_forward.1 = (bf16[512,1024]{1,0:T(8,128)(2,1)S(1)}, f32[8,8,512]{2,1,0:T(8,128)S(1)}) custom-call(bf16[512,1024]{1,0:T(8,128)(2,1)S(1)} %multiply_convert_fusion.2.query, bf16[8,2,512,128]{3,2,1,0:T(8,128)(2,1)S(1)} %bitcast.126), custom_call_target="tpu_custom_call" | custom-call | flops 3221225472 | bytes 4194304 | tf_op jit(solution)/shard_map/cross_forward/pallas_call | solution.py:289
  251.5 11.4 %all-gather.18.cloned.1.call-done = bf16[1024,1024]{1,0:T(8,128)(2,1)} async-done(((bf16[128,1024]{1,0:T(8,128)(2,1)}), bf16[1024,1024]{1,0:T(8,128)(2,1)}) %all-gather.18.cloned.1.call-update) | async-done | bytes 2097168 | tf_op jit(solution)/shard_map/all_gather | solution.py:363
  268.3 77.8 %all-gather.20.cloned.1.call-done = bf16[1024,4096]{1,0:T(8,128)(2,1)} async-done(((bf16[128,4096]{1,0:T(8,128)(2,1)}), bf16[1024,4096]{1,0:T(8,128)(2,1)}) %all-gather.20.cloned.1.call-update) | async-done | bytes 8388624 | tf_op jit(solution)/shard_map/all_gather | solution.py:363
  346.1 28.4 %multiply_convert_fusion = (bf16[512,4096]{1,0:T(8,128)(2,1)}, f32[512,4096]{1,0:T(8,128)}, f32[512,4096]{1,0:T(8,128)}) fusion(f32[4096]{0:T(1024)S(1)} %copy-done.40, bf16[1024,4096]{1,0:T(8,128)(2,1)} %all-gather.20.cloned.1.call-done, f32[512,1024]{1,0:T(8,128)} %copy-done.10, f32[1024]{0:T(1024)S(1)} %bitcast.171, f32[1024]{0:T(1024)S(1)} %bitcast.158, ...), kind=kOutput, calls=%fused_computation.4 | convolution fusion | flops 4436000768 | bytes 31485952 | tf_op jit(solution)/shard_map/dot_general | solution.py:28
  374.6 53.8 %all-gather.22.cloned.1.call-done = bf16[4096,1024]{1,0:T(8,128)(2,1)} async-done(((bf16[512,1024]{1,0:T(8,128)(2,1)}), bf16[4096,1024]{1,0:T(8,128)(2,1)}) %all-gather.22.cloned.1.call-update) | async-done | bytes 8388624 | tf_op jit(solution)/shard_map/all_gather | solution.py:363
  428.3 9.9 fusion.48
  443.0 15.2 %convert_reduce_fusion = (f32[4096]{0:T(1024)S(1)}, bf16[512,4096]{1,0:T(8,128)(2,1)}) fusion(f32[512,4096]{1,0:T(8,128)} %get-tuple-element.52, f32[512,4096]{1,0:T(8,128)} %get-tuple-element.97, f32[4096]{0:T(1024)S(1)} %copy-done.40, bf16[512,1024]{1,0:T(8,128)(2,1)S(1)} %get-tuple-element.40, bf16[4096,1024]{1,0:T(8,128)(2,1)} %all-gather.22.cloned.1.call-done), kind=kOutput, calls=%fused_computation.2 | convolution fusion | flops 4330614784 | bytes 30441472 | tf_op jit(solution)/shard_map/dot_general | solution.py:38
  458.2 9.7 multiply_reduce_fusion
  472.9 13.9 %cross_backward.1 = (bf16[512,1024]{1,0:T(8,128)(2,1)S(1)}, bf16[8,2,512,128]{3,2,1,0:T(8,128)(2,1)}) custom-call(bf16[512,1024]{1,0:T(8,128)(2,1)S(1)} %multiply_convert_fusion.2.query, bf16[8,2,512,128]{3,2,1,0:T(8,128)(2,1)S(1)} %bitcast.127, bf16[512,1024]{1,0:T(8,128)(2,1)S(1)} %convolution_convert_fusion.8.mixed_grad, ...), custom_call_target="tpu_custom_call" | custom-call | flops 8053063680 | bytes 8388608 | tf_op jit(solution)/shard_map/cross_backward/pallas_call | solution.py:315
  486.9 5.5 multiply_reduce_fusion.1
  498.8 4.4 convolution_convert_fusion.4
  508.7 9.3 convolution_convert_fusion.1
  523.9 10.3 %convolution_convert_fusion = bf16[4096,1024]{1,0:T(8,128)(2,1)} fusion(bf16[512,4096]{1,0:T(8,128)(2,1)} %get-tuple-element.51, bf16[512,1024]{1,0:T(8,128)(2,1)} %copy-done.28), kind=kOutput, calls=%fused_computation.18 | convolution fusion | flops 4299161600 | bytes 13631488 | tf_op jit(solution)/shard_map/dot_general | solution.py:32
  537.8 37.4 %all_to_all.20 = bf16[8,512,128]{2,1,0:T(8,128)(2,1)S(1)} all-to-all(bf16[8,512,128]{2,1,0:T(8,128)(2,1)S(1)} %bitcast.132), channel_id=1, replica_groups=mesh['rep'=4,'shard'=8] {'shard'}, dimensions={0} | all-to-all | bytes 2097152 | tf_op jit(solution)/shard_map/all_to_all | solution.py:367
  575.2 50.3 %self_backward.1 = bf16[4096,384]{1,0:T(8,128)(2,1)} custom-call(s32[8]{0:T(128)S(1)} %select_reduce_fusion.owner, bf16[4096,384]{1,0:T(8,128)(2,1)} %copy-done, bf16[128,4096]{1,0:T(8,128)(2,1)S(1)} %copy-done.3, bf16[4096,128]{1,0:T(8,128)(2,1)S(1)} %bitcast.125, bf16[4096,128]{1,0:T(8,128)(2,1)S(1)} %copy-done.2, f32[8,8,512]{2,1,0:T(8,128)S(1)} %get-tuple-element.24.total), custom_call_target="tpu_custom_call" | custom-call | flops 24159191040 | bytes 10485760 | tf_op jit(solution)/shard_map/self_backward/pallas_call | solution.py:234
  625.5 8.7 convolution_convert_fusion.2
  638.0 6.1 fusion.14
  656.6 10.9 %collective-permute-done.24 = f32[17,1024]{1,0:T(8,128)} collective-permute-done((f32[17,1024]{1,0:T(8,128)S(1)}, f32[17,1024]{1,0:T(8,128)}, u32[]{:S(2)}, u32[]{:S(2)}) %collective-permute-start.24) | collective-permute-done | bytes 69664 | tf_op jit(solution)/shard_map/ppermute | solution.py:338
  676.8 4.4 collective-permute-done.25
  701.0 9.3 collective-permute-done.28
  716.3 43.1 %reduce-scatter.21.cloned.1.call-done = bf16[128,4096]{1,0:T(8,128)(2,1)} async-done(((bf16[1024,4096]{1,0:T(8,128)(2,1)}), bf16[128,4096]{1,0:T(8,128)(2,1)}) %reduce-scatter.21.cloned.1.call-update) | async-done | bytes 1048592 | tf_op jit(solution)/shard_map/reduce_scatter | solution.py:371
  767.4 34.8 %reduce-scatter.13.cloned.1.call-done = bf16[64,1024]{1,0:T(8,128)(2,1)} async-done(((bf16[512,1024]{1,0:T(8,128)(2,1)}), bf16[64,1024]{1,0:T(8,128)(2,1)}) %reduce-scatter.13.cloned.1.call-update) | async-done | bytes 131088 | tf_op jit(solution)/shard_map/reduce_scatter | solution.py:483
  803.8 88.3 %reduce-scatter.23.cloned.1.call-done = bf16[512,1024]{1,0:T(8,128)(2,1)} async-done(((bf16[4096,1024]{1,0:T(8,128)(2,1)}), bf16[512,1024]{1,0:T(8,128)(2,1)}) %reduce-scatter.23.cloned.1.call-update) | async-done | bytes 1048592 | tf_op jit(solution)/shard_map/reduce_scatter | solution.py:371
  915.8 4.9 collective-permute-done.19
  922.1 6.5 collective-permute-done.23
  936.0 46.3 %reduce-scatter.9.cloned.1.call-done = bf16[512,1024]{1,0:T(8,128)(2,1)} async-done(((bf16[4096,1024]{1,0:T(8,128)(2,1)}), bf16[512,1024]{1,0:T(8,128)(2,1)}) %reduce-scatter.9.cloned.1.call-update) | async-done | bytes 1048592 | tf_op jit(solution)/shard_map/reduce_scatter | solution.py:498
  (292 shorter events, 168.4 us)
Async XLA Ops:
  7.2 57.7 %all-gather.16.cloned.1.call-start = ((), (), s32[]{:S(2)}) async-start(), calls=%async_computation.15 | async-start | bytes 1179648 | tf_op jit(solution)/shard_map/all_gather | solution.py:363
  7.9 121.6 %all-gather.10.cloned.1.call-start = ((), (), s32[]{:S(2)}) async-start(), calls=%async_computation.12 | async-start | bytes 9437184 | tf_op jit(solution)/shard_map/all_gather | solution.py:363
  8.7 180.8 %all-gather.12.cloned.1.call-start = ((), (), s32[]{:S(2)}) async-start(), calls=%async_computation.13 | async-start | bytes 2359296 | tf_op jit(solution)/shard_map/all_gather | solution.py:363
  9.4 226.2 %all-gather.14.cloned.1.call-start = ((), (), s32[]{:S(2)}) async-start(), calls=%async_computation.14 | async-start | bytes 2359296 | tf_op jit(solution)/shard_map/all_gather | solution.py:363
  13.0 51.2 %all-to-all-start = ((bf16[8,128,640]{1,2,0:T(8,128)(2,1)}), bf16[8,128,640]{1,2,0:T(8,128)(2,1)S(1)}, u32[]{:S(2)}, u32[]{:S(2)}) async-start(bf16[8,128,640]{1,2,0:T(8,128)(2,1)} %bitcast.4), calls=%async_computation | async-start | bytes 2621440 | tf_op jit(solution)/shard_map/all_to_all | solution.py:367
  19.3 219.7 %all-gather.24.cloned.1.call-start = ((), (), s32[]{:S(2)}) async-start(), calls=%async_computation.27 | async-start | bytes 2359296 | tf_op jit(solution)/shard_map/all_gather | solution.py:443
  68.0 194.9 %all-gather.18.cloned.1.call-start = ((), (), s32[]{:S(2)}) async-start(), calls=%async_computation.16 | async-start | bytes 2359296 | tf_op jit(solution)/shard_map/all_gather | solution.py:363
  68.6 277.5 %all-gather.20.cloned.1.call-start = ((), (), s32[]{:S(2)}) async-start(), calls=%async_computation.17 | async-start | bytes 9437184 | tf_op jit(solution)/shard_map/all_gather | solution.py:363
  69.3 359.0 %all-gather.22.cloned.1.call-start = ((), (), s32[]{:S(2)}) async-start(), calls=%async_computation.18 | async-start | bytes 9437184 | tf_op jit(solution)/shard_map/all_gather | solution.py:363
  185.5 45.4 %all-to-all-start.1 = ((bf16[8,512,128]{1,2,0:T(8,128)(2,1)}), bf16[8,512,128]{1,2,0:T(8,128)(2,1)S(1)}, u32[]{:S(2)}, u32[]{:S(2)}) async-start(bf16[8,512,128]{1,2,0:T(8,128)(2,1)} %copy.69), calls=%async_computation.1 | async-start | bytes 2097152 | tf_op jit(solution)/shard_map/all_to_all | solution.py:367
  189.1 332.2 %reduce-scatter.11.cloned.1.call-start = ((), (), s32[]{:S(2)}) async-start(), calls=%async_computation.20 | async-start | bytes 2359296 | tf_op jit(solution)/shard_map/reduce_scatter | solution.py:478
  486.8 160.7 %reduce-scatter.15.cloned.1.call-start = ((), (), s32[]{:S(2)}) async-start(), calls=%async_computation.22 | async-start | bytes 2359296 | tf_op jit(solution)/shard_map/reduce_scatter | solution.py:371
  498.8 155.0 %reduce-scatter.17.cloned.1.call-start = ((), (), s32[]{:S(2)}) async-start(), calls=%async_computation.23 | async-start | bytes 2359296 | tf_op jit(solution)/shard_map/reduce_scatter | solution.py:371
  503.3 152.3 %reduce-scatter.19.cloned.1.call-start = ((), (), s32[]{:S(2)}) async-start(), calls=%async_computation.24 | async-start | bytes 2359296 | tf_op jit(solution)/shard_map/reduce_scatter | solution.py:371
  507.1 252.4 %reduce-scatter.21.cloned.1.call-start = ((), (), s32[]{:S(2)}) async-start(), calls=%async_computation.25 | async-start | bytes 9437184 | tf_op jit(solution)/shard_map/reduce_scatter | solution.py:371
  518.0 284.2 %reduce-scatter.13.cloned.1.call-start = ((), (), s32[]{:S(2)}) async-start(), calls=%async_computation.21 | async-start | bytes 1179648 | tf_op jit(solution)/shard_map/reduce_scatter | solution.py:483
  523.9 368.2 %reduce-scatter.23.cloned.1.call-start = ((), (), s32[]{:S(2)}) async-start(), calls=%async_computation.26 | async-start | bytes 9437184 | tf_op jit(solution)/shard_map/reduce_scatter | solution.py:371
  534.3 448.0 %reduce-scatter.9.cloned.1.call-start = ((), (), s32[]{:S(2)}) async-start(), calls=%async_computation.19 | async-start | bytes 9437184 | tf_op jit(solution)/shard_map/reduce_scatter | solution.py:498
  644.7 47.3 %collective-permute-start.2 = (bf16[512,640]{0,1:T(8,128)(2,1)S(1)}, bf16[512,640]{0,1:T(8,128)(2,1)}, u32[]{:S(2)}, u32[]{:S(2)}) collective-permute-start(bf16[512,640]{0,1:T(8,128)(2,1)S(1)} %get-tuple-element.57), channel_id=1, source_target_pairs={{0,16},{8,24},{16,0},{24,8},{1,17},{9,25},{17,1},{25,9},{2,18},{10... | collective-permute-start | bytes 1966088 | tf_op jit(solution)/shard_map/ppermute | solution.py:338
  646.0 49.1 %collective-permute-start = (bf16[512,640]{0,1:T(8,128)(2,1)S(1)}, bf16[512,640]{0,1:T(8,128)(2,1)S(1)}, u32[]{:S(2)}, u32[]{:S(2)}) collective-permute-start(bf16[512,640]{0,1:T(8,128)(2,1)S(1)} %get-tuple-element.56), channel_id=1, source_target_pairs={{0,8},{8,0},{16,24},{24,16},{1,9},{9,1},{17,25},{25,17},{2,10},{10... | collective-permute-start | bytes 1966088 | tf_op jit(solution)/shard_map/ppermute | solution.py:338
  648.6 21.2 %collective-permute-start.4 = (bf16[64,1024]{1,0:T(8,128)(2,1)S(1)}, bf16[64,1024]{1,0:T(8,128)(2,1)S(1)}, u32[]{:S(2)}, u32[]{:S(2)}) collective-permute-start(bf16[64,1024]{1,0:T(8,128)(2,1)S(1)} %get-tuple-element.76), channel_id=1, source_target_pairs={{0,8},{8,0},{16,24},{24,16},{1,9},{9,1},{17,25},{25,17},{2,10},{10... | collective-permute-start | bytes 393224 | tf_op jit(solution)/shard_map/ppermute | solution.py:338
  649.2 21.2 %collective-permute-start.6 = (bf16[64,1024]{1,0:T(8,128)(2,1)S(1)}, bf16[64,1024]{1,0:T(8,128)(2,1)S(1)}, u32[]{:S(2)}, u32[]{:S(2)}) collective-permute-start(bf16[64,1024]{1,0:T(8,128)(2,1)S(1)} %get-tuple-element.77), channel_id=1, source_target_pairs={{0,16},{8,24},{16,0},{24,8},{1,17},{9,25},{17,1},{25,9},{2,18},{10... | collective-permute-start | bytes 393224 | tf_op jit(solution)/shard_map/ppermute | solution.py:338
  693.2 17.1 %collective-permute-start.3 = (bf16[512,640]{0,1:T(8,128)(2,1)S(1)}, bf16[512,640]{0,1:T(8,128)(2,1)S(1)}, u32[]{:S(2)}, u32[]{:S(2)}) collective-permute-start(bf16[512,640]{0,1:T(8,128)(2,1)S(1)} %add_convert_fusion.6), channel_id=1, source_target_pairs={{0,8},{8,0},{16,24},{24,16},{1,9},{9,1},{17,25},{25,17},{2,10},{10... | collective-permute-start | bytes 1966088 | tf_op jit(solution)/shard_map/ppermute | solution.py:338
  695.3 15.4 %collective-permute-start.1 = (bf16[512,640]{0,1:T(8,128)(2,1)S(1)}, bf16[512,640]{0,1:T(8,128)(2,1)S(1)}, u32[]{:S(2)}, u32[]{:S(2)}) collective-permute-start(bf16[512,640]{0,1:T(8,128)(2,1)S(1)} %add_convert_fusion.8), channel_id=1, source_target_pairs={{0,16},{8,24},{16,0},{24,8},{1,17},{9,25},{17,1},{25,9},{2,18},{10... | collective-permute-start | bytes 1966088 | tf_op jit(solution)/shard_map/ppermute | solution.py:338
  712.2 188.7 %all-to-all-start.3 = ((bf16[8,128,640]{1,2,0:T(8,128)(2,1)}), bf16[8,128,640]{1,2,0:T(8,128)(2,1)S(1)}, u32[]{:S(2)}, u32[]{:S(2)}) async-start(bf16[8,128,640]{1,2,0:T(8,128)(2,1)} %copy_bitcast_fusion.1), calls=%async_computation.6 | async-start | bytes 2621440 | tf_op jit(solution)/shard_map/all_to_all | solution.py:367
  761.7 135.6 %collective-permute-start.16 = (bf16[64,4096]{1,0:T(8,128)(2,1)}, bf16[64,4096]{1,0:T(8,128)(2,1)S(1)}, u32[]{:S(2)}, u32[]{:S(2)}) collective-permute-start(bf16[64,4096]{1,0:T(8,128)(2,1)} %get-tuple-element.64), channel_id=1, source_target_pairs={{0,8},{8,0},{16,24},{24,16},{1,9},{9,1},{17,25},{25,17},{2,10},{10... | collective-permute-start | bytes 1572872 | tf_op jit(solution)/shard_map/ppermute | solution.py:338
  764.0 134.1 %collective-permute-start.18 = (bf16[64,4096]{1,0:T(8,128)(2,1)S(1)}, bf16[64,4096]{1,0:T(8,128)(2,1)}, u32[]{:S(2)}, u32[]{:S(2)}) collective-permute-start(bf16[64,4096]{1,0:T(8,128)(2,1)S(1)} %get-tuple-element.65), channel_id=1, source_target_pairs={{0,16},{8,24},{16,0},{24,8},{1,17},{9,25},{17,1},{25,9},{2,18},{10... | collective-permute-start | bytes 1572872 | tf_op jit(solution)/shard_map/ppermute | solution.py:338
  894.4 16.6 %collective-permute-start.20 = (bf16[256,1024]{1,0:T(8,128)(2,1)}, bf16[256,1024]{1,0:T(8,128)(2,1)}, u32[]{:S(2)}, u32[]{:S(2)}) collective-permute-start(bf16[256,1024]{1,0:T(8,128)(2,1)} %get-tuple-element.60), channel_id=1, source_target_pairs={{0,8},{8,0},{16,24},{24,16},{1,9},{9,1},{17,25},{25,17},{2,10},{10... | collective-permute-start | bytes 1572872 | tf_op jit(solution)/shard_map/ppermute | solution.py:338
  900.5 20.2 %collective-permute-start.19 = (bf16[64,4096]{1,0:T(8,128)(2,1)}, bf16[64,4096]{1,0:T(8,128)(2,1)}, u32[]{:S(2)}, u32[]{:S(2)}) collective-permute-start(bf16[64,4096]{1,0:T(8,128)(2,1)} %get-tuple-element.63), channel_id=1, source_target_pairs={{0,8},{8,0},{16,24},{24,16},{1,9},{9,1},{17,25},{25,17},{2,10},{10... | collective-permute-start | bytes 1572872 | tf_op jit(solution)/shard_map/ppermute | solution.py:338
  910.4 23.9 %collective-permute-start.17 = (bf16[64,4096]{1,0:T(8,128)(2,1)S(1)}, bf16[64,4096]{1,0:T(8,128)(2,1)S(1)}, u32[]{:S(2)}, u32[]{:S(2)}) collective-permute-start(bf16[64,4096]{1,0:T(8,128)(2,1)S(1)} %get-tuple-element.62), channel_id=1, source_target_pairs={{0,16},{8,24},{16,0},{24,8},{1,17},{9,25},{17,1},{25,9},{2,18},{10... | collective-permute-start | bytes 1572872 | tf_op jit(solution)/shard_map/ppermute | solution.py:338
  912.6 16.0 %collective-permute-start.23 = (bf16[256,1024]{1,0:T(8,128)(2,1)S(1)}, bf16[256,1024]{1,0:T(8,128)(2,1)S(1)}, u32[]{:S(2)}, u32[]{:S(2)}) collective-permute-start(bf16[256,1024]{1,0:T(8,128)(2,1)S(1)} %get-tuple-element.59), channel_id=1, source_target_pairs={{0,8},{8,0},{16,24},{24,16},{1,9},{9,1},{17,25},{25,17},{2,10},{10... | collective-permute-start | bytes 1572872 | tf_op jit(solution)/shard_map/ppermute | solution.py:338
  914.1 18.4 %collective-permute-start.21 = (bf16[256,1024]{1,0:T(8,128)(2,1)S(1)}, bf16[256,1024]{1,0:T(8,128)(2,1)S(1)}, u32[]{:S(2)}, u32[]{:S(2)}) collective-permute-start(bf16[256,1024]{1,0:T(8,128)(2,1)S(1)} %get-tuple-element.58), channel_id=1, source_target_pairs={{0,16},{8,24},{16,0},{24,8},{1,17},{9,25},{17,1},{25,9},{2,18},{10... | collective-permute-start | bytes 1572872 | tf_op jit(solution)/shard_map/ppermute | solution.py:338
  (59 other events, 838.4 us)
Sparse Core Ops, SparseCore 0:
  9.6 31.9 all-gather.15
  43.2 86.2 all-gather.9
  131.1 28.0 all-gather.11
  160.6 28.5 all-gather.13
  191.3 42.6 all-gather.23
  235.5 27.4 all-gather.17
  264.5 81.5 all-gather.19
  347.7 80.5 all-gather.21
  487.0 34.3 reduce-scatter.10
  523.4 41.1 reduce-scatter.14
  567.0 42.2 reduce-scatter.16
  612.0 34.3 reduce-scatter.18
  648.8 110.6 reduce-scatter.20
  762.2 39.9 reduce-scatter.12
  804.3 87.7 reduce-scatter.22
  894.3 87.9 reduce-scatter.8

commit v2 on v1

--- a/solution.py
+++ b/solution.py
@@ -14,7 +14,7 @@
 masked_score = -1000000000.0
 norm_epsilon = 1e-05
 low_type = jnp.bfloat16
-MESH_AXES = ("rep", "shard")
+SHARD = ("line", "core")
 
 
 def norm_rows(values, gain_row, shift_row):
@@ -54,10 +54,26 @@
     return key_index <= query_index
 
 
-def self_forward_kernel(tok, width, half, owner, qkv, value_t, mixed, total):
+def turn_columns(source, start, out, tok):
+    width, rows = out.shape
+    for row in range(0, rows, tok):
+        block = source[row : row + tok, start : start + width]
+        out[:, row : row + tok] = jnp.transpose(block)
+
+
+def self_forward_kernel(tok, width, half, place, owner, *refs):
+    blocks, (weight, bias, scale, qkv, mixed, total, value_t) = refs[:-7], refs[-7:]
     slot = pl.program_id(0)
     heads = width // HEAD_DIM
-    base = pl.multiple_of(owner[slot] * tok, tok)
+
+    @pl.when(slot == 0)
+    def _():
+        for index, block in enumerate(blocks):
+            rows = (product(block[...], weight[...]) + bias[...]) * scale[...]
+            qkv[index * tok : (index + 1) * tok, :] = rows.astype(low_type)
+        turn_columns(qkv, 2 * width, value_t, tok)
+
+    base = pl.multiple_of(place[slot] * tok, tok)
     query = qkv[pl.ds(base, tok), :width]
 
     def step(start, carry, causal):
@@ -88,30 +104,47 @@
     )
     whole = jnp.minimum(slot, half)
     carry = lax.fori_loop(
-        0, whole, lambda j, c: step(pl.multiple_of(owner[j] * tok, tok), c, False), first
+        0, whole, lambda j, c: step(pl.multiple_of(place[j] * tok, tok), c, False), first
     )
     carry = step(base, carry, True)
     mix = jnp.concatenate([part[2] / part[1] for part in carry], 0)
-    mixed[pl.ds(base, tok), :] = jnp.transpose(mix).astype(low_type)
+    target = pl.multiple_of(owner[slot] * tok, tok)
+    mixed[pl.ds(target, tok), :] = jnp.transpose(mix).astype(low_type)
     for head in range(heads):
         total[head : head + 1, :] = carry[head][0] + jnp.log(carry[head][1])
 
 
 def self_backward_kernel(
-    tok, width, half, scale, owner, qkv, key_t, mixed_grad, mixed, total, out, key_sum, value_sum
+    tok,
+    width,
+    half,
+    scale,
+    place,
+    owner,
+    qkv,
+    mixed_grad,
+    mixed,
+    total,
+    out,
+    placed,
+    key_t,
+    key_sum,
+    value_sum,
 ):
     slot = pl.program_id(0)
     heads = width // HEAD_DIM
-    base = pl.multiple_of(owner[slot] * tok, tok)
 
     @pl.when(slot == 0)
     def _():
+        turn_columns(qkv, width, key_t, tok)
         key_sum[...] = jnp.zeros_like(key_sum)
         value_sum[...] = jnp.zeros_like(value_sum)
 
+    base = pl.multiple_of(place[slot] * tok, tok)
+    target = pl.multiple_of(owner[slot] * tok, tok)
     query = qkv[pl.ds(base, tok), :width]
-    grad = mixed_grad[pl.ds(base, tok), :]
-    both = grad.astype(jnp.float32) * mixed[pl.ds(base, tok), :].astype(jnp.float32)
+    grad = mixed_grad[pl.ds(target, tok), :]
+    both = grad.astype(jnp.float32) * mixed[pl.ds(target, tok), :].astype(jnp.float32)
     both = jnp.transpose(both)
     deltas = [jnp.sum(both[head_columns(h)], 0, keepdims=True) for h in range(heads)]
     totals = [total[h : h + 1, :] for h in range(heads)]
@@ -139,16 +172,25 @@
     first = tuple(jnp.zeros((HEAD_DIM, tok), jnp.float32) for _ in range(heads))
     whole = jnp.minimum(slot, half)
     carry = lax.fori_loop(
-        0, whole, lambda j, c: step(pl.multiple_of(owner[j] * tok, tok), c, False), first
+        0, whole, lambda j, c: step(pl.multiple_of(place[j] * tok, tok), c, False), first
     )
     carry = step(base, carry, True)
-    query_grad = jnp.transpose(jnp.concatenate(carry, 0)).astype(low_type)
-    out[pl.ds(base, tok), :width] = query_grad * scale
+    query_grad = jnp.transpose(jnp.concatenate(carry, 0)).astype(low_type) * scale
+    placed[pl.ds(base, tok), :width] = query_grad
 
     @pl.when(slot == pl.num_programs(0) - 1)
     def _():
-        out[:, width : 2 * width] = key_sum[...].astype(low_type)
-        out[:, 2 * width :] = value_sum[...].astype(low_type)
+        placed[:, width : 2 * width] = key_sum[...].astype(low_type)
+        placed[:, 2 * width :] = value_sum[...].astype(low_type)
+
+        def move(p, carry):
+            source = pl.multiple_of(place[p] * tok, tok)
+            out[pl.ds(pl.multiple_of(owner[p] * tok, tok), tok), :] = placed[
+                pl.ds(source, tok), :
+            ]
+            return carry
+
+        lax.fori_loop(0, pl.num_programs(0), move, 0)
 
 
 def cross_forward_kernel(width, query, pair, mixed, total):
@@ -198,36 +240,42 @@
     return pl.BlockSpec(shape, lambda *_: (0,) * len(shape), pipeline_mode=pl.Buffered(1))
 
 
-def self_forward(owners, qkv, value_t, tok):
-    rows, width = qkv.shape[0], qkv.shape[1] // 3
-    group = rows // tok
+def self_forward(place, owner, blocks, weight, bias, scale):
+    tok, group = blocks[0].shape[0], len(blocks)
+    width = weight.shape[1] // 3
+    rows = group * tok
     pairs = group * (group // 4 + 1)
+    bias, scale = bias[None], scale[None]
+    inputs = (*blocks, weight, bias, scale)
     return pl.pallas_call(
         functools.partial(self_forward_kernel, tok, width, group // 2),
         out_shape=(
+            jax.ShapeDtypeStruct((rows, 3 * width), low_type),
             jax.ShapeDtypeStruct((rows, width), low_type),
             jax.ShapeDtypeStruct((group, 8, tok), jnp.float32),
         ),
         grid_spec=pltpu.PrefetchScalarGridSpec(
-            num_scalar_prefetch=1,
+            num_scalar_prefetch=2,
             grid=(group,),
-            in_specs=[whole_block(qkv.shape), whole_block(value_t.shape)],
+            in_specs=[whole_block(each.shape) for each in inputs],
             out_specs=[
+                pl.BlockSpec((rows, 3 * width), lambda *_: (0, 0)),
                 pl.BlockSpec((rows, width), lambda *_: (0, 0)),
-                pl.BlockSpec((None, 8, tok), lambda p, _: (p, 0, 0)),
+                pl.BlockSpec((None, 8, tok), lambda p, *_: (p, 0, 0)),
             ],
-        ),
-        compiler_params=kernel_options(40),
+            scratch_shapes=[pltpu.VMEM((width, rows), low_type)],
+        ),
+        compiler_params=kernel_options(52),
         cost_estimate=pl.CostEstimate(
             flops=pairs * tok * tok * width * 12,
             transcendentals=pairs * tok * tok * (width // HEAD_DIM),
-            bytes_accessed=rows * width * 10,
+            bytes_accessed=rows * (width * 10 + weight.shape[0] * 2),
         ),
         name="self_forward",
-    )(owners, qkv, value_t)
-
-
-def self_backward(owners, qkv, key_t, mixed_grad, mixed, total, tok):
+    )(place, owner, *inputs)
+
+
+def self_backward(place, owner, qkv, mixed_grad, mixed, total, tok):
     rows, width = qkv.shape[0], qkv.shape[1] // 3
     group = rows // tok
     pairs = group * (group // 4 + 1)
@@ -235,31 +283,34 @@
         functools.partial(
             self_backward_kernel, tok, width, group // 2, HEAD_DIM ** (-0.5)
         ),
-        out_shape=jax.ShapeDtypeStruct(qkv.shape, low_type),
+        out_shape=(
+            jax.ShapeDtypeStruct(qkv.shape, low_type),
+            jax.ShapeDtypeStruct(qkv.shape, low_type),
+        ),
         grid_spec=pltpu.PrefetchScalarGridSpec(
-            num_scalar_prefetch=1,
+            num_scalar_prefetch=2,
             grid=(group,),
             in_specs=[
                 whole_block(qkv.shape),
-                whole_block(key_t.shape),
                 whole_block(mixed_grad.shape),
                 whole_block(mixed.shape),
-                pl.BlockSpec((None, 8, tok), lambda p, _: (p, 0, 0)),
+                pl.BlockSpec((None, 8, tok), lambda p, *_: (p, 0, 0)),
             ],
-            out_specs=pl.BlockSpec(qkv.shape, lambda *_: (0, 0)),
+            out_specs=[pl.BlockSpec(qkv.shape, lambda *_: (0, 0))] * 2,
             scratch_shapes=[
+                pltpu.VMEM((width, rows), low_type),
                 pltpu.VMEM((rows, width), jnp.float32),
                 pltpu.VMEM((rows, width), jnp.float32),
             ],
         ),
-        compiler_params=kernel_options(48),
+        compiler_params=kernel_options(52),
         cost_estimate=pl.CostEstimate(
             flops=pairs * tok * tok * width * 30,
             transcendentals=pairs * tok * tok * (width // HEAD_DIM),
             bytes_accessed=rows * width * 20,
         ),
         name="self_backward",
-    )(owners, qkv, key_t, mixed_grad, mixed, total)
+    )(place, owner, qkv, mixed_grad, mixed, total)
 
 
 def split_columns(values, group):
@@ -332,46 +383,73 @@
     return of_heads(query_grad, group), pair_grad
 
 
-def flip(values, axis_bit):
-    axis, bit = axis_bit
+def swap(values, axis, offset):
     size = lax.axis_size(axis)
-    return lax.ppermute(values, axis, [(i, i ^ bit) for i in range(size)])
-
-
-def bits_of(axis):
-    size = lax.axis_size(axis)
-    return [(axis, 1 << i) for i in range(size.bit_length() - 1)]
-
-
-def sum_over(values, bits):
-    for bit in bits:
+    return lax.ppermute(values, axis, [(i, i ^ offset) for i in range(size)])
+
+
+def sum_over(values, steps):
+    for axis, offset in steps:
         values = (
-            values.astype(jnp.float32) + flip(values, bit).astype(jnp.float32)
+            values.astype(jnp.float32) + swap(values, axis, offset).astype(jnp.float32)
         ).astype(values.dtype)
     return values
 
 
-def sum_over_rep(values):
-    bits = bits_of("rep")
-    middle = values.shape[0] // 2
-    return jnp.concatenate(
-        [sum_over(values[:middle], bits), sum_over(values[middle:], bits[::-1])], 0
-    )
+def bits_of(axis):
+    return [(axis, 1 << i) for i in range(lax.axis_size(axis).bit_length() - 1)]
+
+
+def spread_over_rep(values):
+    return [values] + [swap(values, "rep", d) for d in range(1, lax.axis_size("rep"))]
+
+
+def rep_order(pieces):
+    own = lax.axis_index("rep")
+    count = len(pieces)
+    return [lax.select_n(own, *[pieces[d ^ i] for i in range(count)]) for d in range(count)]
+
+
+def trade_over_rep(pieces):
+    return [pieces[0]] + [swap(pieces[d], "rep", d) for d in range(1, len(pieces))]
+
+
+def sum_of(terms):
+    return sum(term.astype(jnp.float32) for term in terms)
+
+
+def scatter_over_line(values):
+    line, own = lax.axis_size("line"), lax.axis_index("line")
+    terms = [lax.dynamic_index_in_dim(values, own, 0, keepdims=False)]
+    for k in range(1, line):
+        piece = lax.dynamic_index_in_dim(values, (own + k) % line, 0, keepdims=False)
+        terms.append(lax.ppermute(piece, "line", [(i, (i + k) % line) for i in range(line)]))
+    return sum_of(terms)
+
+
+def stage(values):
+    return lax.optimization_barrier(values)
+
+
+def shift(values):
+    line = lax.axis_size("line")
+    return lax.ppermute(values, "line", [(i, (i + 1) % line) for i in range(line)])
 
 
 def gather_rows(values):
-    return lax.all_gather(values, "shard", axis=0, tiled=True)
+    return lax.all_gather(values, SHARD, axis=0, tiled=True)
+
+
+def scatter_rows(values):
+    return lax.psum_scatter(values, SHARD, scatter_dimension=0, tiled=True)
 
 
 def exchange(values):
-    return lax.all_to_all(values, "shard", split_axis=0, concat_axis=0, tiled=True)
-
-
-def reduce_weight(former, latter):
-    reduced = lax.psum_scatter(
-        product_left(former, latter).astype(low_type), "shard", scatter_dimension=0, tiled=True
-    )
-    return sum_over_rep(reduced).astype(jnp.float32)
+    return lax.all_to_all(values, SHARD, split_axis=0, concat_axis=0, tiled=True)
+
+
+def gelu(values):
+    return jax.nn.gelu(values, approximate=False)
 
 
 def local(
@@ -391,11 +469,15 @@
     norm_gains,
     norm_shifts,
 ):
-    group = lax.axis_size("shard")
-    member = lax.axis_index("shard")
+    reps, line = lax.axis_size("rep"), lax.axis_size("line")
+    rep, core = lax.axis_index("rep"), lax.axis_index("core")
+    group = 2 * line
+    member = 2 * lax.axis_index("line") + core
     tok, model = layer_input.shape
+    feed = w_fc1.shape[1]
     weight_rows = w_self_qkv.shape[0]
     width = model // group
+    unit = feed // (group * reps)
     score_scale = HEAD_DIM ** (-0.5)
     slot_table = placement[0]
     device_ids = jnp.arange(group, dtype=jnp.int32)
@@ -411,36 +493,102 @@
 
     slices = jnp.concatenate(
         [
-            w_self_qkv.reshape(weight_rows, 3, group, width),
-            w_cross_kv.reshape(weight_rows, 2, group, width),
+            w_self_qkv.reshape(reps, weight_rows // reps, 3, group, width),
+            w_cross_kv.reshape(reps, weight_rows // reps, 2, group, width),
         ],
-        1,
-    )
-    slices = slices.transpose(2, 0, 1, 3).reshape(group, weight_rows, 5 * width)
-    slices = exchange(slices).reshape(model, 5 * width)
-    head_qkv, head_ckv = slices[:, : 3 * width], slices[:, 3 * width :]
-    all_inputs = gather_rows(layer_input)
-    all_states = gather_rows(encoder_states)
-    full_out = gather_rows(w_self_out)
-    full_cross_q = gather_rows(w_cross_q)
-    full_cross_out = gather_rows(w_cross_out)
-    wfirst = gather_rows(w_fc1)
-    wsecond = gather_rows(w_fc2)
+        2,
+    )
+    slices = lax.dynamic_index_in_dim(slices, rep, 0, keepdims=False)
+    slices = slices.transpose(2, 0, 1, 3).reshape(group, weight_rows // reps, 5 * width)
+    first_cut = w_fc1.reshape(weight_rows, line, 2, reps, unit)
+    first_cut = lax.dynamic_index_in_dim(first_cut, rep, 3, keepdims=False)
+    first_own = lax.dynamic_index_in_dim(first_cut, core, 2, keepdims=False)
+    first_other = lax.dynamic_index_in_dim(first_cut, 1 - core, 2, keepdims=False)
+    first_own = first_own.reshape(weight_rows, line * unit)
+    first_other = swap(first_other.reshape(weight_rows, line * unit), "core", 1)
+    first_cut = jnp.where(
+        core == 0,
+        jnp.concatenate([first_own, first_other], 0),
+        jnp.concatenate([first_other, first_own], 0),
+    )
+    second_cut = lax.dynamic_slice_in_dim(w_fc2, rep * unit, unit, 0)
+    bias_cut = lax.dynamic_index_in_dim(
+        fc1_bias.reshape(line, 2, reps, unit), core, 1, keepdims=False
+    )
+    bias_cut = [bias_cut[:, r].reshape(line * unit) for r in range(reps)]
+    bias_cut = rep_order(bias_cut)
+
+    square = jnp.stack([w_self_out, w_cross_q, w_cross_out], 0)
+    square = square.reshape(3, reps, weight_rows // reps, model)
+    square = lax.dynamic_index_in_dim(square, rep, 1, keepdims=False)
+    square = square.reshape(-1, model // (line * unit), line * unit).transpose(1, 0, 2)
+    square = square.reshape(-1, line * unit)
 
     inputs = layer_input.astype(jnp.float32)
     zeros = jnp.zeros((width,), jnp.float32)
     head_bias = jnp.concatenate([own_columns(proj_biases[0]), zeros, own_columns(proj_biases[1])])
     head_scale = jnp.concatenate([jnp.full((width,), score_scale), jnp.ones((2 * width,))])
-    qkv = ((product(all_inputs, head_qkv) + head_bias) * head_scale).astype(low_type)
-    key_t, value_t = jnp.transpose(qkv[:, width : 2 * width]), jnp.transpose(qkv[:, 2 * width :])
-    head_mixed, self_total = self_forward(owners, qkv, value_t, tok)
-    self_low = join_columns(exchange(head_mixed.reshape(group, tok, width)))
-
     cross_bias = jnp.concatenate([zeros, own_columns(proj_biases[4])])
+
+    slices = exchange(slices)
+    both_cut = lax.all_gather(
+        jnp.concatenate([first_cut, square], 0), "line", axis=0, tiled=True
+    ).reshape(line, -1, line * unit)
+    near, far = [1 << i for i in range(reps.bit_length() - 1)], []
+    far = [d for d in range(1, reps) if d not in near]
+    block, slices, both_cut = stage((layer_input, slices, both_cut))
+
+    blocks = [block, swap(block, "core", 1)]
+    block = shift(block)
+    slices = spread_over_rep(slices)
+    block, slices, blocks, encoder_states = stage((block, slices, blocks, encoder_states))
+
+    blocks += [block, swap(block, "core", 1)]
+    block = shift(block)
+    square = spread_over_rep(both_cut[:, 2 * weight_rows :])
+    slices = jnp.stack(rep_order(slices), 1).reshape(model, 5 * width)
+    head_qkv, head_ckv = slices[:, : 3 * width], slices[:, 3 * width :]
+    all_states = gather_rows(encoder_states)
+    block, square, blocks, all_states, head_ckv, head_qkv = stage(
+        (block, square, blocks, all_states, head_ckv, head_qkv)
+    )
+
+    for step in range(line - 2):
+        blocks += [block, swap(block, "core", 1)]
+        if step < line - 3:
+            block = shift(block)
+    wfirst = {0: both_cut[:, : 2 * weight_rows].reshape(model, line * unit)}
+    wfirst.update({d: swap(wfirst[0], "rep", d) for d in near})
+    square = jnp.stack(rep_order(square), 1)
+    other = swap(square, "core", 1)
     head_pair = (product(all_states, head_ckv) + cross_bias).astype(low_type)
-    states = all_states.shape[0]
     head_pair = split_columns(head_pair, 2)
-    pairs = lax.all_gather(head_pair, "shard", axis=0, tiled=False)
+    blocks, wfirst, other, square, head_pair, second_cut = stage(
+        (blocks, wfirst, other, square, head_pair, second_cut)
+    )
+
+    wfirst.update({d: swap(wfirst[0], "rep", d) for d in far})
+    wsecond = {0: lax.all_gather(second_cut, "line", axis=0, tiled=True)}
+    back = (lax.axis_index("line") - owners // 2) % line
+    places = 2 * back + ((owners % 2) ^ core)
+    qkv, head_mixed, self_total = self_forward(
+        places, owners, blocks, head_qkv, head_bias, head_scale
+    )
+    all_inputs = jnp.concatenate(blocks, 0)
+    square = jnp.where(core == 0, jnp.stack([square, other], 1), jnp.stack([other, square], 1))
+    square = square.reshape(line, 2, reps, -1, 3, weight_rows // reps, line * unit)
+    full_out, full_cross_q, full_cross_out = [
+        square[:, :, :, :, i].transpose(0, 1, 2, 4, 3, 5).reshape(model, model)
+        for i in range(3)
+    ]
+    head_mixed, wfirst, wsecond = stage((head_mixed, wfirst, wsecond))
+
+    wsecond.update({d: swap(wsecond[0], "rep", d) for d in near})
+    pairs = lax.all_gather(head_pair, SHARD, axis=0, tiled=False)
+    self_low = exchange(head_mixed.reshape(group, tok, width))
+    self_low, wsecond, pairs, all_inputs = stage((self_low, wsecond, pairs, all_inputs))
+    wsecond.update({d: swap(wsecond[0], "rep", d) for d in far})
+    self_low = join_columns(self_low)
 
     first_sum = inputs + (product(self_low, full_out) + proj_biases[2])
     first_norm, norm1_back = jax.vjp(norm_rows, first_sum, norm_gains[0], norm_shifts[0])
@@ -449,70 +597,130 @@
         low_type
     )
     cross_low, cross_total = cross_forward(cross_queries, pairs)
+    cross_low, wsecond = stage((cross_low, wsecond))
     second_sum = first_norm + (product(cross_low, full_cross_out) + proj_biases[5])
     second_norm, norm2_back = jax.vjp(norm_rows, second_sum, norm_gains[1], norm_shifts[1])
     second_low = second_norm.astype(low_type)
-    pre_act = product(second_low, wfirst) + fc1_bias
-    hidden, gelu_back = jax.vjp(lambda values: jax.nn.gelu(values, approximate=False), pre_act)
-    hidden_low = hidden.astype(low_type)
-    third_sum = second_norm + (product(hidden_low, wsecond) + proj_biases[6])
+
+    second_both = jnp.concatenate([second_low, swap(second_low, "core", 1)], 0)
+    feed_sum, hidden, gelu_back = 0.0, [], []
+    for part in range(reps):
+        active, back = jax.vjp(gelu, product(second_both, wfirst[part]) + bias_cut[part])
+        hidden.append(active.astype(low_type))
+        gelu_back.append(back)
+        feed_sum = feed_sum + product(hidden[part], wsecond[part])
+    feed_other = swap(feed_sum[tok:].astype(low_type), "core", 1).astype(jnp.float32)
+    third_sum = second_norm + (feed_sum[:tok] + feed_other + proj_biases[6])
     result, norm3_back = jax.vjp(norm_rows, third_sum, norm_gains[2], norm_shifts[2])
     output = result.astype(low_type)
 
     third_grad, gain_three, shift_three = norm3_back(out_grad.astype(jnp.float32))
     feed_grad = third_grad.astype(low_type)
-    grad_fc2 = reduce_weight(hidden_low, feed_grad)
     bias_fc2 = column_sums(feed_grad)
-    pre_grad = gelu_back(product_right(feed_grad, wsecond))[0].astype(low_type)
-    grad_fc1 = reduce_weight(second_low, pre_grad)
-    bias_fc1 = column_sums(pre_grad)
-    second_grad, gain_two, shift_two = norm2_back(third_grad + product_right(pre_grad, wfirst))
+    feed_both = jnp.concatenate([feed_grad, swap(feed_grad, "core", 1)], 0)
+    second_parts = [
+        product_left(hidden[part], feed_both).astype(low_type) for part in range(reps)
+    ]
+    feed_both, second_parts = stage((feed_both, second_parts))
+    second_terms = trade_over_rep(second_parts)
+    back_sum, first_parts, bias_parts = 0.0, [], []
+    for part in range(reps):
+        pre_grad = gelu_back[part](product_right(feed_both, wsecond[part]))[0].astype(low_type)
+        first_parts.append(product_left(second_both, pre_grad).astype(low_type))
+        bias_parts.append(column_sums(pre_grad))
+        back_sum = back_sum + product_right(pre_grad, wfirst[part])
+    back_other = swap(back_sum[tok:].astype(low_type), "core", 1).astype(jnp.float32)
+    second_grad, gain_two, shift_two = norm2_back(third_grad + (back_sum[:tok] + back_other))
+    second_grad, first_parts = stage((second_grad, first_parts))
+    first_terms = trade_over_rep(first_parts)
+
     cross_out_grad = second_grad.astype(low_type)
-    grad_cross_out = reduce_weight(cross_low, cross_out_grad)
+    part_cross_out = product_left(cross_low, cross_out_grad).astype(low_type)
     bias_cross_out = column_sums(cross_out_grad)
     cross_mixed_grad = product_right(cross_out_grad, full_cross_out).astype(low_type)
     cross_q_grad, pair_grad = cross_backward(
         cross_queries, pairs, cross_mixed_grad, cross_low, cross_total
     )
-    own_pair_grad = join_columns(
-        lax.psum_scatter(pair_grad, "shard", scatter_dimension=0, tiled=False)
-    )
-    grad_cross_q = reduce_weight(first_low, cross_q_grad)
+    cross_q_grad, second_terms = stage((cross_q_grad, second_terms))
+    second_sums = lax.psum_scatter(
+        sum_of(second_terms).astype(low_type), "line", scatter_dimension=0, tiled=True
+    )
+    own_pair_grad = lax.psum_scatter(pair_grad, SHARD, scatter_dimension=0, tiled=False)
+    part_cross_q = product_left(first_low, cross_q_grad).astype(low_type)
     bias_cross_q = column_sums(cross_q_grad)
-    bias_cross_v = in_columns(column_sums(own_pair_grad[:, width:]))
-    enc_grad = lax.psum_scatter(
-        product_right(own_pair_grad, head_ckv).astype(low_type),
-        "shard",
-        scatter_dimension=0,
-        tiled=True,
-    ).astype(jnp.float32)
     first_grad, gain_one, shift_one = norm1_back(
         second_grad + product_right(cross_q_grad, full_cross_q)
     )
     self_out_grad = first_grad.astype(low_type)
-    grad_self_out = reduce_weight(self_low, self_out_grad)
     bias_self_out = column_sums(self_out_grad)
     self_mixed_grad = product_right(self_out_grad, full_out).astype(low_type)
-    head_grad = exchange(split_columns(self_mixed_grad, group)).reshape(group * tok, width)
-    qkv_grad = self_backward(owners, qkv, key_t, head_grad, head_mixed, self_total, tok)
-    input_part = lax.psum_scatter(
-        product_right(qkv_grad, head_qkv).astype(low_type),
-        "shard",
-        scatter_dimension=0,
-        tiled=True,
-    )
+    head_grad = exchange(split_columns(self_mixed_grad, group))
+    part_self_out = product_left(self_low, self_out_grad).astype(low_type)
+
+    square = jnp.stack([part_self_out, part_cross_q, part_cross_out], 0)
+    square = square.reshape(3, line, 2, reps, weight_rows // reps, model)
+    other = swap(lax.dynamic_index_in_dim(square, 1 - core, 2, keepdims=False), "core", 1)
+    square = lax.dynamic_index_in_dim(square, core, 2, keepdims=False)
+    square = (square.astype(jnp.float32) + other.astype(jnp.float32)).astype(low_type)
+    square = rep_order([square[:, :, r] for r in range(reps)])
+    head_grad, square, first_terms, own_pair_grad = stage(
+        (head_grad, square, first_terms, own_pair_grad)
+    )
+    square_terms = trade_over_rep(square)
+    first_sums = lax.psum_scatter(
+        sum_of(first_terms).astype(low_type), "line", scatter_dimension=0, tiled=True
+    )
+    own_pair_grad = join_columns(own_pair_grad)
+    enc_grad = scatter_rows(product_right(own_pair_grad, head_ckv).astype(low_type))
+    head_grad = head_grad.reshape(group * tok, width)
+    qkv_grad, placed_grad = self_backward(
+        places, owners, qkv, head_grad, head_mixed, self_total, tok
+    )
+    qkv_grad, placed_grad, square_terms, first_sums, second_sums, enc_grad = stage(
+        (qkv_grad, placed_grad, square_terms, first_sums, second_sums, enc_grad)
+    )
+    input_part = scatter_rows(product_right(qkv_grad, head_qkv).astype(low_type))
     input_grad = first_grad + input_part.astype(jnp.float32)
+
+    bias_cross_v = in_columns(column_sums(own_pair_grad[:, width:]))
+
+    grad_fc2 = jnp.concatenate(rep_order(spread_over_rep(second_sums)), 0).astype(jnp.float32)
+    first_sums = first_sums.reshape(2, weight_rows, line * unit)
+    first_sums = jnp.stack(rep_order(spread_over_rep(first_sums)), 1)
+    first_own = lax.dynamic_index_in_dim(first_sums, core, 0, keepdims=False)
+    first_other = lax.dynamic_index_in_dim(first_sums, 1 - core, 0, keepdims=False)
+    first_other = swap(first_other, "core", 1)
+    grad_fc1 = jnp.where(
+        core == 0, jnp.stack([first_own, first_other], 0), jnp.stack([first_other, first_own], 0)
+    )
+    grad_fc1 = grad_fc1.reshape(2, reps, weight_rows, line, unit).transpose(2, 3, 0, 1, 4)
+    grad_fc1 = grad_fc1.reshape(weight_rows, feed).astype(jnp.float32)
+    bias_parts = jnp.stack([part.reshape(line, unit) for part in rep_order(bias_parts)], 1)
+    bias_fc1 = jnp.where(
+        jnp.arange(2)[None, :, None, None] == core, bias_parts[:, None], 0.0
+    ).reshape(feed)
+
+    square = sum_of(square_terms).astype(low_type)
+    square = scatter_over_line(square.transpose(1, 0, 2, 3))
+    square = jnp.stack(rep_order(spread_over_rep(square.astype(low_type))), 1)
+    grad_self_out, grad_cross_q, grad_cross_out = [
+        square[i].reshape(weight_rows, model).astype(jnp.float32) for i in range(3)
+    ]
+
     slice_grad = jnp.concatenate(
-        [product_left(all_inputs, qkv_grad), product_left(all_states, own_pair_grad)], 1
+        [product_left(all_inputs, placed_grad), product_left(all_states, own_pair_grad)], 1
     ).astype(low_type)
-    slice_grad = sum_over_rep(slice_grad).reshape(group, weight_rows, 5 * width)
-    slice_grad = exchange(slice_grad).astype(jnp.float32)
-    slice_grad = slice_grad.reshape(group, weight_rows, 5, width).transpose(1, 2, 0, 3)
+    slice_grad = slice_grad.reshape(group, reps, weight_rows // reps, 5 * width)
+    slice_grad = rep_order([slice_grad[:, r] for r in range(reps)])
+    slice_grad = exchange(sum_of(trade_over_rep(slice_grad)).astype(low_type))
+    slice_grad = jnp.stack(rep_order(spread_over_rep(slice_grad)), 0)
+    slice_grad = slice_grad.reshape(reps, group, weight_rows // reps, 5, width)
+    slice_grad = slice_grad.transpose(0, 2, 3, 1, 4).astype(jnp.float32)
     slice_grad = slice_grad.reshape(weight_rows, 5 * model)
     grad_self_qkv, grad_cross_kv = slice_grad[:, : 3 * model], slice_grad[:, 3 * model :]
+
     bias_self_q = in_columns(column_sums(qkv_grad[:, :width]))
     bias_self_v = in_columns(column_sums(qkv_grad[:, 2 * width :]))
-    everywhere = bits_of("rep") + bits_of("shard")
     small = jnp.concatenate(
         [
             jnp.stack(
@@ -537,11 +745,11 @@
         ],
         0,
     )
-    small = sum_over(small, everywhere)
+    small = sum_over(small, bits_of("core") + bits_of("rep") + bits_of("line"))
     return (
         output,
         input_grad,
-        enc_grad,
+        enc_grad.astype(jnp.float32),
         grad_self_qkv,
         grad_self_out,
         grad_cross_q,
@@ -557,10 +765,14 @@
 
 
 def solution(mesh):
-    rows, cut = P(("rep", "shard"), None), P("shard", None)
+    reps, group = mesh.devices.shape
+    split = jax.sharding.Mesh(
+        mesh.devices.reshape(reps, group // 2, 2), ("rep",) + SHARD
+    )
+    rows, cut = P(("rep",) + SHARD, None), P(SHARD, None)
     return jax.shard_map(
         local,
-        mesh=mesh,
+        mesh=split,
         in_specs=(rows,) * 3 + (P("rep", None),) + (cut,) * 7 + (P(),) * 4,
         out_specs=(rows,) * 3 + (cut,) * 7 + (P(),) * 4,
         check_vma=False,

time: 1000 us -> 756 us (0.76)
  waiting for transfers between devices: 558 us -> 257 us
  local copies, waits for them, and re-layouts: 50.2 us -> 76.8 us
  other arithmetic: 33.3 us -> 58 us
  starting transfers between devices: 46.3 us -> 63.2 us
  blocking collectives: 37.4 us -> 21.4 us
  Pallas kernels: 111 us -> 123 us
  matrix products: 140 us -> 130 us
    reduce_scatter x8 -> x5, waiting for transfers between devices: 216 us -> 7.19 us  [the longest x2 7.17 us: scatter_rows(): return lax.psum_scatter(values, SHARD, scatter_dimension=0, tiled=True)]
    all_gather x8 -> x4, waiting for transfers between devices: 202 us -> 26 us  [the longest x1 26 us: local(): lax.all_gather(jnp.concatenate([first_cut, square], 0), 'line', axis=0, t...]
    ppermute x29 -> x59, waiting for transfers between devices: 48.7 us -> 217 us  [the longest x53 162 us: swap(): return lax.ppermute(values, axis, [(i, i ^ offset) for i in range(size)])]
    all_to_all x3, waiting for transfers between devices: 86.2 us -> 6.16 us  [exchange(): lax.all_to_all(values, SHARD, split_axis=0, concat_axis=0, tiled=True)]
    ppermute x29 -> x59, starting transfers between devices: 31.4 us -> 49.4 us  [the longest x53 47 us: swap(): return lax.ppermute(values, axis, [(i, i ^ offset) for i in range(size)])]
    all_to_all x1, blocking collectives: 37.4 us -> 21.4 us  [exchange(): lax.all_to_all(values, SHARD, split_axis=0, concat_axis=0, tiled=True)]
    unnamed x91 -> x186, local copies, waits for them, and re-layouts: 19.4 us -> 32.1 us
    select_n x0 -> x11, other arithmetic: none -> 10.3 us  [the longest x1 5.76 us: local(): jnp.where(core == 0, jnp.stack([square, other], 1), jnp.stack([other, squ...]
  transfers between devices with their start and end apart: 48 -> 71, of which waited for: 26 -> 29; matrix products, arithmetic and copies ran while one was open for 17% -> 20% of each run, Pallas kernels for 10% -> 17%
where the time goes in v2:
time: 756 us; the launch traced here: 746 us
  waiting for transfers between devices  257 us (34%)
  matrix products  130 us (17%)
  Pallas kernels  123 us (16%)
  local copies, waits for them, and re-layouts  76.8 us (10%)
  starting transfers between devices  63.2 us (8%)
  other arithmetic  58 us (8%)
  blocking collectives  21.4 us (3%)
  between operations  16.1 us (2%)
    ppermute x53, waiting for transfers between devices, swap(): return lax.ppermute(values, axis, [(i, i ^ offset) for i in range(size)])  162 us
    dot_general x12, matrix products, product(): return jnp.dot(former, latter, preferred_element_type=jnp.float32)  60.1 us
    pallas_call x1, Pallas kernels, self_backward(): pl.pallas_call(functools.partial(self_backward_kernel, tok, width, group...  52.1 us
    ppermute x53, starting transfers between devices, swap(): return lax.ppermute(values, axis, [(i, i ^ offset) for i in range(size)])  47 us
    pallas_call x1, Pallas kernels, self_forward(): pl.pallas_call(functools.partial(self_forward_kernel, tok, width, group /...  46.4 us
    dot_general x13, matrix products, product_right(): lax.dot_general(former, latter, (((1,), (1,)), ((), ())), preferred_eleme...  35.4 us
    dot_general x13, matrix products, product_left(): lax.dot_general(former, latter, (((0,), (0,)), ((), ())), preferred_eleme...  34 us
    ppermute x3, waiting for transfers between devices, shift(): lax.ppermute(values, 'line', [(i, (i + 1) % line) for i in range(line)])  33 us
  transfers between devices with their start and end apart: 71, of which 29 were waited for; matrix products, arithmetic and copies ran while one was open for 20% of the time, Pallas kernels for 17%

profile of v2, /device:TPU:0, one launch (start us, length us, event | category | flops | bytes accessed | tf_op | source)
XLA Modules:
  0.0 745.5 jit_solution(3643919187126039377)
XLA Ops:
  12.7 21.4 %all_to_all.20 = bf16[8,32,640]{2,1,0:T(8,128)(2,1)S(1)} all-to-all(bf16[8,32,640]{2,1,0:T(8,128)(2,1)S(1)} %reshape.619), channel_id=1, replica_groups=mesh['rep'=4,'line'=4,'core'=2] {'line','core'}, dimensions={0} | all-to-all | bytes 655360 | tf_op jit(solution)/shard_map/all_to_all | solution.py:448
  34.0 26.0 %all-gather.6.cloned.1.call-done = bf16[1792,512]{1,0:T(8,128)(2,1)} async-done(((bf16[448,512]{1,0:T(8,128)(2,1)}), bf16[1792,512]{1,0:T(8,128)(2,1)}) %all-gather.6.cloned.1.call-update) | async-done | bytes 1835024 | tf_op jit(solution)/shard_map/all_gather | solution.py:534
  63.6 7.0 collective-permute-done.2
  70.7 7.8 %collective-permute-done.3 = bf16[8,32,640]{2,1,0:T(8,128)(2,1)S(1)} collective-permute-done((bf16[8,32,640]{2,1,0:T(8,128)(2,1)S(1)}, bf16[8,32,640]{2,1,0:T(8,128)(2,1)S(1)}, u32[]{:S(2)}, u32[]{:S(2)}) %collective-permute-start.3) | collective-permute-done | bytes 327712 | tf_op jit(solution)/shard_map/ppermute | solution.py:388
  78.4 8.5 %collective-permute-done.1.refs_2_ = bf16[512,1024]{1,0:T(8,128)(2,1)S(1)} collective-permute-done((bf16[512,1024]{1,0:T(8,128)(2,1)S(1)}, bf16[512,1024]{1,0:T(8,128)(2,1)S(1)}, u32[]{:S(2)}, u32[]{:S(2)}) %collective-permute-start.1) | collective-permute-done | bytes 1048608 | tf_op jit(solution)/shard_map/ppermute | solution.py:436
  94.7 15.1 %collective-permute-done.7 = bf16[4,192,512]{2,1,0:T(8,128)(2,1)} collective-permute-done((bf16[4,192,512]{2,1,0:T(8,128)(2,1)S(1)}, bf16[4,192,512]{2,1,0:T(8,128)(2,1)}, u32[]{:S(2)}, u32[]{:S(2)}) %collective-permute-start.7) | collective-permute-done | bytes 786464 | tf_op jit(solution)/shard_map/ppermute | solution.py:388
  109.8 17.7 %collective-permute-done.8 = bf16[4,192,512]{2,1,0:T(8,128)(2,1)} collective-permute-done((bf16[4,192,512]{2,1,0:T(8,128)(2,1)S(1)}, bf16[4,192,512]{2,1,0:T(8,128)(2,1)}, u32[]{:S(2)}, u32[]{:S(2)}) %collective-permute-start.8) | collective-permute-done | bytes 786464 | tf_op jit(solution)/shard_map/ppermute | solution.py:388
  134.9 24.4 %collective-permute-done.12.refs_6_ = bf16[512,1024]{1,0:T(8,128)(2,1)} collective-permute-done((bf16[512,1024]{1,0:T(8,128)(2,1)}, bf16[512,1024]{1,0:T(8,128)(2,1)}, u32[]{:S(2)}, u32[]{:S(2)}) %collective-permute-start.12) | collective-permute-done | bytes 1048608 | tf_op jit(solution)/shard_map/ppermute | solution.py:436
  172.9 46.4 %self_forward.1 = (bf16[4096,384]{1,0:T(8,128)(2,1)}, bf16[4096,128]{1,0:T(8,128)(2,1)S(1)}, f32[8,8,512]{2,1,0:T(8,128)S(1)}) custom-call(s32[8]{0:T(128)S(1)} %fusion.64.place, s32[8]{0:T(128)S(1)} %select_reduce_fusion.owner, bf16[512,1024]{1,0:T(8,128)(2,1)} %refs_0_, bf16[512,1024]{1,0:T(8,128)(2,1)} %collective-permute-done.5.refs_1_, ...), custom_call_target="tpu_custom_call" | custom-call | flops 9663676416 | bytes 13631488 | tf_op jit(solution)/shard_map/self_forward/pallas_call | solution.py:250
  224.9 5.8 maximum_select_fusion
  260.6 7.6 %collective-permute-done.18 = bf16[512,1024]{1,0:T(8,128)(2,1)S(1)} collective-permute-done((bf16[512,1024]{1,0:T(8,128)(2,1)S(1)}, bf16[512,1024]{1,0:T(8,128)(2,1)S(1)}, u32[]{:S(2)}, u32[]{:S(2)}) %collective-permute-start.18) | collective-permute-done | bytes 1048608 | tf_op jit(solution)/shard_map/ppermute | solution.py:388
  274.9 10.7 %multiply_convert_fusion.4.query = bf16[512,1024]{1,0:T(8,128)(2,1)S(1)} fusion(bf16[1024,1024]{1,0:T(8,128)(2,1)S(1)} %bitcast.368, f32[1024]{0:T(1024)S(1)} %bitcast.424, f32[512,1024]{1,0:T(8,128)S(1)} %get-tuple-element.364, f32[1024]{0:T(1024)S(1)} %bitcast.426, f32[1024]{0:T(1024)S(1)} %bitcast.414, f32[512]{0:T(512)S(1)} %fusion.60, ...), kind=kOutput, calls=%fused_computation.119 | convolution fusion | flops 1077936128 | bytes 5259264 | tf_op jit(solution)/shard_map/dot_general | solution.py:28
  285.6 10.9 %cross_forward.1 = (bf16[512,1024]{1,0:T(8,128)(2,1)S(1)}, f32[8,8,512]{2,1,0:T(8,128)S(1)}) custom-call(bf16[512,1024]{1,0:T(8,128)(2,1)S(1)} %multiply_convert_fusion.4.query, bf16[8,2,512,128]{3,2,1,0:T(8,128)(2,1)S(1)} %bitcast.350), custom_call_target="tpu_custom_call" | custom-call | flops 3221225472 | bytes 4194304 | tf_op jit(solution)/shard_map/cross_forward/pallas_call | solution.py:340
  302.9 9.3 %multiply_convert_fusion.1 = (bf16[1024,512]{1,0:T(8,128)(2,1)S(1)}, f32[1024,512]{1,0:T(8,128)}, f32[1024,512]{1,0:T(8,128)}) fusion(f32[512]{0:T(512)S(1)} %bitcast.437, bf16[1024,512]{1,0:T(8,128)(2,1)} %collective-permute-done.15, bf16[512,1024]{1,0:T(8,128)(2,1)S(1)} %collective-permute-done.21, bf16[512,1024]{1,0:T(8,128)(2,1)S(1)} %fusion.33), kind=kOutput, calls=%fused_computation.77 | convolution fusion | flops 1112539136 | bytes 8390656 | tf_op jit(solution)/shard_map/dot_general | solution.py:28
  314.7 9.0 %multiply_convert_fusion.3 = (bf16[1024,512]{1,0:T(8,128)(2,1)S(1)}, f32[1024,512]{1,0:T(8,128)}, f32[1024,512]{1,0:T(8,128)}) fusion(f32[512]{0:T(512)S(1)} %bitcast.435, bf16[1024,512]{1,0:T(8,128)(2,1)} %bitcast.20, bf16[512,1024]{1,0:T(8,128)(2,1)S(1)} %collective-permute-done.21, bf16[512,1024]{1,0:T(8,128)(2,1)S(1)} %fusion.33), kind=kOutput, calls=%fused_computation.103 | convolution fusion | flops 1112539136 | bytes 8390656 | tf_op jit(solution)/shard_map/dot_general | solution.py:28
  325.0 9.1 %multiply_convert_fusion.2 = (bf16[1024,512]{1,0:T(8,128)(2,1)S(1)}, f32[1024,512]{1,0:T(8,128)}, f32[1024,512]{1,0:T(8,128)}) fusion(f32[512]{0:T(512)S(1)} %bitcast.433, bf16[1024,512]{1,0:T(8,128)(2,1)} %collective-permute-done.14, bf16[512,1024]{1,0:T(8,128)(2,1)S(1)} %collective-permute-done.21, bf16[512,1024]{1,0:T(8,128)(2,1)S(1)} %fusion.33), kind=kOutput, calls=%fused_computation.90 | convolution fusion | flops 1112539136 | bytes 8390656 | tf_op jit(solution)/shard_map/dot_general | solution.py:28
  335.4 9.4 %multiply_convert_fusion = (bf16[1024,512]{1,0:T(8,128)(2,1)S(1)}, f32[1024,512]{1,0:T(8,128)}, f32[1024,512]{1,0:T(8,128)}) fusion(f32[512]{0:T(512)S(1)} %bitcast.431, bf16[1024,512]{1,0:T(8,128)(2,1)} %collective-permute-done.17, bf16[512,1024]{1,0:T(8,128)(2,1)S(1)} %collective-permute-done.21, bf16[512,1024]{1,0:T(8,128)(2,1)S(1)} %fusion.33), kind=kOutput, calls=%fused_computation.64 | convolution fusion | flops 1112539136 | bytes 8390656 | tf_op jit(solution)/shard_map/dot_general | solution.py:28
  405.7 13.9 %cross_backward.1 = (bf16[512,1024]{1,0:T(8,128)(2,1)S(1)}, bf16[8,2,512,128]{3,2,1,0:T(8,128)(2,1)}) custom-call(bf16[512,1024]{1,0:T(8,128)(2,1)S(1)} %multiply_convert_fusion.4.query, bf16[8,2,512,128]{3,2,1,0:T(8,128)(2,1)S(1)} %bitcast.351, bf16[512,1024]{1,0:T(8,128)(2,1)S(1)} %convolution_convert_fusion.6.mixed_grad, ...), custom_call_target="tpu_custom_call" | custom-call | flops 8053063680 | bytes 8388608 | tf_op jit(solution)/shard_map/cross_backward/pallas_call | solution.py:366
  419.6 17.7 %collective-permute-done.26 = bf16[512,1024]{1,0:T(8,128)(2,1)S(1)} collective-permute-done((bf16[512,1024]{1,0:T(8,128)(2,1)}, bf16[512,1024]{1,0:T(8,128)(2,1)S(1)}, u32[]{:S(2)}, u32[]{:S(2)}) %collective-permute-start.26) | collective-permute-done | bytes 1048608 | tf_op jit(solution)/shard_map/ppermute | solution.py:388
  455.9 4.6 all-to-all-start.2
  475.5 15.6 %collective-permute-done.29 = bf16[1024,512]{1,0:T(8,128)(2,1)S(1)} collective-permute-done((bf16[1024,512]{1,0:T(8,128)(2,1)}, bf16[1024,512]{1,0:T(8,128)(2,1)S(1)}, u32[]{:S(2)}, u32[]{:S(2)}) %collective-permute-start.29) | collective-permute-done | bytes 1048608 | tf_op jit(solution)/shard_map/ppermute | solution.py:388
  491.1 22.3 %collective-permute-done.30 = bf16[1024,512]{1,0:T(8,128)(2,1)S(1)} collective-permute-done((bf16[1024,512]{1,0:T(8,128)(2,1)}, bf16[1024,512]{1,0:T(8,128)(2,1)S(1)}, u32[]{:S(2)}, u32[]{:S(2)}) %collective-permute-start.30) | collective-permute-done | bytes 1048608 | tf_op jit(solution)/shard_map/ppermute | solution.py:388
  523.6 52.1 %self_backward.1 = (bf16[4096,384]{1,0:T(8,128)(2,1)}, bf16[4096,384]{1,0:T(8,128)(2,1)}) custom-call(s32[8]{0:T(128)S(1)} %copy-done.8, s32[8]{0:T(128)S(1)} %copy-done.6, bf16[4096,384]{1,0:T(8,128)(2,1)} %get-tuple-element.177.qkv, bf16[4096,128]{1,0:T(8,128)(2,1)S(1)} %bitcast.349, bf16[4096,128]{1,0:T(8,128)(2,1)} %copy-done.2, ...), custom_call_target="tpu_custom_call" | custom-call | flops 24159191040 | bytes 10485760 | tf_op jit(solution)/shard_map/self_backward/pallas_call | solution.py:282
  575.7 7.2 reduce-scatter.12.cloned.1.call-done
  582.8 8.8 %convolution_convert_fusion = bf16[4096,1024]{1,0:T(8,128)(2,1)} fusion(bf16[4096,384]{1,0:T(8,128)(2,1)} %get-tuple-element.200, bf16[1024,384]{1,0:T(8,128)(2,1)S(1)} %copy-done.4), kind=kOutput, calls=%fused_computation | convolution fusion | flops 3225419776 | bytes 12320768 | tf_op jit(solution)/shard_map/dot_general | solution.py:38
  603.5 8.8 %convolution_convert_fusion.15 = bf16[1024,384]{1,0:T(8,128)(2,1)S(1)} fusion(bf16[4096,1024]{1,0:T(8,128)(2,1)} %constant_dynamic-update-slice_fusion, bf16[4096,384]{1,0:T(8,128)(2,1)} %get-tuple-element.203), kind=kOutput, calls=%fused_computation.155 | convolution fusion | flops 3221618688 | bytes 12320768 | tf_op jit(solution)/shard_map/dot_general | solution.py:32
  620.5 22.2 %collective-permute-done.42 = bf16[3,32,1024]{2,1,0:T(8,128)(2,1)S(1)} collective-permute-done((bf16[3,32,1024]{2,1,0:T(8,128)(2,1)S(1)}, bf16[3,32,1024]{2,1,0:T(8,128)(2,1)S(1)}, u32[]{:S(2)}, u32[]{:S(2)}) %collective-permute-start.42) | collective-permute-done | bytes 196640 | tf_op jit(solution)/shard_map/ppermute | solution.py:426
  644.9 7.5 collective-permute-done.56
  670.1 5.2 collective-permute-done.57
  677.4 4.9 collective-permute-done.35
  696.4 6.2 all-to-all-done.3
  710.3 8.8 %collective-permute-done.39 = bf16[8,32,640]{2,1,0:T(8,128)(2,1)S(1)} collective-permute-done((bf16[8,32,640]{2,1,0:T(8,128)(2,1)S(1)}, bf16[8,32,640]{2,1,0:T(8,128)(2,1)S(1)}, u32[]{:S(2)}, u32[]{:S(2)}) %collective-permute-start.39) | collective-permute-done | bytes 327712 | tf_op jit(solution)/shard_map/ppermute | solution.py:388
  (487 shorter events, 277.5 us)
Async XLA Ops:
  7.2 52.8 %all-gather.6.cloned.1.call-start = ((), (), s32[]{:S(2)}) async-start(), calls=%async_computation.9 | async-start | bytes 2293760 | tf_op jit(solution)/shard_map/all_gather | solution.py:534
  11.7 115.8 %all-gather.8.cloned.1.call-start = ((), (), s32[]{:S(2)}) async-start(), calls=%async_computation.10 | async-start | bytes 1179648 | tf_op jit(solution)/shard_map/all_gather | solution.py:440
  87.9 131.4 %all-gather.10.cloned.1.call-start = ((), (), s32[]{:S(2)}) async-start(), calls=%async_computation.11 | async-start | bytes 1310720 | tf_op jit(solution)/shard_map/all_gather | solution.py:571
  88.0 39.5 %collective-permute-start.6 = (bf16[512,1024]{1,0:T(8,128)(2,1)}, bf16[512,1024]{1,0:T(8,128)(2,1)}, u32[]{:S(2)}, u32[]{:S(2)}) collective-permute-start(bf16[512,1024]{1,0:T(8,128)(2,1)} %copy-done.38), channel_id=1, source_target_pairs={{0,2},{2,4},{4,6},{6,0},{1,3},{3,5},{5,7},{7,1},{8,10},{10,12},{12... | collective-permute-start | bytes 3145736 | tf_op jit(solution)/shard_map/ppermute | solution.py:436
  88.1 39.5 %collective-permute-start.10 = (bf16[512,1024]{1,0:T(8,128)(2,1)}, bf16[512,1024]{1,0:T(8,128)(2,1)}, u32[]{:S(2)}, u32[]{:S(2)}) collective-permute-start(bf16[512,1024]{1,0:T(8,128)(2,1)} %copy-done.38), channel_id=1, source_target_pairs={{0,1},{1,0},{2,3},{3,2},{4,5},{5,4},{6,7},{7,6},{8,9},{9,8},{10,11... | collective-permute-start | bytes 3145736 | tf_op jit(solution)/shard_map/ppermute | solution.py:388
  90.9 36.6 %collective-permute-start.8 = (bf16[4,192,512]{2,1,0:T(8,128)(2,1)S(1)}, bf16[4,192,512]{2,1,0:T(8,128)(2,1)}, u32[]{:S(2)}, u32[]{:S(2)}) collective-permute-start(bf16[4,192,512]{2,1,0:T(8,128)(2,1)S(1)} %slice.146), channel_id=1, source_target_pairs={{0,16},{8,24},{16,0},{24,8},{1,17},{9,25},{17,1},{25,9},{2,18},{10... | collective-permute-start | bytes 2359304 | tf_op jit(solution)/shard_map/ppermute | solution.py:388
  92.4 35.1 %collective-permute-start.9 = (bf16[4,192,512]{2,1,0:T(8,128)(2,1)S(1)}, bf16[4,192,512]{2,1,0:T(8,128)(2,1)}, u32[]{:S(2)}, u32[]{:S(2)}) collective-permute-start(bf16[4,192,512]{2,1,0:T(8,128)(2,1)S(1)} %slice.146), channel_id=1, source_target_pairs={{0,24},{8,16},{16,8},{24,0},{1,25},{9,17},{17,9},{25,1},{2,26},{10... | collective-permute-start | bytes 2359304 | tf_op jit(solution)/shard_map/ppermute | solution.py:388
  131.4 31.3 %collective-permute-start.16 = (bf16[4,4,192,512]{3,2,0,1:T(8,128)(2,1)}, bf16[4,4,192,512]{3,2,0,1:T(8,128)(2,1)}, u32[]{:S(2)}, u32[]{:S(2)}) collective-permute-start(bf16[4,4,192,512]{3,2,0,1:T(8,128)(2,1)} %pad_maximum_fusion.1), channel_id=1, source_target_pairs={{0,1},{1,0},{2,3},{3,2},{4,5},{5,4},{6,7},{7,6},{8,9},{9,8},{10,11... | collective-permute-start | bytes 9437192 | tf_op jit(solution)/shard_map/ppermute | solution.py:388
  132.8 29.9 %collective-permute-start.14 = (bf16[1024,512]{1,0:T(8,128)(2,1)}, bf16[1024,512]{1,0:T(8,128)(2,1)}, u32[]{:S(2)}, u32[]{:S(2)}) collective-permute-start(bf16[1024,512]{1,0:T(8,128)(2,1)} %bitcast.20), channel_id=1, source_target_pairs={{0,8},{8,0},{16,24},{24,16},{1,9},{9,1},{17,25},{25,17},{2,10},{10... | collective-permute-start | bytes 3145736 | tf_op jit(solution)/shard_map/ppermute | solution.py:388
  134.0 28.7 %collective-permute-start.15 = (bf16[1024,512]{1,0:T(8,128)(2,1)}, bf16[1024,512]{1,0:T(8,128)(2,1)}, u32[]{:S(2)}, u32[]{:S(2)}) collective-permute-start(bf16[1024,512]{1,0:T(8,128)(2,1)} %bitcast.20), channel_id=1, source_target_pairs={{0,16},{8,24},{16,0},{24,8},{1,17},{9,25},{17,1},{25,9},{2,18},{10... | collective-permute-start | bytes 3145736 | tf_op jit(solution)/shard_map/ppermute | solution.py:388
  162.7 106.8 %all-gather.12.cloned.1.call-start = ((), (), s32[]{:S(2)}) async-start(), calls=%async_computation.17 | async-start | bytes 2359296 | tf_op jit(solution)/shard_map/all_gather | solution.py:587
  163.5 55.8 %collective-permute-start.17 = (bf16[1024,512]{1,0:T(8,128)(2,1)}, bf16[1024,512]{1,0:T(8,128)(2,1)}, u32[]{:S(2)}, u32[]{:S(2)}) collective-permute-start(bf16[1024,512]{1,0:T(8,128)(2,1)} %bitcast.20), channel_id=1, source_target_pairs={{0,24},{8,16},{16,8},{24,0},{1,25},{9,17},{17,9},{25,1},{2,26},{10... | collective-permute-start | bytes 3145736 | tf_op jit(solution)/shard_map/ppermute | solution.py:388
  220.6 48.8 %all-to-all-start.1 = ((bf16[8,512,128]{1,2,0:T(8,128)(2,1)}), bf16[8,512,128]{1,2,0:T(8,128)(2,1)}, u32[]{:S(2)}, u32[]{:S(2)}) async-start(bf16[8,512,128]{1,2,0:T(8,128)(2,1)} %copy.201), calls=%async_computation.1 | async-start | bytes 2097152 | tf_op jit(solution)/shard_map/all_to_all | solution.py:448
  224.9 289.5 %reduce-scatter.6.cloned.1.call-start = ((), (), s32[]{:S(2)}) async-start(), calls=%async_computation.12 | async-start | bytes 2359296 | tf_op jit(solution)/shard_map/reduce_scatter | solution.py:648
  388.0 31.6 %collective-permute-start.25 = (bf16[512,1024]{1,0:T(8,128)(2,1)}, bf16[512,1024]{1,0:T(8,128)(2,1)S(1)}, u32[]{:S(2)}, u32[]{:S(2)}) collective-permute-start(bf16[512,1024]{1,0:T(8,128)(2,1)} %convolution_convert_fusion.13), channel_id=1, source_target_pairs={{0,8},{8,0},{16,24},{24,16},{1,9},{9,1},{17,25},{25,17},{2,10},{10... | collective-permute-start | bytes 3145736 | tf_op jit(solution)/shard_map/ppermute | solution.py:388
  389.5 47.8 %collective-permute-start.26 = (bf16[512,1024]{1,0:T(8,128)(2,1)}, bf16[512,1024]{1,0:T(8,128)(2,1)S(1)}, u32[]{:S(2)}, u32[]{:S(2)}) collective-permute-start(bf16[512,1024]{1,0:T(8,128)(2,1)} %convolution_convert_fusion.12), channel_id=1, source_target_pairs={{0,16},{8,24},{16,0},{24,8},{1,17},{9,25},{17,1},{25,9},{2,18},{10... | collective-permute-start | bytes 3145736 | tf_op jit(solution)/shard_map/ppermute | solution.py:388
  390.1 47.3 %collective-permute-start.27 = (bf16[512,1024]{1,0:T(8,128)(2,1)}, bf16[512,1024]{1,0:T(8,128)(2,1)S(1)}, u32[]{:S(2)}, u32[]{:S(2)}) collective-permute-start(bf16[512,1024]{1,0:T(8,128)(2,1)} %convolution_convert_fusion.11), channel_id=1, source_target_pairs={{0,24},{8,16},{16,8},{24,0},{1,25},{9,17},{17,9},{25,1},{2,26},{10... | collective-permute-start | bytes 3145736 | tf_op jit(solution)/shard_map/ppermute | solution.py:388
  455.9 58.5 %all-to-all-start.2 = ((bf16[8,512,128]{2,1,0:T(8,128)(2,1)}), bf16[8,512,128]{2,1,0:T(8,128)(2,1)S(1)}, u32[]{:S(2)}, u32[]{:S(2)}) async-start(bf16[8,512,128]{2,1,0:T(8,128)(2,1)} %bitcast.363), calls=%async_computation.2 | async-start | bytes 2097152 | tf_op jit(solution)/shard_map/all_to_all | solution.py:448
  460.5 115.1 %reduce-scatter.10.cloned.1.call-start = ((), (), s32[]{:S(2)}) async-start(), calls=%async_computation.14 | async-start | bytes 1310720 | tf_op jit(solution)/shard_map/reduce_scatter | solution.py:645
  464.6 111.0 %reduce-scatter.8.cloned.1.call-start = ((), (), s32[]{:S(2)}) async-start(), calls=%async_computation.13 | async-start | bytes 1310720 | tf_op jit(solution)/shard_map/reduce_scatter | solution.py:670
  465.5 47.9 %collective-permute-start.30 = (bf16[1024,512]{1,0:T(8,128)(2,1)}, bf16[1024,512]{1,0:T(8,128)(2,1)S(1)}, u32[]{:S(2)}, u32[]{:S(2)}) collective-permute-start(bf16[1024,512]{1,0:T(8,128)(2,1)} %convolution_convert_fusion.8), channel_id=1, source_target_pairs={{0,16},{8,24},{16,0},{24,8},{1,17},{9,25},{17,1},{25,9},{2,18},{10... | collective-permute-start | bytes 3145736 | tf_op jit(solution)/shard_map/ppermute | solution.py:388
  466.6 47.7 %collective-permute-start.31 = (bf16[1024,512]{1,0:T(8,128)(2,1)}, bf16[1024,512]{1,0:T(8,128)(2,1)}, u32[]{:S(2)}, u32[]{:S(2)}) collective-permute-start(bf16[1024,512]{1,0:T(8,128)(2,1)} %convolution_convert_fusion.7), channel_id=1, source_target_pairs={{0,24},{8,16},{16,8},{24,0},{1,25},{9,17},{17,9},{25,1},{2,26},{10... | collective-permute-start | bytes 3145736 | tf_op jit(solution)/shard_map/ppermute | solution.py:388
  518.2 64.6 %reduce-scatter.12.cloned.1.call-start = ((), (), s32[]{:S(2)}) async-start(), calls=%async_computation.15 | async-start | bytes 1179648 | tf_op jit(solution)/shard_map/reduce_scatter | solution.py:444
  518.3 57.3 %collective-permute-start.32 = (bf16[3,4,32,1024]{3,2,1,0:T(8,128)(2,1)}, bf16[3,4,32,1024]{3,2,1,0:T(8,128)(2,1)}, u32[]{:S(2)}, u32[]{:S(2)}) collective-permute-start(bf16[3,4,32,1024]{3,2,1,0:T(8,128)(2,1)} %get-tuple-element.188), channel_id=1, source_target_pairs={{0,8},{8,0},{16,24},{24,16},{1,9},{9,1},{17,25},{25,17},{2,10},{10... | collective-permute-start | bytes 2359304 | tf_op jit(solution)/shard_map/ppermute | solution.py:388
  519.8 55.8 %collective-permute-start.33 = (bf16[3,4,32,1024]{3,2,1,0:T(8,128)(2,1)}, bf16[3,4,32,1024]{3,2,1,0:T(8,128)(2,1)}, u32[]{:S(2)}, u32[]{:S(2)}) collective-permute-start(bf16[3,4,32,1024]{3,2,1,0:T(8,128)(2,1)} %get-tuple-element.189), channel_id=1, source_target_pairs={{0,16},{8,24},{16,0},{24,8},{1,17},{9,25},{17,1},{25,9},{2,18},{10... | collective-permute-start | bytes 2359304 | tf_op jit(solution)/shard_map/ppermute | solution.py:388
  520.3 55.3 %collective-permute-start.34 = (bf16[3,4,32,1024]{3,2,1,0:T(8,128)(2,1)}, bf16[3,4,32,1024]{3,2,1,0:T(8,128)(2,1)}, u32[]{:S(2)}, u32[]{:S(2)}) collective-permute-start(bf16[3,4,32,1024]{3,2,1,0:T(8,128)(2,1)} %fusion.36), channel_id=1, source_target_pairs={{0,24},{8,16},{16,8},{24,0},{1,25},{9,17},{17,9},{25,1},{2,26},{10... | collective-permute-start | bytes 2359304 | tf_op jit(solution)/shard_map/ppermute | solution.py:388
  523.5 212.2 %reduce-scatter.14.cloned.1.call-start = ((), (), s32[]{:S(2)}) async-start(), calls=%async_computation.16 | async-start | bytes 9437184 | tf_op jit(solution)/shard_map/reduce_scatter | solution.py:444
  596.4 58.2 %collective-permute-start.48 = (bf16[2,128,512]{1,2,0:T(8,128)(2,1)S(1)}, bf16[2,128,512]{1,2,0:T(8,128)(2,1)S(1)}, u32[]{:S(2)}, u32[]{:S(2)}) collective-permute-start(bf16[2,128,512]{1,2,0:T(8,128)(2,1)S(1)} %copy.229), channel_id=1, source_target_pairs={{0,16},{8,24},{16,0},{24,8},{1,17},{9,25},{17,1},{25,9},{2,18},{10... | collective-permute-start | bytes 786440 | tf_op jit(solution)/shard_map/ppermute | solution.py:388
  598.0 57.4 %collective-permute-start.49 = (bf16[2,128,512]{1,2,0:T(8,128)(2,1)S(1)}, bf16[2,128,512]{1,2,0:T(8,128)(2,1)S(1)}, u32[]{:S(2)}, u32[]{:S(2)}) collective-permute-start(bf16[2,128,512]{1,2,0:T(8,128)(2,1)S(1)} %copy.229), channel_id=1, source_target_pairs={{0,24},{8,16},{16,8},{24,0},{1,25},{9,17},{17,9},{25,1},{2,26},{10... | collective-permute-start | bytes 786440 | tf_op jit(solution)/shard_map/ppermute | solution.py:388
  599.7 57.4 %collective-permute-start.47 = (bf16[2,128,512]{1,2,0:T(8,128)(2,1)S(1)}, bf16[2,128,512]{1,2,0:T(8,128)(2,1)S(1)}, u32[]{:S(2)}, u32[]{:S(2)}) collective-permute-start(bf16[2,128,512]{1,2,0:T(8,128)(2,1)S(1)} %copy.229), channel_id=1, source_target_pairs={{0,8},{8,0},{16,24},{24,16},{1,9},{9,1},{17,25},{25,17},{2,10},{10... | collective-permute-start | bytes 786440 | tf_op jit(solution)/shard_map/ppermute | solution.py:388
  662.5 30.9 %collective-permute-start.45 = (bf16[3,32,1024]{2,1,0:T(8,128)(2,1)S(1)}, bf16[3,32,1024]{2,1,0:T(8,128)(2,1)}, u32[]{:S(2)}, u32[]{:S(2)}) collective-permute-start(bf16[3,32,1024]{2,1,0:T(8,128)(2,1)S(1)} %fusion.48), channel_id=1, source_target_pairs={{0,16},{8,24},{16,0},{24,8},{1,17},{9,25},{17,1},{25,9},{2,18},{10... | collective-permute-start | bytes 589832 | tf_op jit(solution)/shard_map/ppermute | solution.py:388
  677.4 29.5 %collective-permute-start.50 = (bf16[4,128,512]{1,2,0:T(8,128)(2,1)S(1)}, bf16[4,128,512]{1,2,0:T(8,128)(2,1)}, u32[]{:S(2)}, u32[]{:S(2)}) collective-permute-start(bf16[4,128,512]{1,2,0:T(8,128)(2,1)S(1)} %get-tuple-element.323), channel_id=1, source_target_pairs={{0,1},{1,0},{2,3},{3,2},{4,5},{5,4},{6,7},{7,6},{8,9},{9,8},{10,11... | collective-permute-start | bytes 1572872 | tf_op jit(solution)/shard_map/ppermute | solution.py:388
  (124 other events, 1978.3 us)
Sparse Core Ops, SparseCore 0:
  11.8 48.1 all-gather.5
  88.1 28.6 all-gather.7
  162.8 26.5 all-gather.9
  191.5 28.5 all-gather.11
  441.3 41.4 reduce-scatter.5
  484.9 35.3 reduce-scatter.9
  523.2 25.7 reduce-scatter.7
  551.9 30.8 reduce-scatter.11
  591.8 106.9 reduce-scatter.13

commit v3 on v2

v3 whole, which is shorter than its diff:
```python
import functools

import jax
import jax.numpy as jnp
from jax import lax
from jax.experimental import pallas as pl
from jax.experimental.pallas import tpu as pltpu
from jax.sharding import PartitionSpec as P

HEADS = 16
HEAD_DIM = 64
LANES = 128

masked_score = -1000000000.0
norm_epsilon = 1e-05
low_type = jnp.bfloat16
SHARD = ("line", "core")


def norm_rows(values, gain_row, shift_row):
    row_mean = jnp.mean(values, -1, keepdims=True)
    centered = values - row_mean
    variance = jnp.mean(centered * centered, -1, keepdims=True)
    return centered * lax.rsqrt(variance + norm_epsilon) * gain_row + shift_row


def product(former, latter):
    return jnp.dot(former, latter, preferred_element_type=jnp.float32)


def product_left(former, latter):
    return lax.dot_general(
        former, latter, (((0,), (0,)), ((), ())), preferred_element_type=jnp.float32
    )


def product_right(former, latter):
    return lax.dot_general(
        former, latter, (((1,), (1,)), ((), ())), preferred_element_type=jnp.float32
    )


def column_sums(values):
    return jnp.sum(values.astype(jnp.float32), 0)


def head_columns(index):
    return slice(index * HEAD_DIM, (index + 1) * HEAD_DIM)


def causal_rows(keys, queries):
    key_index = lax.broadcasted_iota(jnp.int32, (keys, queries), 0)
    query_index = lax.broadcasted_iota(jnp.int32, (keys, queries), 1)
    return key_index <= query_index


def of_head(values, head):
    if values.shape[1] == HEAD_DIM:
        return values
    column = lax.broadcasted_iota(jnp.int32, values.shape, 1)
    inside = (column >= head * HEAD_DIM) & (column < (head + 1) * HEAD_DIM)
    return jnp.where(inside, values, jnp.zeros_like(values))


def turn_head(source, start, width, head, out, tok):
    for row in range(0, source.shape[0], tok):
        block = jnp.transpose(source[row : row + tok, start : start + width])
        out[:, row : row + tok] = block[head_columns(head)]


def over_keys(slot, half, tok, step, first, keep):
    @pl.when(slot < half)
    def _():
        keep(
            lax.fori_loop(0, slot, lambda j, c: step(pl.multiple_of(j * tok, tok), tok, c), first)
        )

    @pl.when(slot >= half)
    def _():
        keep(step(0, half * tok, first))


def self_forward_kernel(tok, width, half, head, count, owner, slot_of, *refs):
    if count:
        blocks, (weight, bias, scale, qkv, mixed, total, value_t) = refs[:count], refs[count:]
    else:
        qkv, mixed, total, value_t = refs
    slot = pl.program_id(0)

    @pl.when(slot == 0)
    def _():
        if count:
            for index, block in enumerate(blocks):
                rows = (product(block[...], weight[...]) + bias[...]) * scale[...]
                start = pl.multiple_of(slot_of[index] * tok, tok)
                qkv[pl.ds(start, tok), :] = rows.astype(low_type)
        turn_head(qkv, 2 * width, width, head, value_t, tok)

    base = pl.multiple_of(slot * tok, tok)
    query_t = jnp.transpose(of_head(qkv[pl.ds(base, tok), :width], head))

    def step(start, seen, carry, causal=False):
        top, weight, mix = carry
        keys = qkv[pl.ds(start, seen), width : 2 * width]
        scores = product(keys, query_t)
        if causal:
            scores = jnp.where(causal_rows(seen, tok), scores, masked_score)
        new_top = jnp.maximum(top, jnp.max(scores, 0, keepdims=True))
        scale = jnp.exp(top - new_top)
        power = jnp.exp(scores - new_top)
        weight = weight * scale + jnp.sum(power, 0, keepdims=True)
        mix = mix * scale + product(value_t[:, pl.ds(start, seen)], power.astype(low_type))
        return (new_top, weight, mix)

    first = (
        jnp.full((1, tok), -1e30, jnp.float32),
        jnp.zeros((1, tok), jnp.float32),
        jnp.zeros((HEAD_DIM, tok), jnp.float32),
    )

    def keep(carry):
        top, weight, mix = step(base, tok, carry, True)
        mixed[...] = (mix / weight).astype(low_type)
        total[...] = top + jnp.log(weight)

    over_keys(slot, half, tok, step, first, keep)


def self_backward_kernel(tok, width, half, head, scale, count, owner, place, *refs):
    blocks, refs = refs[:count], refs[count:]
    qkv, mixed_grad, mixed, total, out, slice_grad = refs[:6]
    key_t, key_sum, value_sum, rows, slice_sum, arrived = refs[6:]
    slot = pl.program_id(0)
    copies = [
        pltpu.make_async_copy(block, rows.at[i], arrived.at[i]) for i, block in enumerate(blocks)
    ]

    @pl.when(slot == 0)
    def _():
        for copy in copies:
            copy.start()
        turn_head(qkv, width, width, head, key_t, tok)
        key_sum[...] = jnp.zeros_like(key_sum)
        value_sum[...] = jnp.zeros_like(value_sum)

    base = pl.multiple_of(slot * tok, tok)
    query = of_head(qkv[pl.ds(base, tok), :width], head)
    query_t = jnp.transpose(query)
    narrow = mixed_grad[...]
    delta = jnp.sum(narrow.astype(jnp.float32) * mixed[...].astype(jnp.float32), 0, keepdims=True)
    empty = jnp.zeros_like(narrow)
    heads = width // HEAD_DIM
    grad_t = jnp.concatenate([narrow if h == head else empty for h in range(heads)], 0)
    grad = jnp.transpose(grad_t)

    def step(start, seen, carry, causal=False):
        keys = qkv[pl.ds(start, seen), width : 2 * width]
        values = qkv[pl.ds(start, seen), 2 * width :]
        power = jnp.exp(product(keys, query_t) - total[...])
        if causal:
            power = jnp.where(causal_rows(seen, tok), power, 0.0)
        slope = product(values, grad_t)
        score_grad = (power * (slope - delta)).astype(low_type)
        value_sum[pl.ds(start, seen), :] += product(power.astype(low_type), grad)
        key_sum[pl.ds(start, seen), :] += product(score_grad, query)
        return carry + product(key_t[:, pl.ds(start, seen)], score_grad)

    def keep(carry):
        query_grad = step(base, tok, carry, True).astype(low_type) * scale
        out[pl.ds(owner[slot], 1), :HEAD_DIM, :] = query_grad[None]

    over_keys(slot, half, tok, step, jnp.zeros((HEAD_DIM, tok), jnp.float32), keep)

    @pl.when(slot == pl.num_programs(0) - 1)
    def _():
        for copy in copies:
            copy.wait()
        slice_sum[...] = jnp.zeros_like(slice_sum)
        model = rows.shape[2]
        ones = jnp.ones((tok, LANES), low_type)

        def finish(p, carry):
            source = pl.ds(pl.multiple_of(p * tok, tok), tok)
            key_grad = jnp.transpose(key_sum[source, :])[head_columns(head)]
            value_grad = jnp.transpose(value_sum[source, :])[head_columns(head)]
            target = pl.ds(owner[p], 1)
            out[target, HEAD_DIM : 2 * HEAD_DIM, :] = key_grad.astype(low_type)[None]
            out[target, 2 * HEAD_DIM :, :] = value_grad.astype(low_type)[None]
            columns = out[target][0]
            slice_sum[:, :model] += product(columns, rows[pl.ds(place[p], 1)][0])
            slice_sum[:, model:] += product(columns, ones)
            return carry

        lax.fori_loop(0, pl.num_programs(0), finish, 0)
        slice_grad[...] = slice_sum[...]


def cross_forward_kernel(width, query, pair, mixed, total):
    keys, values = pair[0], jnp.transpose(pair[1])
    mixes = []
    for head in range(width // HEAD_DIM):
        cols = head_columns(head)
        scores = product_right(keys[:, cols], query[:, cols])
        top = jnp.max(scores, 0, keepdims=True)
        power = jnp.exp(scores - top)
        weight = jnp.sum(power, 0, keepdims=True)
        mixes.append(product(values[cols], power.astype(low_type)) / weight)
        total[head : head + 1, :] = top + jnp.log(weight)
    mixed[...] = jnp.transpose(jnp.concatenate(mixes, 0)).astype(low_type)


def cross_backward_kernel(width, scale, query, pair, mixed_grad, mixed, total, out, pair_grad):
    heads = width // HEAD_DIM
    keys, values = pair[0], pair[1]
    keys_t = jnp.transpose(keys)
    grad = mixed_grad[...]
    both = jnp.transpose(grad.astype(jnp.float32) * mixed[...].astype(jnp.float32))
    query_parts, key_parts, value_parts = [], [], []
    for head in range(heads):
        cols = head_columns(head)
        scores = product_right(keys[:, cols], query[:, cols])
        power = jnp.exp(scores - total[head : head + 1, :])
        slope = product_right(values[:, cols], grad[:, cols])
        delta = jnp.sum(both[cols], 0, keepdims=True)
        score_grad = (power * (slope - delta)).astype(low_type)
        value_parts.append(product(power.astype(low_type), grad[:, cols]))
        key_parts.append(product(score_grad, query[:, cols]))
        query_parts.append(product(keys_t[cols], score_grad))
    query_grad = jnp.transpose(jnp.concatenate(query_parts, 0)).astype(low_type)
    out[...] = query_grad * scale
    pair_grad[0] = jnp.concatenate(key_parts, 1).astype(low_type)
    pair_grad[1] = jnp.concatenate(value_parts, 1).astype(low_type)


declared = pl.CostEstimate(flops=2**20, transcendentals=0, bytes_accessed=2**16)


def kernel_options(megabytes):
    return pltpu.CompilerParams(
        dimension_semantics=("arbitrary",), vmem_limit_bytes=megabytes * 2**20
    )


def whole_block(shape):
    return pl.BlockSpec(shape, lambda *_: (0,) * len(shape), pipeline_mode=pl.Buffered(1))


def self_forward(head, owner, slot_of, tok, qkv, blocks=(), weight=None, bias=None, scale=None):
    make = qkv is None
    group = owner.shape[0]
    rows = group * tok
    width = (weight if make else qkv).shape[1] // 3
    inputs = (*blocks, weight, bias[None], scale[None]) if make else (qkv,)
    out_shape = [
        jax.ShapeDtypeStruct((group, HEAD_DIM, tok), low_type),
        jax.ShapeDtypeStruct((group, 1, tok), jnp.float32),
    ]
    out_specs = [
        pl.BlockSpec((None, HEAD_DIM, tok), lambda p, owner, _: (owner[p], 0, 0)),
        pl.BlockSpec((None, 1, tok), lambda p, *_: (p, 0, 0)),
    ]
    if make:
        out_shape = [jax.ShapeDtypeStruct((rows, 3 * width), low_type)] + out_shape
        out_specs = [pl.BlockSpec((rows, 3 * width), lambda *_: (0, 0))] + out_specs
    made = pl.pallas_call(
        functools.partial(
            self_forward_kernel, tok, width, group // 2, head, len(blocks)
        ),
        out_shape=out_shape,
        grid_spec=pltpu.PrefetchScalarGridSpec(
            num_scalar_prefetch=2,
            grid=(group,),
            in_specs=[whole_block(each.shape) for each in inputs],
            out_specs=out_specs,
            scratch_shapes=[pltpu.VMEM((HEAD_DIM, rows), low_type)],
        ),
        compiler_params=kernel_options(52),
        cost_estimate=declared,
        name="self_forward",
    )(owner, slot_of, *inputs)
    return made if make else [qkv, *made]


def self_backward(head, owner, place, blocks, qkv, mixed_grad, mixed, total):
    rows, width = qkv.shape[0], qkv.shape[1] // 3
    tok, model = blocks[0].shape
    group = rows // tok
    owned = pl.BlockSpec((None, HEAD_DIM, tok), lambda p, owner, _: (owner[p], 0, 0))
    return pl.pallas_call(
        functools.partial(
            self_backward_kernel, tok, width, group // 2, head, HEAD_DIM ** (-0.5), group
        ),
        out_shape=(
            jax.ShapeDtypeStruct((group, 3 * HEAD_DIM, tok), low_type),
            jax.ShapeDtypeStruct((3 * HEAD_DIM, model + LANES), jnp.float32),
        ),
        grid_spec=pltpu.PrefetchScalarGridSpec(
            num_scalar_prefetch=2,
            grid=(group,),
            in_specs=[pl.BlockSpec(memory_space=pl.ANY)] * group
            + [
                whole_block(qkv.shape),
                owned,
                owned,
                pl.BlockSpec((None, 1, tok), lambda p, *_: (p, 0, 0)),
            ],
            out_specs=[
                pl.BlockSpec((group, 3 * HEAD_DIM, tok), lambda *_: (0, 0, 0)),
                pl.BlockSpec((3 * HEAD_DIM, model + LANES), lambda *_: (0, 0)),
            ],
            scratch_shapes=[
                pltpu.VMEM((HEAD_DIM, rows), low_type),
                pltpu.VMEM((rows, width), jnp.float32),
                pltpu.VMEM((rows, width), jnp.float32),
                pltpu.VMEM((group, tok, model), low_type),
                pltpu.VMEM((3 * HEAD_DIM, model + LANES), jnp.float32),
                pltpu.SemaphoreType.DMA((group,)),
            ],
        ),
        compiler_params=kernel_options(52),
        cost_estimate=declared,
        name="self_backward",
    )(owner, place, *blocks, qkv, mixed_grad, mixed, total)


def split_columns(values, group):
    rows = values.shape[0]
    return values.reshape(rows, group, -1).transpose(1, 0, 2)


def join_columns(values):
    return values.transpose(1, 0, 2).reshape(values.shape[1], -1)


def by_head(values, group):
    rows, width = values.shape[0], values.shape[1] // group
    if width % LANES == 0:
        return values, pl.BlockSpec((rows, width), lambda g: (0, g))
    return split_columns(values, group), pl.BlockSpec((None, rows, width), lambda g: (g, 0, 0))


def of_heads(values, group):
    return values if values.ndim == 2 else join_columns(values)


def cross_forward(queries, pairs):
    group, _, states, width = pairs.shape
    rows = queries.shape[0]
    queries, query_spec = by_head(queries, group)
    mixed, total = pl.pallas_call(
        functools.partial(cross_forward_kernel, width),
        out_shape=(
            jax.ShapeDtypeStruct(queries.shape, low_type),
            jax.ShapeDtypeStruct((group, 8, rows), jnp.float32),
        ),
        grid=(group,),
        in_specs=[query_spec, pl.BlockSpec((None, 2, states, width), lambda g: (g, 0, 0, 0))],
        out_specs=[query_spec, pl.BlockSpec((None, 8, rows), lambda g: (g, 0, 0))],
        compiler_params=kernel_options(32),
        cost_estimate=declared,
        name="cross_forward",
    )(queries, pairs)
    return of_heads(mixed, group), total


def cross_backward(queries, pairs, mixed_grad, mixed, total):
    group, _, states, width = pairs.shape
    rows = queries.shape[0]
    queries, spec = by_head(queries, group)
    mixed_grad, mixed = by_head(mixed_grad, group)[0], by_head(mixed, group)[0]
    pair_spec = pl.BlockSpec((None, 2, states, width), lambda g: (g, 0, 0, 0))
    query_grad, pair_grad = pl.pallas_call(
        functools.partial(cross_backward_kernel, width, HEAD_DIM ** (-0.5)),
        out_shape=(
            jax.ShapeDtypeStruct(queries.shape, low_type),
            jax.ShapeDtypeStruct(pairs.shape, low_type),
        ),
        grid=(group,),
        in_specs=[spec, pair_spec, spec, spec, pl.BlockSpec((None, 8, rows), lambda g: (g, 0, 0))],
        out_specs=[spec, pair_spec],
        compiler_params=kernel_options(32),
        cost_estimate=declared,
        name="cross_backward",
    )(queries, pairs, mixed_grad, mixed, total)
    return of_heads(query_grad, group), pair_grad


def swap(values, axis, offset):
    size = lax.axis_size(axis)
    return lax.ppermute(values, axis, [(i, i ^ offset) for i in range(size)])


def sum_over(values, steps):
    for axis, offset in steps:
        values = (
            values.astype(jnp.float32) + swap(values, axis, offset).astype(jnp.float32)
        ).astype(values.dtype)
    return values


def bits_of(axis):
    return [(axis, 1 << i) for i in range(lax.axis_size(axis).bit_length() - 1)]


def spread_over_rep(values):
    return [values] + [swap(values, "rep", d) for d in range(1, lax.axis_size("rep"))]


def double(values, offset):
    return jnp.concatenate([values, swap(values, "rep", offset)], 0)


def rep_order(pieces):
    own = lax.axis_index("rep")
    count = len(pieces)
    return [lax.select_n(own, *[pieces[d ^ i] for i in range(count)]) for d in range(count)]


def trade_over_rep(pieces):
    return [pieces[0]] + [swap(pieces[d], "rep", d) for d in range(1, len(pieces))]


def sum_of(terms):
    return sum(term.astype(jnp.float32) for term in terms)


def trade_over_line(values):
    line, own = lax.axis_size("line"), lax.axis_index("line")
    terms = [lax.dynamic_index_in_dim(values, own, 0, keepdims=False)]
    for k in range(1, line):
        piece = lax.dynamic_index_in_dim(values, (own + k) % line, 0, keepdims=False)
        terms.append(lax.ppermute(piece, "line", [(i, (i + k) % line) for i in range(line)]))
    return terms


def two_rows(values):
    high = values.astype(low_type)
    return jnp.concatenate([high, (values - high.astype(jnp.float32)).astype(low_type)], -2)


def one_row(values):
    high, low = jnp.split(values.astype(jnp.float32), 2, -2)
    return high + low


def stage(values):
    return lax.optimization_barrier(values)


def shift(values):
    line = lax.axis_size("line")
    return lax.ppermute(values, "line", [(i, (i + 1) % line) for i in range(line)])


def gather_rows(values):
    return lax.all_gather(values, SHARD, axis=0, tiled=True)


def scatter_rows(values):
    return lax.psum_scatter(values, SHARD, scatter_dimension=0, tiled=True)


def exchange(values):
    return lax.all_to_all(values, SHARD, split_axis=0, concat_axis=0, tiled=True)


def gelu(values):
    return jax.nn.gelu(values, approximate=False)


def local(
    layer_input,
    encoder_states,
    out_grad,
    placement,
    w_self_qkv,
    w_self_out,
    w_cross_q,
    w_cross_kv,
    w_cross_out,
    w_fc1,
    w_fc2,
    proj_biases,
    fc1_bias,
    norm_gains,
    norm_shifts,
):
    reps, line = lax.axis_size("rep"), lax.axis_size("line")
    rep, core = lax.axis_index("rep"), lax.axis_index("core")
    group = 2 * line
    member = 2 * lax.axis_index("line") + core
    tok, model = layer_input.shape
    feed = w_fc1.shape[1]
    weight_rows = w_self_qkv.shape[0]
    width = model // group
    unit = feed // (group * reps)
    score_scale = HEAD_DIM ** (-0.5)
    slot_table = placement[0]
    device_ids = jnp.arange(group, dtype=jnp.int32)
    owners = jnp.sum(
        jnp.where(slot_table[None, :] == device_ids[:, None], device_ids[None, :], 0), 1
    )

    def own_columns(row):
        return lax.dynamic_slice(row, (member * width,), (width,))

    def in_columns(row):
        return lax.dynamic_update_slice(jnp.zeros((model,), jnp.float32), row, (member * width,))

    slices = jnp.concatenate(
        [
            w_self_qkv.reshape(reps, weight_rows // reps, 3, group, width),
            w_cross_kv.reshape(reps, weight_rows // reps, 2, group, width),
        ],
        2,
    )
    slices = lax.dynamic_index_in_dim(slices, rep, 0, keepdims=False)
    slices = slices.transpose(2, 0, 1, 3).reshape(group, weight_rows // reps, 5 * width)
    first_cut = w_fc1.reshape(weight_rows, line, 2, reps, unit)
    first_cut = lax.dynamic_index_in_dim(first_cut, rep, 3, keepdims=False)
    first_own = lax.dynamic_index_in_dim(first_cut, core, 2, keepdims=False)
    first_other = lax.dynamic_index_in_dim(first_cut, 1 - core, 2, keepdims=False)
    first_own = first_own.reshape(weight_rows, line * unit)
    first_other = swap(first_other.reshape(weight_rows, line * unit), "core", 1)
    first_cut = jnp.where(
        core == 0,
        jnp.concatenate([first_own, first_other], 0),
        jnp.concatenate([first_other, first_own], 0),
    )
    second_cut = lax.dynamic_slice_in_dim(w_fc2, rep * unit, unit, 0)
    bias_cut = lax.dynamic_index_in_dim(
        fc1_bias.reshape(line, 2, reps, unit), core, 1, keepdims=False
    )
    bias_cut = [bias_cut[:, r].reshape(line * unit) for r in range(reps)]
    bias_cut = rep_order(bias_cut)

    square = jnp.stack([w_self_out, w_cross_q, w_cross_out], 0)
    square = square.reshape(3, reps, weight_rows // reps, model)
    square = lax.dynamic_index_in_dim(square, rep, 1, keepdims=False)
    square = square.reshape(-1, model // (line * unit), line * unit).transpose(1, 0, 2)
    square = square.reshape(-1, line * unit)

    inputs = layer_input.astype(jnp.float32)
    zeros = jnp.zeros((width,), jnp.float32)
    head_bias = jnp.concatenate([own_columns(proj_biases[0]), zeros, own_columns(proj_biases[1])])
    head_scale = jnp.concatenate([jnp.full((width,), score_scale), jnp.ones((2 * width,))])
    cross_bias = jnp.concatenate([zeros, own_columns(proj_biases[4])])

    near = [1 << i for i in range(reps.bit_length() - 1)]
    far = [d for d in range(1, reps) if d not in near]
    slices = exchange(slices)
    blocks = [layer_input, swap(layer_input, "core", 1)]
    block = shift(layer_input)
    block, slices, blocks, first_cut, square, encoder_states, second_cut = stage(
        (block, slices, blocks, first_cut, square, encoder_states, second_cut)
    )

    both_cut = lax.all_gather(
        jnp.concatenate([first_cut, square], 0), "line", axis=0, tiled=True
    ).reshape(line, -1, line * unit)
    blocks += [block, swap(block, "core", 1)]
    block = shift(block)
    slices = spread_over_rep(slices)
    block, slices, blocks, encoder_states = stage((block, slices, blocks, encoder_states))

    for step in range(line - 3):
        blocks += [block, swap(block, "core", 1)]
        block = shift(block)
    slices = jnp.stack(rep_order(slices), 1).reshape(model, 5 * width)
    head_qkv, head_ckv = slices[:, : 3 * width], slices[:, 3 * width :]
    all_states = gather_rows(encoder_states)
    block, blocks, both_cut, head_qkv, head_ckv, all_states, second_cut = stage(
        (block, blocks, both_cut, head_qkv, head_ckv, all_states, second_cut)
    )

    blocks += [block, swap(block, "core", 1)]
    square = spread_over_rep(both_cut[:, 2 * weight_rows :])
    second_cut = lax.all_gather(second_cut, "line", axis=0, tiled=True)
    wfirst = {0: both_cut[:, : 2 * weight_rows].reshape(model, line * unit)}
    head_pair = (product(all_states, head_ckv) + cross_bias).astype(low_type)
    head_pair = split_columns(head_pair, 2)
    wsecond = {0: second_cut}
    back = (lax.axis_index("line") - owners // 2) % line
    places = 2 * back + ((owners % 2) ^ core)
    slot_of = jnp.sum(
        jnp.where(places[None, :] == device_ids[:, None], device_ids[None, :], 0), 1
    )
    heads = width // HEAD_DIM
    made, turn, self_totals, self_mixed, self_low = None, owners, [], [], []
    for head in range(heads):
        extra = () if head else (blocks, head_qkv, head_bias, head_scale)
        made, mixed, total = self_forward(head, turn, slot_of, tok, made, *extra)
        self_totals.append(total)
        if head == 0:
            mixed, turn, square, head_pair = stage((mixed, turn, square, head_pair))
            wfirst.update({d: swap(wfirst[0], "rep", d) for d in near})
            square = jnp.stack(rep_order(square), 1)
            square_other = swap(square, "core", 1)
        if head == heads - 1:
            held = (mixed, wfirst, square, square_other)
            held, wsecond, self_low = stage((held, wsecond, self_low))
            mixed, wfirst, square, square_other = held
            wfirst.update({d: swap(wfirst[0], "rep", d) for d in far})
            wsecond.update({d: swap(wsecond[0], "rep", d) for d in near})
        self_mixed.append(mixed)
        self_low.append(exchange(mixed))
    qkv = made
    square = jnp.where(
        core == 0, jnp.stack([square, square_other], 1), jnp.stack([square_other, square], 1)
    )
    square = square.reshape(line, 2, reps, -1, 3, weight_rows // reps, line * unit)
    full_out, full_cross_q, full_cross_out = [
        square[:, :, :, :, i].transpose(0, 1, 2, 4, 3, 5).reshape(model, model)
        for i in range(3)
    ]
    pairs = lax.all_gather(head_pair, SHARD, axis=0, tiled=False)
    self_low, pairs = stage((self_low, pairs))
    self_low = jnp.stack(self_low, 1).reshape(model, tok)

    first_sum = inputs + (product_left(self_low, full_out) + proj_biases[2])
    first_norm, norm1_back = jax.vjp(norm_rows, first_sum, norm_gains[0], norm_shifts[0])
    first_low = first_norm.astype(low_type)
    cross_queries = ((product(first_low, full_cross_q) + proj_biases[3]) * score_scale).astype(
        low_type
    )
    turned = jnp.transpose(stage((head_qkv, cross_queries))[0])
    turned = turned.reshape(3, heads, HEAD_DIM, model).transpose(1, 0, 2, 3)
    turned = gather_rows(turned.reshape(-1, model))
    turned = turned.reshape(group, heads, 3 * HEAD_DIM, model)

    cross_low, cross_total = cross_forward(cross_queries, pairs)
    cross_low, wfirst, wsecond = stage((cross_low, wfirst, wsecond))
    wsecond.update({d: swap(wsecond[0], "rep", d) for d in far})
    second_sum = first_norm + (product(cross_low, full_cross_out) + proj_biases[5])
    second_norm, norm2_back = jax.vjp(norm_rows, second_sum, norm_gains[1], norm_shifts[1])
    second_low = second_norm.astype(low_type)

    second_both = jnp.concatenate([second_low, swap(second_low, "core", 1)], 0)
    feed_sum, hidden, gelu_back = 0.0, [], []
    for part in range(reps):
        active, back = jax.vjp(gelu, product(second_both, wfirst[part]) + bias_cut[part])
        hidden.append(active.astype(low_type))
        gelu_back.append(back)
        feed_sum = feed_sum + product(hidden[part], wsecond[part])
    feed_sum, turned = stage((feed_sum, turned))
    feed_other = swap(feed_sum[tok:].astype(low_type), "core", 1).astype(jnp.float32)
    third_sum = second_norm + (feed_sum[:tok] + feed_other + proj_biases[6])
    result, norm3_back = jax.vjp(norm_rows, third_sum, norm_gains[2], norm_shifts[2])
    output = result.astype(low_type)

    third_grad, gain_three, shift_three = norm3_back(out_grad.astype(jnp.float32))
    feed_grad = third_grad.astype(low_type)
    bias_fc2 = column_sums(feed_grad)
    feed_both = jnp.concatenate([feed_grad, swap(feed_grad, "core", 1)], 0)
    second_parts = [
        product_left(hidden[part], feed_both).astype(low_type) for part in range(reps)
    ]
    feed_both, second_parts = stage((feed_both, second_parts))
    second_terms = {0: second_parts[0]}
    second_terms.update({d: swap(second_parts[d], "rep", d) for d in near})
    back_sum, first_parts, bias_parts = 0.0, [], []
    for part in range(reps):
        pre_grad = gelu_back[part](product_right(feed_both, wsecond[part]))[0].astype(low_type)
        first_parts.append(product_left(second_both, pre_grad).astype(low_type))
        bias_parts.append(column_sums(pre_grad))
        back_sum = back_sum + product_right(pre_grad, wfirst[part])
    back_sum, second_terms, first_parts = stage((back_sum, second_terms, first_parts))
    second_terms.update({d: swap(second_parts[d], "rep", d) for d in far})
    back_other = swap(back_sum[tok:].astype(low_type), "core", 1).astype(jnp.float32)
    second_grad, gain_two, shift_two = norm2_back(third_grad + (back_sum[:tok] + back_other))
    first_terms = {0: first_parts[0]}
    first_terms.update({d: swap(first_parts[d], "rep", d) for d in near})

    cross_out_grad = second_grad.astype(low_type)
    part_cross_out = product_left(cross_low, cross_out_grad).astype(low_type)
    bias_cross_out = column_sums(cross_out_grad)
    cross_mixed_grad = product_right(cross_out_grad, full_cross_out).astype(low_type)
    cross_q_grad, pair_grad = cross_backward(
        cross_queries, pairs, cross_mixed_grad, cross_low, cross_total
    )
    cross_q_grad, pair_grad, second_terms = stage((cross_q_grad, pair_grad, second_terms))
    second_sums = sum_of(second_terms.values()).astype(low_type)
    second_sums = lax.psum_scatter(second_sums, "line", scatter_dimension=0, tiled=True)
    own_pair_grad = lax.psum_scatter(pair_grad, SHARD, scatter_dimension=0, tiled=False)
    part_cross_q = product_left(first_low, cross_q_grad).astype(low_type)
    bias_cross_q = column_sums(cross_q_grad)
    first_grad, gain_one, shift_one = norm1_back(
        second_grad + product_right(cross_q_grad, full_cross_q)
    )
    self_out_grad = first_grad.astype(low_type)
    bias_self_out = column_sums(self_out_grad)
    mixed_grad = product_right(full_out, self_out_grad).astype(low_type)
    mixed_grad, first_terms = stage((mixed_grad, first_terms))
    mixed_grad = mixed_grad.reshape(group, heads, HEAD_DIM, tok)
    mixed_grad = [exchange(mixed_grad[:, head]) for head in range(heads)]
    part_self_out = product(self_low, self_out_grad).astype(low_type)

    square = jnp.stack([part_self_out, part_cross_q, part_cross_out], 0)
    square = square.reshape(3, line, 2, reps, weight_rows // reps, model)
    square_own = lax.dynamic_index_in_dim(square, core, 2, keepdims=False)
    square_other = swap(lax.dynamic_index_in_dim(square, 1 - core, 2, keepdims=False), "core", 1)

    bias_parts = jnp.stack([part.reshape(line, unit) for part in rep_order(bias_parts)], 1)
    bias_fc1 = jnp.where(
        jnp.arange(2)[None, :, None, None] == core, bias_parts[:, None], 0.0
    ).reshape(feed)
    small = jnp.concatenate(
        [
            jnp.stack(
                [
                    bias_self_out,
                    bias_cross_q,
                    bias_cross_out,
                    bias_fc2,
                    gain_one,
                    gain_two,
                    gain_three,
                    shift_one,
                    shift_two,
                    shift_three,
                ],
                0,
            ),
            bias_fc1.reshape(-1, model),
        ],
        0,
    )
    hops = bits_of("core") + bits_of("rep") + bits_of("line")

    def hop(values, count):
        for _ in range(count):
            values = values + swap(values, *hops.pop(0))
        return values

    small = hop(small, 1)
    square = square_own.astype(jnp.float32) + square_other.astype(jnp.float32)
    square = square.astype(low_type).transpose(2, 1, 0, 3, 4)
    square = rep_order([square[r] for r in range(reps)])
    mixed_grad[0], square, small, second_sums = stage(
        (mixed_grad[0], square, small, second_sums)
    )
    first_terms.update({d: swap(first_parts[d], "rep", d) for d in far})
    square_terms = trade_over_rep(square)
    wide = 2 * line * unit
    second_sums = second_sums.reshape(unit, model // wide, wide).transpose(1, 0, 2)
    second_sums = double(second_sums.reshape(1, -1, wide), near[0])
    turn = owners

    part_rows = weight_rows // reps

    def with_sums(values, sums):
        rows = two_rows(jnp.broadcast_to(sums, sums.shape[:-2] + (8,) + sums.shape[-1:]))
        return jnp.concatenate([values.astype(low_type), rows], -2)

    def split_sums(values):
        return values[..., :part_rows, :], one_row(values[..., part_rows:, :])[..., :1, :]

    def trade_slices(values):
        sums = jnp.broadcast_to(values[model : model + 1], (group, 1, values.shape[1]))
        values = values[:model].reshape(group, reps, part_rows, -1)
        values = [with_sums(values[:, r], sums) for r in range(reps)]
        return trade_over_rep(rep_order(values))

    def exchange_slices(terms):
        return exchange(with_sums(*split_sums(sum_of(terms))))

    def join_slices(values):
        values, sums = split_sums(values.astype(jnp.float32))
        values = jnp.stack(rep_order(spread_over_rep(values.astype(low_type))), 0)
        values = values.transpose(0, 2, 1, 3).reshape(weight_rows, group, -1)
        return values, sums[:, 0][None]

    parts, slice_parts = [], []
    for head in range(heads):
        part, slice_part = self_backward(
            head,
            turn,
            places,
            blocks,
            qkv,
            mixed_grad[head],
            self_mixed[head],
            self_totals[head],
        )
        if head == 0:
            held = (part, slice_part, turn, first_terms, second_sums, square_terms)
            held, mixed_grad, own_pair_grad = stage((held, mixed_grad, own_pair_grad))
            part, slice_part, turn, first_terms, second_sums, square_terms = held
            first_sums = sum_of(first_terms.values()).astype(low_type)
            first_sums = lax.psum_scatter(first_sums, "line", scatter_dimension=0, tiled=True)
            for offset in near[1:]:
                second_sums = double(second_sums, offset)
            small = hop(small, 1)
            own_pair_grad = join_columns(own_pair_grad)
            enc_grad = scatter_rows(product_right(own_pair_grad, head_ckv).astype(low_type))
            pair_sums = jnp.sum(own_pair_grad.astype(jnp.float32), 0)
            pair_sums = jnp.broadcast_to(pair_sums, (LANES, 2 * width))
            pair_slices = jnp.concatenate([product_left(all_states, own_pair_grad), pair_sums], 0)
            square_terms = trade_over_line(sum_of(square_terms).astype(low_type))
        if head == heads - 1:
            held = (part, slice_part, square_terms, first_sums, second_sums, small)
            held, parts, slice_parts = stage((held, parts, slice_parts))
            part, slice_part, square_terms, first_sums, second_sums, small = held
        parts.append(exchange(part))
        slice_parts.append(jnp.transpose(slice_part))

    slice_parts = trade_slices(
        jnp.concatenate([slice_parts[0], pair_slices] + slice_parts[1:], 1)
    )
    first_sums = first_sums.reshape(2, weight_rows, line * unit).transpose(1, 0, 2)
    first_sums = double(first_sums.reshape(1, -1, wide), near[0])
    square = double(sum_of(square_terms).astype(low_type)[None], near[0])
    parts, slice_parts, first_sums, square = stage((parts, slice_parts, first_sums, square))

    slice_parts = exchange_slices(slice_parts)
    for offset in near[1:]:
        square = double(square, offset)
        first_sums = double(first_sums, offset)
    small = hop(small, 1)
    second_sums = jnp.stack(rep_order([second_sums[d] for d in range(reps)]), 0)
    second_sums = second_sums.reshape(reps, model // wide, unit, wide)
    grad_fc2 = second_sums.transpose(0, 2, 1, 3).reshape(-1, model).astype(jnp.float32)
    input_grad = first_grad
    for head in range(heads):
        rows = turned[:, head].reshape(group * 3 * HEAD_DIM, model)
        input_grad = input_grad + product_left(parts[head].reshape(rows.shape[0], tok), rows)
    slice_parts, first_sums, square, input_grad, grad_fc2, small, enc_grad = stage(
        (slice_parts, first_sums, square, input_grad, grad_fc2, small, enc_grad)
    )

    first_sums = jnp.stack(rep_order([first_sums[d] for d in range(reps)]), 0)
    first_sums = first_sums.reshape(reps, weight_rows, 2, line, unit)
    first_own = lax.dynamic_index_in_dim(first_sums, core, 2, keepdims=False)
    first_other = lax.dynamic_index_in_dim(first_sums, 1 - core, 2, keepdims=False)
    first_other = swap(first_other.reshape(-1, line * unit), "core", 1)
    first_other = first_other.reshape(first_own.shape)

    slice_parts = join_slices(slice_parts)
    small = hop(small, len(hops))
    square = jnp.stack(rep_order([square[d] for d in range(reps)]), 1).astype(jnp.float32)
    grad_self_out, grad_cross_q, grad_cross_out = [
        square[i].reshape(weight_rows, model) for i in range(3)
    ]
    grad_fc1 = jnp.where(
        core == 0, jnp.stack([first_own, first_other], 0), jnp.stack([first_other, first_own], 0)
    )
    grad_fc1 = grad_fc1.transpose(2, 3, 0, 1, 4).reshape(weight_rows, feed).astype(jnp.float32)

    def of_self(values):
        found, start = [], 0
        for head in range(heads):
            found.append(values[..., start : start + 3 * HEAD_DIM])
            start += 3 * HEAD_DIM + (0 if head else 2 * width)
        found = [each.reshape(-1, group, 3, HEAD_DIM) for each in found]
        return jnp.stack(found, 3).transpose(0, 2, 1, 3, 4).reshape(-1, 3, model)

    def of_cross(values):
        values = values[..., 3 * HEAD_DIM : 3 * HEAD_DIM + 2 * width]
        return values.reshape(-1, group, 2, width).transpose(0, 2, 1, 3).reshape(-1, 2, model)

    grad_self_qkv = of_self(slice_parts[0].astype(jnp.float32)).reshape(weight_rows, 3 * model)
    grad_cross_kv = of_cross(slice_parts[0].astype(jnp.float32)).reshape(weight_rows, 2 * model)
    bias_self, bias_cross_v = of_self(slice_parts[1]), of_cross(slice_parts[1])[0, 1]
    grad_biases = jnp.stack(
        [
            bias_self[0, 0],
            bias_self[0, 2],
            small[0],
            small[1],
            bias_cross_v,
            small[2],
            small[3],
        ],
        0,
    )
    return (
        output,
        input_grad,
        enc_grad.astype(jnp.float32),
        grad_self_qkv,
        grad_self_out,
        grad_cross_q,
        grad_cross_kv,
        grad_cross_out,
        grad_fc1,
        grad_fc2,
        grad_biases,
        small[10:].reshape(-1),
        small[4:7],
        small[7:10],
    )


def solution(mesh):
    reps, group = mesh.devices.shape
    split = jax.sharding.Mesh(
        mesh.devices.reshape(reps, group // 2, 2), ("rep",) + SHARD
    )
    rows, cut = P(("rep",) + SHARD, None), P(SHARD, None)
    return jax.shard_map(
        local,
        mesh=split,
        in_specs=(rows,) * 3 + (P("rep", None),) + (cut,) * 7 + (P(),) * 4,
        out_specs=(rows,) * 3 + (cut,) * 7 + (P(),) * 4,
        check_vma=False,
    )
```

time: 756 us -> 750 us (level)
  waiting for transfers between devices: 257 us -> 200 us
  starting transfers between devices: 63.2 us -> 107 us
  local copies, waits for them, and re-layouts: 76.8 us -> 106 us
  blocking collectives: 21.4 us -> 0 us
  matrix products: 130 us -> 115 us
    ppermute x53 -> x50, waiting for transfers between devices: 162 us -> 90.1 us  [swap(): return lax.ppermute(values, axis, [(i, i ^ offset) for i in range(size)])]
    ppermute x3, waiting for transfers between devices: 33 us -> 62.7 us  [shift(): lax.ppermute(values, 'line', [(i, (i + 1) % line) for i in range(line)])]
    all_gather x1, waiting for transfers between devices: 26 us -> 0.01 us  [local(): lax.all_gather(jnp.concatenate([first_cut, square], 0), 'line', axis=0, t...]
    all_to_all x3 -> x8, waiting for transfers between devices: 6.16 us -> 32 us  [exchange(): lax.all_to_all(values, SHARD, split_axis=0, concat_axis=0, tiled=True)]
    all_to_all x3 -> x8, starting transfers between devices: 13.3 us -> 35.3 us  [exchange(): lax.all_to_all(values, SHARD, split_axis=0, concat_axis=0, tiled=True)]
    all_to_all x1 -> x0, blocking collectives: 21.4 us -> none  [exchange(): lax.all_to_all(values, SHARD, split_axis=0, concat_axis=0, tiled=True)]
    reduce_scatter x2, starting transfers between devices: 0.25 us -> 11.1 us  [the longest x1 11.1 us: local(): lax.psum_scatter(second_sums, 'line', scatter_dimension=0, tiled=True)]
    ppermute x3, waiting for transfers between devices: 22.2 us -> 12.3 us  [trade_over_line(): lax.ppermute(piece, 'line', [(i, (i + k) % line) for i in range(line)])]
  transfers between devices with their start and end apart: 71 -> 73, of which waited for: 29 -> 27; matrix products, arithmetic and copies ran while one was open for 20% -> 30% of each run, Pallas kernels for 17% -> 18%
where the time goes in v3:
time: 750 us; the launch traced here: 739 us
  waiting for transfers between devices  200 us (27%)
  Pallas kernels  130 us (17%)
  matrix products  115 us (15%)
  starting transfers between devices  107 us (14%)
  local copies, waits for them, and re-layouts  106 us (14%)
  other arithmetic  64.8 us (9%)
  between operations  16.2 us (2%)
    ppermute x50, waiting for transfers between devices, swap(): return lax.ppermute(values, axis, [(i, i ^ offset) for i in range(size)])  90.1 us
    ppermute x3, waiting for transfers between devices, shift(): lax.ppermute(values, 'line', [(i, (i + 1) % line) for i in range(line)])  62.7 us
    pallas_call x2, Pallas kernels, self_backward(): pl.pallas_call(functools.partial(self_backward_kernel, tok, width, group...  61 us
    dot_general x12, matrix products, product(): return jnp.dot(former, latter, preferred_element_type=jnp.float32)  51.8 us
    ppermute x50, starting transfers between devices, swap(): return lax.ppermute(values, axis, [(i, i ^ offset) for i in range(size)])  46.7 us
    pallas_call x2, Pallas kernels, self_forward(): pl.pallas_call(functools.partial(self_forward_kernel, tok, width, group /...  44.2 us
    unnamed x214, local copies, waits for them, and re-layouts  39.7 us
    all_to_all x8, starting transfers between devices, exchange(): lax.all_to_all(values, SHARD, split_axis=0, concat_axis=0, tiled=True)  35.3 us
  transfers between devices with their start and end apart: 73, of which 27 were waited for; matrix products, arithmetic and copies ran while one was open for 30% of the time, Pallas kernels for 18%

profile of v3, /device:TPU:0, one launch (start us, length us, event | category | flops | bytes accessed | tf_op | source)
XLA Modules:
  0.0 738.6 jit_solution(685671044577286698)
XLA Ops:
  33.8 8.9 %all-to-all-done = bf16[8,32,640]{2,1,0:T(8,128)(2,1)S(1)} async-done(((bf16[8,32,640]{2,1,0:T(8,128)(2,1)}), bf16[8,32,640]{2,1,0:T(8,128)(2,1)S(1)}, u32[]{:S(2)}, u32[]{:S(2)}) %all-to-all-start) | async-done | bytes 327712 | tf_op jit(solution)/shard_map/all_to_all | solution.py:464
  48.8 7.0 collective-permute-done.4
  55.9 7.8 %collective-permute-done.5 = bf16[8,32,640]{2,1,0:T(8,128)(2,1)S(1)} collective-permute-done((bf16[8,32,640]{2,1,0:T(8,128)(2,1)S(1)}, bf16[8,32,640]{2,1,0:T(8,128)(2,1)S(1)}, u32[]{:S(2)}, u32[]{:S(2)}) %collective-permute-start.5) | collective-permute-done | bytes 327712 | tf_op jit(solution)/shard_map/ppermute | solution.py:390
  63.6 24.9 %collective-permute-done.3.refs_4_ = bf16[512,1024]{1,0:T(8,128)(2,1)} collective-permute-done((bf16[512,1024]{1,0:T(8,128)(2,1)S(1)}, bf16[512,1024]{1,0:T(8,128)(2,1)}, u32[]{:S(2)}, u32[]{:S(2)}) %collective-permute-start.3) | collective-permute-done | bytes 1048608 | tf_op jit(solution)/shard_map/ppermute | solution.py:452
  93.5 37.8 %collective-permute-done.8.refs_6_ = bf16[512,1024]{1,0:T(8,128)(2,1)} collective-permute-done((bf16[512,1024]{1,0:T(8,128)(2,1)}, bf16[512,1024]{1,0:T(8,128)(2,1)}, u32[]{:S(2)}, u32[]{:S(2)}) %collective-permute-start.8) | collective-permute-done | bytes 1048608 | tf_op jit(solution)/shard_map/ppermute | solution.py:452
  143.6 25.9 %self_forward.2 = (bf16[4096,384]{1,0:T(8,128)(2,1)}, bf16[8,64,512]{2,1,0:T(8,128)(2,1)}, f32[8,1,512]{2,1,0:T(1,128)S(1)}) custom-call(s32[8]{0:T(128)S(1)} %select_reduce_fusion.1.owner, s32[8]{0:T(128)S(1)} %select_reduce_fusion.slot_of, bf16[512,1024]{1,0:T(8,128)(2,1)} %refs_0_.2, bf16[512,1024]{1,0:T(8,128)(2,1)} %copy-done.26, ...), custom_call_target="tpu_custom_call" | custom-call | flops 1048576 | bytes 65536 | tf_op jit(solution)/shard_map/self_forward/pallas_call | solution.py:265
  185.9 18.4 %self_forward.3 = (bf16[8,64,512]{2,1,0:T(8,128)(2,1)}, f32[8,1,512]{2,1,0:T(1,128)S(1)}) custom-call(s32[8]{0:T(128)S(1)} %select_reduce_fusion.1.owner, s32[8]{0:T(128)S(1)} %select_reduce_fusion.slot_of, bf16[4096,384]{1,0:T(8,128)(2,1)} %get-tuple-element.187.refs_0_.refs_8_), custom_call_target="tpu_custom_call" | custom-call | flops 1048576 | bytes 65536 | tf_op jit(solution)/shard_map/self_forward/pallas_call | solution.py:265
  206.8 7.4 %all-to-all-done.1 = bf16[8,64,512]{2,1,0:T(8,128)(2,1)S(1)} async-done(((bf16[8,64,512]{2,1,0:T(8,128)(2,1)}), bf16[8,64,512]{2,1,0:T(8,128)(2,1)S(1)}, u32[]{:S(2)}, u32[]{:S(2)}) %all-to-all-start.1) | async-done | bytes 524320 | tf_op jit(solution)/shard_map/all_to_all | solution.py:464
  248.7 11.1 %reduce-scatter.5.cloned.1.call-start = ((), (), s32[]{:S(2)}) async-start(), calls=%async_computation.16 | async-start | bytes 1310720 | tf_op jit(solution)/shard_map/reduce_scatter | solution.py:683
  263.6 10.9 %cross_forward.1 = (bf16[512,1024]{1,0:T(8,128)(2,1)S(1)}, f32[8,8,512]{2,1,0:T(8,128)S(1)}) custom-call(bf16[512,1024]{1,0:T(8,128)(2,1)S(1)} %multiply_convert_fusion.4.query, bf16[8,2,512,128]{3,2,1,0:T(8,128)(2,1)S(1)} %bitcast.392), custom_call_target="tpu_custom_call" | custom-call | flops 1048576 | bytes 65536 | tf_op jit(solution)/shard_map/cross_forward/pallas_call | solution.py:350
  280.0 9.4 %multiply_convert_fusion.3 = (bf16[1024,512]{1,0:T(8,128)(2,1)S(1)}, f32[1024,512]{1,0:T(8,128)}, f32[1024,512]{1,0:T(8,128)}) fusion(f32[512]{0:T(512)S(1)} %bitcast.502, bf16[1024,512]{1,0:T(8,128)(2,1)} %bitcast.25, bf16[512,1024]{1,0:T(8,128)(2,1)S(1)} %collective-permute-done.20, bf16[512,1024]{1,0:T(8,128)(2,1)S(1)} %fusion.31), kind=kOutput, calls=%fused_computation.100 | convolution fusion | flops 1112539136 | bytes 8390656 | tf_op jit(solution)/shard_map/dot_general | solution.py:28
  290.7 9.0 %multiply_convert_fusion.2 = (bf16[1024,512]{1,0:T(8,128)(2,1)S(1)}, f32[1024,512]{1,0:T(8,128)}, f32[1024,512]{1,0:T(8,128)}) fusion(f32[512]{0:T(512)S(1)} %bitcast.504, bf16[1024,512]{1,0:T(8,128)(2,1)} %collective-permute-done.14, bf16[512,1024]{1,0:T(8,128)(2,1)S(1)} %collective-permute-done.20, bf16[512,1024]{1,0:T(8,128)(2,1)S(1)} %fusion.31), kind=kOutput, calls=%fused_computation.87 | convolution fusion | flops 1112539136 | bytes 8390656 | tf_op jit(solution)/shard_map/dot_general | solution.py:28
  302.7 7.8 %multiply_convert_fusion.1 = (bf16[1024,512]{1,0:T(8,128)(2,1)S(1)}, f32[1024,512]{1,0:T(8,128)}, f32[1024,512]{1,0:T(8,128)}) fusion(f32[512]{0:T(512)S(1)} %bitcast.500, bf16[1024,512]{1,0:T(8,128)(2,1)S(1)} %copy-done.80, bf16[512,1024]{1,0:T(8,128)(2,1)S(1)} %collective-permute-done.20, bf16[512,1024]{1,0:T(8,128)(2,1)S(1)} %fusion.31), kind=kOutput, calls=%fused_computation.74 | convolution fusion | flops 1112539136 | bytes 8390656 | tf_op jit(solution)/shard_map/dot_general | solution.py:28
  313.4 9.4 %multiply_convert_fusion = (bf16[1024,512]{1,0:T(8,128)(2,1)S(1)}, f32[1024,512]{1,0:T(8,128)}, f32[1024,512]{1,0:T(8,128)}) fusion(f32[512]{0:T(512)S(1)} %bitcast.498, bf16[1024,512]{1,0:T(8,128)(2,1)} %collective-permute-done.17, bf16[512,1024]{1,0:T(8,128)(2,1)S(1)} %collective-permute-done.20, bf16[512,1024]{1,0:T(8,128)(2,1)S(1)} %fusion.31), kind=kOutput, calls=%fused_computation.61 | convolution fusion | flops 1112539136 | bytes 8390656 | tf_op jit(solution)/shard_map/dot_general | solution.py:28
  382.5 8.3 %collective-permute-done.24 = bf16[512,1024]{1,0:T(8,128)(2,1)S(1)} collective-permute-done((bf16[512,1024]{1,0:T(8,128)(2,1)S(1)}, bf16[512,1024]{1,0:T(8,128)(2,1)S(1)}, u32[]{:S(2)}, u32[]{:S(2)}) %collective-permute-start.24) | collective-permute-done | bytes 1048608 | tf_op jit(solution)/shard_map/ppermute | solution.py:390
  400.9 13.9 %cross_backward.1 = (bf16[512,1024]{1,0:T(8,128)(2,1)S(1)}, bf16[8,2,512,128]{3,2,1,0:T(8,128)(2,1)}) custom-call(bf16[512,1024]{1,0:T(8,128)(2,1)S(1)} %multiply_convert_fusion.4.query, bf16[8,2,512,128]{3,2,1,0:T(8,128)(2,1)S(1)} %bitcast.393, bf16[512,1024]{1,0:T(8,128)(2,1)S(1)} %convolution_convert_fusion.5.mixed_grad, bf16[512,1024]{1,0:T(8,128)(2,1)S(1)} %copy-done.6, ...), custom_call_target="tpu_custom_call" | custom-call | flops 1048576 | bytes 65536 | tf_op jit(solution)/shard_map/cross_backward/pallas_call | solution.py:372
  423.3 4.9 multiply_reduce_fusion.1
  444.6 20.5 %collective-permute-done.28 = bf16[1024,512]{1,0:T(8,128)(2,1)S(1)} collective-permute-done((bf16[1024,512]{1,0:T(8,128)(2,1)}, bf16[1024,512]{1,0:T(8,128)(2,1)S(1)}, u32[]{:S(2)}, u32[]{:S(2)}) %collective-permute-start.28) | collective-permute-done | bytes 1048608 | tf_op jit(solution)/shard_map/ppermute | solution.py:390
  466.6 5.0 all-to-all-start.3
  474.3 6.4 fusion.1
  484.0 10.2 %all-to-all-done.3.refs_9_ = bf16[8,64,512]{2,1,0:T(8,128)(2,1)S(1)} async-done(((bf16[8,64,512]{2,1,0:T(8,128)(2,1)}), bf16[8,64,512]{2,1,0:T(8,128)(2,1)S(1)}, u32[]{:S(2)}, u32[]{:S(2)}) %all-to-all-start.3) | async-done | bytes 524320 | tf_op jit(solution)/shard_map/all_to_all | solution.py:464
  505.5 30.3 %self_backward.2 = (bf16[8,192,512]{2,1,0:T(8,128)(2,1)}, f32[192,1152]{1,0:T(8,128)S(1)}) custom-call(s32[8]{0:T(128)S(1)} %copy-done.8, s32[8]{0:T(128)S(1)} %copy-done.10, bf16[512,1024]{1,0:T(8,128)(2,1)} %refs_0_.2, bf16[512,1024]{1,0:T(8,128)(2,1)} %copy-done.26, bf16[512,1024]{1,0:T(8,128)(2,1)} %copy-done.25, ...), custom_call_target="tpu_custom_call" | custom-call | flops 1048576 | bytes 65536 | tf_op jit(solution)/shard_map/self_backward/pallas_call | solution.py:289
  535.9 7.6 %collective-permute-done.33 = bf16[1,128,1024]{2,1,0:T(8,128)(2,1)S(1)} collective-permute-done((bf16[1,128,1024]{2,1,0:T(8,128)(2,1)}, bf16[1,128,1024]{2,1,0:T(8,128)(2,1)S(1)}, u32[]{:S(2)}, u32[]{:S(2)}) %collective-permute-start.33) | collective-permute-done | bytes 262176 | tf_op jit(solution)/shard_map/ppermute | solution.py:390
  543.5 4.8 all-to-all-start.5
  563.8 6.6 fusion.71
  571.1 30.6 %self_backward.3 = (bf16[8,192,512]{2,1,0:T(8,128)(2,1)}, f32[192,1152]{1,0:T(8,128)S(1)}) custom-call(s32[8]{0:T(128)S(1)} %copy-done.8, s32[8]{0:T(128)S(1)} %copy-done.10, bf16[512,1024]{1,0:T(8,128)(2,1)} %refs_0_.2, bf16[512,1024]{1,0:T(8,128)(2,1)} %copy-done.26, bf16[512,1024]{1,0:T(8,128)(2,1)} %copy-done.25, ...), custom_call_target="tpu_custom_call" | custom-call | flops 1048576 | bytes 65536 | tf_op jit(solution)/shard_map/self_backward/pallas_call | solution.py:289
  603.9 12.3 %collective-permute-done.38 = bf16[3,32,1024]{2,1,0:T(8,128)(2,1)} collective-permute-done((bf16[3,32,1024]{2,1,0:T(8,128)(2,1)}, bf16[3,32,1024]{2,1,0:T(8,128)(2,1)}, u32[]{:S(2)}, u32[]{:S(2)}) %collective-permute-start.38) | collective-permute-done | bytes 196640 | tf_op jit(solution)/shard_map/ppermute | solution.py:432
  616.2 6.3 all-to-all-start.6
  647.7 5.5 collective-permute-done.42
  653.2 10.2 %collective-permute-done.44 = bf16[8,48,640]{2,1,0:T(8,128)(2,1)S(1)} collective-permute-done((bf16[8,48,640]{2,1,0:T(8,128)(2,1)S(1)}, bf16[8,48,640]{2,1,0:T(8,128)(2,1)S(1)}, u32[]{:S(2)}, u32[]{:S(2)}) %collective-permute-start.44) | collective-permute-done | bytes 491552 | tf_op jit(solution)/shard_map/ppermute | solution.py:390
  664.7 5.6 all-to-all-done.6
  688.5 4.9 collective-permute-done.47
  (555 shorter events, 332.9 us)
Async XLA Ops:
  7.2 35.5 %collective-permute-start = (bf16[512,1024]{1,0:T(8,128)(2,1)}, bf16[512,1024]{1,0:T(8,128)(2,1)S(1)}, u32[]{:S(2)}, u32[]{:S(2)}) collective-permute-start(bf16[512,1024]{1,0:T(8,128)(2,1)} %refs_0_.2), channel_id=1, source_target_pairs={{0,2},{2,4},{4,6},{6,0},{1,3},{3,5},{5,7},{7,1},{8,10},{10,12},{12... | collective-permute-start | bytes 3145736 | tf_op jit(solution)/shard_map/ppermute | solution.py:452
  22.5 108.9 %all-gather.7.cloned.1.call-start = ((), (), s32[]{:S(2)}) async-start(), calls=%async_computation.12 | async-start | bytes 2293760 | tf_op jit(solution)/shard_map/all_gather | solution.py:558
  45.1 89.2 %all-gather.9.cloned.1.call-start = ((), (), s32[]{:S(2)}) async-start(), calls=%async_computation.13 | async-start | bytes 1179648 | tf_op jit(solution)/shard_map/all_gather | solution.py:456
  45.1 43.4 %collective-permute-start.3 = (bf16[512,1024]{1,0:T(8,128)(2,1)S(1)}, bf16[512,1024]{1,0:T(8,128)(2,1)}, u32[]{:S(2)}, u32[]{:S(2)}) collective-permute-start(bf16[512,1024]{1,0:T(8,128)(2,1)S(1)} %collective-permute-done.refs_2_), channel_id=1, source_target_pairs={{0,2},{2,4},{4,6},{6,0},{1,3},{3,5},{5,7},{7,1},{8,10},{10,12},{12... | collective-permute-start | bytes 3145736 | tf_op jit(solution)/shard_map/ppermute | solution.py:452
  45.2 43.3 %collective-permute-start.7 = (bf16[512,1024]{1,0:T(8,128)(2,1)S(1)}, bf16[512,1024]{1,0:T(8,128)(2,1)}, u32[]{:S(2)}, u32[]{:S(2)}) collective-permute-start(bf16[512,1024]{1,0:T(8,128)(2,1)S(1)} %collective-permute-done.refs_2_), channel_id=1, source_target_pairs={{0,1},{1,0},{2,3},{3,2},{4,5},{5,4},{6,7},{7,6},{8,9},{9,8},{10,11... | collective-permute-start | bytes 3145736 | tf_op jit(solution)/shard_map/ppermute | solution.py:390
  88.5 118.3 %all-gather.11.cloned.1.call-start = ((), (), s32[]{:S(2)}) async-start(), calls=%async_computation.14 | async-start | bytes 1310720 | tf_op jit(solution)/shard_map/all_gather | solution.py:578
  88.6 42.7 %collective-permute-start.8 = (bf16[512,1024]{1,0:T(8,128)(2,1)}, bf16[512,1024]{1,0:T(8,128)(2,1)}, u32[]{:S(2)}, u32[]{:S(2)}) collective-permute-start(bf16[512,1024]{1,0:T(8,128)(2,1)} %collective-permute-done.3.refs_4_), channel_id=1, source_target_pairs={{0,2},{2,4},{4,6},{6,0},{1,3},{3,5},{5,7},{7,1},{8,10},{10,12},{12... | collective-permute-start | bytes 3145736 | tf_op jit(solution)/shard_map/ppermute | solution.py:452
  92.7 38.6 %collective-permute-start.9 = (bf16[512,1024]{1,0:T(8,128)(2,1)}, bf16[512,1024]{1,0:T(8,128)(2,1)}, u32[]{:S(2)}, u32[]{:S(2)}) collective-permute-start(bf16[512,1024]{1,0:T(8,128)(2,1)} %collective-permute-done.3.refs_4_), channel_id=1, source_target_pairs={{0,1},{1,0},{2,3},{3,2},{4,5},{5,4},{6,7},{7,6},{8,9},{9,8},{10,11... | collective-permute-start | bytes 3145736 | tf_op jit(solution)/shard_map/ppermute | solution.py:390
  137.3 36.4 %collective-permute-start.12 = (bf16[4,192,512]{2,1,0:T(8,128)(2,1)S(1)}, bf16[4,192,512]{2,1,0:T(8,128)(2,1)}, u32[]{:S(2)}, u32[]{:S(2)}) collective-permute-start(bf16[4,192,512]{2,1,0:T(8,128)(2,1)S(1)} %slice.249), channel_id=1, source_target_pairs={{0,16},{8,24},{16,0},{24,8},{1,17},{9,25},{17,1},{25,9},{2,18},{10... | collective-permute-start | bytes 2359304 | tf_op jit(solution)/shard_map/ppermute | solution.py:390
  140.1 97.8 %all-gather.15.cloned.1.call-start = ((), (), s32[]{:S(2)}) async-start(), calls=%async_computation.20 | async-start | bytes 2359296 | tf_op jit(solution)/shard_map/all_gather | solution.py:616
  177.8 36.4 %collective-permute-start.16 = (bf16[4,4,192,512]{3,2,0,1:T(8,128)(2,1)}, bf16[4,4,192,512]{3,2,0,1:T(8,128)(2,1)}, u32[]{:S(2)}, u32[]{:S(2)}) collective-permute-start(bf16[4,4,192,512]{3,2,0,1:T(8,128)(2,1)} %pad_maximum_fusion.1), channel_id=1, source_target_pairs={{0,1},{1,0},{2,3},{3,2},{4,5},{5,4},{6,7},{7,6},{8,9},{9,8},{10,11... | collective-permute-start | bytes 9437192 | tf_op jit(solution)/shard_map/ppermute | solution.py:390
  214.2 60.3 %collective-permute-start.18 = (bf16[512,1024]{1,0:T(8,128)(2,1)}, bf16[512,1024]{1,0:T(8,128)(2,1)}, u32[]{:S(2)}, u32[]{:S(2)}) collective-permute-start(bf16[512,1024]{1,0:T(8,128)(2,1)} %all-gather.11.cloned.1.call-done), channel_id=1, source_target_pairs={{0,8},{8,0},{16,24},{24,16},{1,9},{9,1},{17,25},{25,17},{2,10},{10... | collective-permute-start | bytes 3145736 | tf_op jit(solution)/shard_map/ppermute | solution.py:390
  215.7 58.8 %collective-permute-start.19 = (bf16[512,1024]{1,0:T(8,128)(2,1)}, bf16[512,1024]{1,0:T(8,128)(2,1)}, u32[]{:S(2)}, u32[]{:S(2)}) collective-permute-start(bf16[512,1024]{1,0:T(8,128)(2,1)} %all-gather.11.cloned.1.call-done), channel_id=1, source_target_pairs={{0,16},{8,24},{16,0},{24,8},{1,17},{9,25},{17,1},{25,9},{2,18},{10... | collective-permute-start | bytes 3145736 | tf_op jit(solution)/shard_map/ppermute | solution.py:390
  220.8 106.6 %all-gather.13.cloned.1.call-start = ((), (), s32[]{:S(2)}) async-start(), calls=%async_computation.15 | async-start | bytes 7077888 | tf_op jit(solution)/shard_map/all_gather | solution.py:456
  236.9 37.6 %collective-permute-start.17 = (bf16[1024,512]{1,0:T(8,128)(2,1)}, bf16[1024,512]{1,0:T(8,128)(2,1)}, u32[]{:S(2)}, u32[]{:S(2)}) collective-permute-start(bf16[1024,512]{1,0:T(8,128)(2,1)} %bitcast.25), channel_id=1, source_target_pairs={{0,24},{8,16},{16,8},{24,0},{1,25},{9,17},{17,9},{25,1},{2,26},{10... | collective-permute-start | bytes 3145736 | tf_op jit(solution)/shard_map/ppermute | solution.py:390
  248.7 252.1 %reduce-scatter.5.cloned.1.call-start = ((), (), s32[]{:S(2)}) async-start(), calls=%async_computation.16 | async-start | bytes 1310720 | tf_op jit(solution)/shard_map/reduce_scatter | solution.py:683
  278.1 44.7 %collective-permute-start.21 = (bf16[512,1024]{1,0:T(8,128)(2,1)S(1)}, bf16[512,1024]{1,0:T(8,128)(2,1)S(1)}, u32[]{:S(2)}, u32[]{:S(2)}) collective-permute-start(bf16[512,1024]{1,0:T(8,128)(2,1)S(1)} %copy-done.77), channel_id=1, source_target_pairs={{0,24},{8,16},{16,8},{24,0},{1,25},{9,17},{17,9},{25,1},{2,26},{10... | collective-permute-start | bytes 3145736 | tf_op jit(solution)/shard_map/ppermute | solution.py:390
  423.2 120.3 %reduce-scatter.7.cloned.1.call-start = ((), (), s32[]{:S(2)}) async-start(), calls=%async_computation.17 | async-start | bytes 2359296 | tf_op jit(solution)/shard_map/reduce_scatter | solution.py:684
  472.4 71.1 %collective-permute-start.32 = (bf16[1024,512]{1,0:T(8,128)(2,1)}, bf16[1024,512]{1,0:T(8,128)(2,1)}, u32[]{:S(2)}, u32[]{:S(2)}) collective-permute-start(bf16[1024,512]{1,0:T(8,128)(2,1)} %convolution_convert_fusion.6), channel_id=1, source_target_pairs={{0,24},{8,16},{16,8},{24,0},{1,25},{9,17},{17,9},{25,1},{2,26},{10... | collective-permute-start | bytes 3145736 | tf_op jit(solution)/shard_map/ppermute | solution.py:390
  494.2 49.3 %all-to-all-start.4 = ((bf16[8,64,512]{2,1,0:T(8,128)(2,1)}), bf16[8,64,512]{2,1,0:T(8,128)(2,1)S(1)}, u32[]{:S(2)}, u32[]{:S(2)}) async-start(bf16[8,64,512]{2,1,0:T(8,128)(2,1)} %get-tuple-element.442), calls=%async_computation.5 | async-start | bytes 1048576 | tf_op jit(solution)/shard_map/all_to_all | solution.py:464
  500.8 42.7 %collective-permute-start.34 = (bf16[4,3,32,1024]{3,2,0,1:T(8,128)(2,1)}, bf16[4,3,32,1024]{3,2,0,1:T(8,128)(2,1)}, u32[]{:S(2)}, u32[]{:S(2)}) collective-permute-start(bf16[4,3,32,1024]{3,2,0,1:T(8,128)(2,1)} %get-tuple-element.249), channel_id=1, source_target_pairs={{0,8},{8,0},{16,24},{24,16},{1,9},{9,1},{17,25},{25,17},{2,10},{10... | collective-permute-start | bytes 2359304 | tf_op jit(solution)/shard_map/ppermute | solution.py:390
  502.0 41.5 %collective-permute-start.35 = (bf16[4,3,32,1024]{3,2,0,1:T(8,128)(2,1)}, bf16[4,3,32,1024]{3,2,0,1:T(8,128)(2,1)}, u32[]{:S(2)}, u32[]{:S(2)}) collective-permute-start(bf16[4,3,32,1024]{3,2,0,1:T(8,128)(2,1)} %get-tuple-element.250), channel_id=1, source_target_pairs={{0,16},{8,24},{16,0},{24,8},{1,17},{9,25},{17,1},{25,9},{2,18},{10... | collective-permute-start | bytes 2359304 | tf_op jit(solution)/shard_map/ppermute | solution.py:390
  503.3 40.2 %collective-permute-start.36 = (bf16[4,3,32,1024]{3,2,0,1:T(8,128)(2,1)}, bf16[4,3,32,1024]{3,2,0,1:T(8,128)(2,1)}, u32[]{:S(2)}, u32[]{:S(2)}) collective-permute-start(bf16[4,3,32,1024]{3,2,0,1:T(8,128)(2,1)} %fusion.33), channel_id=1, source_target_pairs={{0,24},{8,16},{16,8},{24,0},{1,25},{9,17},{17,9},{25,1},{2,26},{10... | collective-permute-start | bytes 2359304 | tf_op jit(solution)/shard_map/ppermute | solution.py:390
  504.3 39.1 %collective-permute-start.33 = (bf16[1,128,1024]{2,1,0:T(8,128)(2,1)}, bf16[1,128,1024]{2,1,0:T(8,128)(2,1)S(1)}, u32[]{:S(2)}, u32[]{:S(2)}) collective-permute-start(bf16[1,128,1024]{2,1,0:T(8,128)(2,1)} %bitcast.456), channel_id=1, source_target_pairs={{0,8},{8,0},{16,24},{24,16},{1,9},{9,1},{17,25},{25,17},{2,10},{10... | collective-permute-start | bytes 786440 | tf_op jit(solution)/shard_map/ppermute | solution.py:390
  543.5 72.7 %all-to-all-start.5 = ((bf16[8,192,512]{2,1,0:T(8,128)(2,1)}), bf16[8,192,512]{2,1,0:T(8,128)(2,1)}, u32[]{:S(2)}, u32[]{:S(2)}) async-start(bf16[8,192,512]{2,1,0:T(8,128)(2,1)} %get-tuple-element.268), calls=%async_computation.8 | async-start | bytes 3145728 | tf_op jit(solution)/shard_map/all_to_all | solution.py:464
  548.3 67.9 %reduce-scatter.9.cloned.1.call-start = ((), (), s32[]{:S(2)}) async-start(), calls=%async_computation.18 | async-start | bytes 1310720 | tf_op jit(solution)/shard_map/reduce_scatter | solution.py:790
  553.4 48.4 %collective-permute-start.40 = (bf16[2,128,1024]{2,1,0:T(8,128)(2,1)S(1)}, bf16[2,128,1024]{2,1,0:T(8,128)(2,1)}, u32[]{:S(2)}, u32[]{:S(2)}) collective-permute-start(bf16[2,128,1024]{2,1,0:T(8,128)(2,1)S(1)} %pad_maximum_fusion.20), channel_id=1, source_target_pairs={{0,16},{8,24},{16,0},{24,8},{1,17},{9,25},{17,1},{25,9},{2,18},{10... | collective-permute-start | bytes 1572872 | tf_op jit(solution)/shard_map/ppermute | solution.py:390
  557.8 46.1 %collective-permute-start.37 = (bf16[3,32,1024]{2,1,0:T(8,128)(2,1)}, bf16[3,32,1024]{2,1,0:T(8,128)(2,1)}, u32[]{:S(2)}, u32[]{:S(2)}) collective-permute-start(bf16[3,32,1024]{2,1,0:T(8,128)(2,1)} %get-tuple-element.454), channel_id=1, source_target_pairs={{0,2},{2,4},{4,6},{6,0},{1,3},{3,5},{5,7},{7,1},{8,10},{10,12},{12... | collective-permute-start | bytes 589832 | tf_op jit(solution)/shard_map/ppermute | solution.py:432
  559.8 56.5 %collective-permute-start.38 = (bf16[3,32,1024]{2,1,0:T(8,128)(2,1)}, bf16[3,32,1024]{2,1,0:T(8,128)(2,1)}, u32[]{:S(2)}, u32[]{:S(2)}) collective-permute-start(bf16[3,32,1024]{2,1,0:T(8,128)(2,1)} %get-tuple-element.453), channel_id=1, source_target_pairs={{0,4},{2,6},{4,0},{6,2},{1,5},{3,7},{5,1},{7,3},{8,12},{10,14},{12... | collective-permute-start | bytes 589832 | tf_op jit(solution)/shard_map/ppermute | solution.py:432
  562.1 54.1 %collective-permute-start.39 = (bf16[3,32,1024]{2,1,0:T(8,128)(2,1)}, bf16[3,32,1024]{2,1,0:T(8,128)(2,1)}, u32[]{:S(2)}, u32[]{:S(2)}) collective-permute-start(bf16[3,32,1024]{2,1,0:T(8,128)(2,1)} %get-tuple-element.452), channel_id=1, source_target_pairs={{0,6},{2,0},{4,2},{6,4},{1,7},{3,1},{5,3},{7,5},{8,14},{10,8},{12,... | collective-permute-start | bytes 589832 | tf_op jit(solution)/shard_map/ppermute | solution.py:432
  616.2 54.1 %all-to-all-start.6 = ((bf16[8,192,512]{2,1,0:T(8,128)(2,1)}), bf16[8,192,512]{2,1,0:T(8,128)(2,1)}, u32[]{:S(2)}, u32[]{:S(2)}) async-start(bf16[8,192,512]{2,1,0:T(8,128)(2,1)} %get-tuple-element.271), calls=%async_computation.9 | async-start | bytes 3145728 | tf_op jit(solution)/shard_map/all_to_all | solution.py:464
  622.5 71.0 %reduce-scatter.11.cloned.1.call-start = ((), (), s32[]{:S(2)}) async-start(), calls=%async_computation.19 | async-start | bytes 1179648 | tf_op jit(solution)/shard_map/reduce_scatter | solution.py:460
  (140 other events, 1659.5 us)
Sparse Core Ops, SparseCore 0:
  45.2 60.5 all-gather.6
  107.4 26.8 all-gather.8
  140.2 26.7 all-gather.10
  177.9 38.9 all-gather.14
  248.8 65.5 all-gather.12
  423.4 27.3 reduce-scatter.4
  453.7 39.5 reduce-scatter.6
  552.2 45.7 reduce-scatter.8
  626.2 38.4 reduce-scatter.10

commit v4 on v3

--- a/solution.py
+++ b/solution.py
@@ -1,4 +1,5 @@
 import functools
+import math
 
 import jax
 import jax.numpy as jnp
@@ -192,7 +193,7 @@
             return carry
 
         lax.fori_loop(0, pl.num_programs(0), finish, 0)
-        slice_grad[...] = slice_sum[...]
+        slice_grad[...] = jnp.transpose(slice_sum[...])
 
 
 def cross_forward_kernel(width, query, pair, mixed, total):
@@ -292,7 +293,7 @@
         ),
         out_shape=(
             jax.ShapeDtypeStruct((group, 3 * HEAD_DIM, tok), low_type),
-            jax.ShapeDtypeStruct((3 * HEAD_DIM, model + LANES), jnp.float32),
+            jax.ShapeDtypeStruct((model + LANES, 3 * HEAD_DIM), jnp.float32),
         ),
         grid_spec=pltpu.PrefetchScalarGridSpec(
             num_scalar_prefetch=2,
@@ -306,7 +307,7 @@
             ],
             out_specs=[
                 pl.BlockSpec((group, 3 * HEAD_DIM, tok), lambda *_: (0, 0, 0)),
-                pl.BlockSpec((3 * HEAD_DIM, model + LANES), lambda *_: (0, 0)),
+                pl.BlockSpec((model + LANES, 3 * HEAD_DIM), lambda *_: (0, 0)),
             ],
             scratch_shapes=[
                 pltpu.VMEM((HEAD_DIM, rows), low_type),
@@ -410,6 +411,14 @@
     return jnp.concatenate([values, swap(values, "rep", offset)], 0)
 
 
+def parts_of(values, axis):
+    own = lax.axis_index("rep")
+    return [
+        lax.dynamic_index_in_dim(values, own ^ d, axis, keepdims=False)
+        for d in range(values.shape[axis])
+    ]
+
+
 def rep_order(pieces):
     own = lax.axis_index("rep")
     count = len(pieces)
@@ -418,6 +427,28 @@
 
 def trade_over_rep(pieces):
     return [pieces[0]] + [swap(pieces[d], "rep", d) for d in range(1, len(pieces))]
+
+
+def far_terms(pieces):
+    if len(pieces) != 4:
+        return [swap(pieces[d], "rep", d) for d in range(len(pieces)) if d & (d - 1)]
+    half = pieces[3].shape[0] // 2
+    return [swap(pieces[3][:half], "rep", 1), swap(pieces[3][half:], "rep", 2)]
+
+
+def near_terms(pieces, found):
+    near = [1 << i for i in range(len(pieces).bit_length() - 1)]
+    if len(pieces) != 4:
+        return [swap(pieces[d], "rep", d) for d in near]
+    half = pieces[3].shape[0] // 2
+    one, two = pieces[1], pieces[2]
+    one = jnp.concatenate([one[:half], sum_of([one[half:], found[1]]).astype(low_type)], 0)
+    two = jnp.concatenate([sum_of([two[:half], found[0]]).astype(low_type), two[half:]], 0)
+    return [swap(one, "rep", 1), swap(two, "rep", 2)]
+
+
+def all_terms(pieces, found, near):
+    return [pieces[0]] + near + (found if len(pieces) != 4 else [])
 
 
 def sum_of(terms):
@@ -464,8 +495,16 @@
     return lax.all_to_all(values, SHARD, split_axis=0, concat_axis=0, tiled=True)
 
 
-def gelu(values):
-    return jax.nn.gelu(values, approximate=False)
+def gelu_and_slope(values):
+    reduced = jnp.abs(values) * (0.5**0.5)
+    inverse = 1.0 / (1.0 + 0.3275911 * reduced)
+    bell = jnp.exp(-(reduced * reduced))
+    tail = 1.061405429 * inverse - 1.453152027
+    tail = tail * inverse + 1.421413741
+    tail = tail * inverse - 0.284496736
+    tail = (tail * inverse + 0.254829592) * inverse * bell * 0.5
+    normal = jnp.where(values >= 0.0, 1.0 - tail, tail)
+    return values * normal, normal + values * (bell * (0.5 / math.pi) ** 0.5)
 
 
 def local(
@@ -623,11 +662,6 @@
     cross_queries = ((product(first_low, full_cross_q) + proj_biases[3]) * score_scale).astype(
         low_type
     )
-    turned = jnp.transpose(stage((head_qkv, cross_queries))[0])
-    turned = turned.reshape(3, heads, HEAD_DIM, model).transpose(1, 0, 2, 3)
-    turned = gather_rows(turned.reshape(-1, model))
-    turned = turned.reshape(group, heads, 3 * HEAD_DIM, model)
-
     cross_low, cross_total = cross_forward(cross_queries, pairs)
     cross_low, wfirst, wsecond = stage((cross_low, wfirst, wsecond))
     wsecond.update({d: swap(wsecond[0], "rep", d) for d in far})
@@ -635,14 +669,18 @@
     second_norm, norm2_back = jax.vjp(norm_rows, second_sum, norm_gains[1], norm_shifts[1])
     second_low = second_norm.astype(low_type)
 
+    turned = jnp.transpose(stage((head_qkv, second_low))[0])
+    turned = turned.reshape(3, heads, HEAD_DIM, model).transpose(1, 0, 2, 3)
+    turned = gather_rows(turned.reshape(-1, model))
+    turned = turned.reshape(group, heads, 3 * HEAD_DIM, model)
+
     second_both = jnp.concatenate([second_low, swap(second_low, "core", 1)], 0)
-    feed_sum, hidden, gelu_back = 0.0, [], []
+    feed_sum, hidden, slopes = 0.0, [], []
     for part in range(reps):
-        active, back = jax.vjp(gelu, product(second_both, wfirst[part]) + bias_cut[part])
+        active, slope = gelu_and_slope(product(second_both, wfirst[part]) + bias_cut[part])
         hidden.append(active.astype(low_type))
-        gelu_back.append(back)
+        slopes.append(slope)
         feed_sum = feed_sum + product(hidden[part], wsecond[part])
-    feed_sum, turned = stage((feed_sum, turned))
     feed_other = swap(feed_sum[tok:].astype(low_type), "core", 1).astype(jnp.float32)
     third_sum = second_norm + (feed_sum[:tok] + feed_other + proj_biases[6])
     result, norm3_back = jax.vjp(norm_rows, third_sum, norm_gains[2], norm_shifts[2])
@@ -656,44 +694,50 @@
         product_left(hidden[part], feed_both).astype(low_type) for part in range(reps)
     ]
     feed_both, second_parts = stage((feed_both, second_parts))
-    second_terms = {0: second_parts[0]}
-    second_terms.update({d: swap(second_parts[d], "rep", d) for d in near})
+    second_found = far_terms(second_parts)
     back_sum, first_parts, bias_parts = 0.0, [], []
     for part in range(reps):
-        pre_grad = gelu_back[part](product_right(feed_both, wsecond[part]))[0].astype(low_type)
+        pre_grad = (product_right(feed_both, wsecond[part]) * slopes[part]).astype(low_type)
         first_parts.append(product_left(second_both, pre_grad).astype(low_type))
         bias_parts.append(column_sums(pre_grad))
         back_sum = back_sum + product_right(pre_grad, wfirst[part])
-    back_sum, second_terms, first_parts = stage((back_sum, second_terms, first_parts))
-    second_terms.update({d: swap(second_parts[d], "rep", d) for d in far})
+        if part == reps // 2 - 1:
+            feed_both, back_sum, second_found = stage((feed_both, back_sum, second_found))
+            second_near = near_terms(second_parts, second_found)
+    back_sum, second_near, first_parts = stage((back_sum, second_near, first_parts))
+    second_sums = sum_of(all_terms(second_parts, second_found, second_near)).astype(low_type)
     back_other = swap(back_sum[tok:].astype(low_type), "core", 1).astype(jnp.float32)
     second_grad, gain_two, shift_two = norm2_back(third_grad + (back_sum[:tok] + back_other))
-    first_terms = {0: first_parts[0]}
-    first_terms.update({d: swap(first_parts[d], "rep", d) for d in near})
+    second_grad, second_sums, first_parts = stage((second_grad, second_sums, first_parts))
+    second_sums = lax.psum_scatter(second_sums, "line", scatter_dimension=0, tiled=True)
+    first_found = far_terms(first_parts)
 
     cross_out_grad = second_grad.astype(low_type)
-    part_cross_out = product_left(cross_low, cross_out_grad).astype(low_type)
-    bias_cross_out = column_sums(cross_out_grad)
     cross_mixed_grad = product_right(cross_out_grad, full_cross_out).astype(low_type)
     cross_q_grad, pair_grad = cross_backward(
         cross_queries, pairs, cross_mixed_grad, cross_low, cross_total
     )
-    cross_q_grad, pair_grad, second_terms = stage((cross_q_grad, pair_grad, second_terms))
-    second_sums = sum_of(second_terms.values()).astype(low_type)
-    second_sums = lax.psum_scatter(second_sums, "line", scatter_dimension=0, tiled=True)
+    cross_q_grad, pair_grad, first_found, turned = stage(
+        (cross_q_grad, pair_grad, first_found, turned)
+    )
+    first_near = near_terms(first_parts, first_found)
     own_pair_grad = lax.psum_scatter(pair_grad, SHARD, scatter_dimension=0, tiled=False)
-    part_cross_q = product_left(first_low, cross_q_grad).astype(low_type)
-    bias_cross_q = column_sums(cross_q_grad)
     first_grad, gain_one, shift_one = norm1_back(
         second_grad + product_right(cross_q_grad, full_cross_q)
     )
     self_out_grad = first_grad.astype(low_type)
-    bias_self_out = column_sums(self_out_grad)
     mixed_grad = product_right(full_out, self_out_grad).astype(low_type)
-    mixed_grad, first_terms = stage((mixed_grad, first_terms))
     mixed_grad = mixed_grad.reshape(group, heads, HEAD_DIM, tok)
+    held = (self_low, first_low, cross_low, self_out_grad, cross_q_grad, cross_out_grad)
+    mixed_grad, held = stage((mixed_grad, held))
+    self_low, first_low, cross_low, self_out_grad, cross_q_grad, cross_out_grad = held
     mixed_grad = [exchange(mixed_grad[:, head]) for head in range(heads)]
     part_self_out = product(self_low, self_out_grad).astype(low_type)
+    part_cross_q = product_left(first_low, cross_q_grad).astype(low_type)
+    part_cross_out = product_left(cross_low, cross_out_grad).astype(low_type)
+    bias_self_out = column_sums(self_out_grad)
+    bias_cross_q = column_sums(cross_q_grad)
+    bias_cross_out = column_sums(cross_out_grad)
 
     square = jnp.stack([part_self_out, part_cross_q, part_cross_out], 0)
     square = square.reshape(3, line, 2, reps, weight_rows // reps, model)
@@ -735,11 +779,12 @@
     small = hop(small, 1)
     square = square_own.astype(jnp.float32) + square_other.astype(jnp.float32)
     square = square.astype(low_type).transpose(2, 1, 0, 3, 4)
-    square = rep_order([square[r] for r in range(reps)])
-    mixed_grad[0], square, small, second_sums = stage(
-        (mixed_grad[0], square, small, second_sums)
-    )
-    first_terms.update({d: swap(first_parts[d], "rep", d) for d in far})
+    square = parts_of(square, 0)
+    held = (square, small, second_sums, first_near)
+    mixed_grad[0], held = stage((mixed_grad[0], held))
+    square, small, second_sums, first_near = held
+    first_sums = sum_of(all_terms(first_parts, first_found, first_near)).astype(low_type)
+    first_sums = lax.psum_scatter(first_sums, "line", scatter_dimension=0, tiled=True)
     square_terms = trade_over_rep(square)
     wide = 2 * line * unit
     second_sums = second_sums.reshape(unit, model // wide, wide).transpose(1, 0, 2)
@@ -758,8 +803,7 @@
     def trade_slices(values):
         sums = jnp.broadcast_to(values[model : model + 1], (group, 1, values.shape[1]))
         values = values[:model].reshape(group, reps, part_rows, -1)
-        values = [with_sums(values[:, r], sums) for r in range(reps)]
-        return trade_over_rep(rep_order(values))
+        return trade_over_rep([with_sums(part, sums) for part in parts_of(values, 1)])
 
     def exchange_slices(terms):
         return exchange(with_sums(*split_sums(sum_of(terms))))
@@ -783,57 +827,54 @@
             self_totals[head],
         )
         if head == 0:
-            held = (part, slice_part, turn, first_terms, second_sums, square_terms)
+            small = hop(small, 1)
+            held = (part, slice_part, turn, first_sums, second_sums, square_terms, small)
             held, mixed_grad, own_pair_grad = stage((held, mixed_grad, own_pair_grad))
-            part, slice_part, turn, first_terms, second_sums, square_terms = held
-            first_sums = sum_of(first_terms.values()).astype(low_type)
-            first_sums = lax.psum_scatter(first_sums, "line", scatter_dimension=0, tiled=True)
+            part, slice_part, turn, first_sums, second_sums, square_terms, small = held
+            own_pair_grad = join_columns(own_pair_grad)
+            enc_grad = scatter_rows(product_right(own_pair_grad, head_ckv).astype(low_type))
             for offset in near[1:]:
                 second_sums = double(second_sums, offset)
-            small = hop(small, 1)
-            own_pair_grad = join_columns(own_pair_grad)
-            enc_grad = scatter_rows(product_right(own_pair_grad, head_ckv).astype(low_type))
+            first_sums = first_sums.reshape(2, weight_rows, line * unit).transpose(1, 0, 2)
+            first_sums = double(first_sums.reshape(1, -1, wide), near[0])
             pair_sums = jnp.sum(own_pair_grad.astype(jnp.float32), 0)
             pair_sums = jnp.broadcast_to(pair_sums, (LANES, 2 * width))
             pair_slices = jnp.concatenate([product_left(all_states, own_pair_grad), pair_sums], 0)
             square_terms = trade_over_line(sum_of(square_terms).astype(low_type))
         if head == heads - 1:
-            held = (part, slice_part, square_terms, first_sums, second_sums, small)
+            held = (part, slice_part, first_sums, second_sums, square_terms, enc_grad)
             held, parts, slice_parts = stage((held, parts, slice_parts))
-            part, slice_part, square_terms, first_sums, second_sums, small = held
+            part, slice_part, first_sums, second_sums, square_terms, enc_grad = held
         parts.append(exchange(part))
-        slice_parts.append(jnp.transpose(slice_part))
+        slice_parts.append(slice_part)
 
     slice_parts = trade_slices(
         jnp.concatenate([slice_parts[0], pair_slices] + slice_parts[1:], 1)
     )
-    first_sums = first_sums.reshape(2, weight_rows, line * unit).transpose(1, 0, 2)
-    first_sums = double(first_sums.reshape(1, -1, wide), near[0])
+    for offset in near[1:]:
+        first_sums = double(first_sums, offset)
     square = double(sum_of(square_terms).astype(low_type)[None], near[0])
     parts, slice_parts, first_sums, square = stage((parts, slice_parts, first_sums, square))
 
     slice_parts = exchange_slices(slice_parts)
     for offset in near[1:]:
         square = double(square, offset)
-        first_sums = double(first_sums, offset)
     small = hop(small, 1)
     second_sums = jnp.stack(rep_order([second_sums[d] for d in range(reps)]), 0)
     second_sums = second_sums.reshape(reps, model // wide, unit, wide)
     grad_fc2 = second_sums.transpose(0, 2, 1, 3).reshape(-1, model).astype(jnp.float32)
-    input_grad = first_grad
-    for head in range(heads):
-        rows = turned[:, head].reshape(group * 3 * HEAD_DIM, model)
-        input_grad = input_grad + product_left(parts[head].reshape(rows.shape[0], tok), rows)
-    slice_parts, first_sums, square, input_grad, grad_fc2, small, enc_grad = stage(
-        (slice_parts, first_sums, square, input_grad, grad_fc2, small, enc_grad)
-    )
-
     first_sums = jnp.stack(rep_order([first_sums[d] for d in range(reps)]), 0)
     first_sums = first_sums.reshape(reps, weight_rows, 2, line, unit)
     first_own = lax.dynamic_index_in_dim(first_sums, core, 2, keepdims=False)
     first_other = lax.dynamic_index_in_dim(first_sums, 1 - core, 2, keepdims=False)
     first_other = swap(first_other.reshape(-1, line * unit), "core", 1)
     first_other = first_other.reshape(first_own.shape)
+    input_grad = first_grad
+    rows = turned.reshape(-1, model)
+    input_grad = input_grad + product_left(jnp.stack(parts, 1).reshape(rows.shape[0], tok), rows)
+    held = (first_own, first_other, square, input_grad, grad_fc2, small)
+    slice_parts, held = stage((slice_parts, held))
+    first_own, first_other, square, input_grad, grad_fc2, small = held
 
     slice_parts = join_slices(slice_parts)
     small = hop(small, len(hops))

time: 750 us -> 722 us (0.963)
  local copies, waits for them, and re-layouts: 106 us -> 87.8 us
  Pallas kernels: 130 us -> 144 us
  waiting for transfers between devices: 200 us -> 189 us
  starting transfers between devices: 107 us -> 98.6 us
    dot_general x12, matrix products: 51.8 us -> 37.9 us  [product(): return jnp.dot(former, latter, preferred_element_type=jnp.float32)]
    pallas_call x1, Pallas kernels: 10.9 us -> 23.4 us  [cross_forward(): pl.pallas_call(functools.partial(cross_forward_kernel, width), out_shape=...]
    reduce_scatter x1, starting transfers between devices: 11.1 us -> 0.45 us  [local(): lax.psum_scatter(second_sums, 'line', scatter_dimension=0, tiled=True)]
    ppermute x50 -> x52, waiting for transfers between devices: 90.1 us -> 81.1 us  [swap(): return lax.ppermute(values, axis, [(i, i ^ offset) for i in range(size)])]
    select_n x9 -> x5, other arithmetic: 7.96 us -> 0.37 us  [rep_order(): lax.select_n(own, *[pieces[d ^ i] for i in range(count)])]
    unnamed x214 -> x212, local copies, waits for them, and re-layouts: 39.7 us -> 34.9 us
    dot_general x14 -> x13, matrix products: 32.4 us -> 36.8 us  [product_left(): lax.dot_general(former, latter, (((0,), (0,)), ((), ())), preferred_eleme...]
    ppermute x50 -> x52, starting transfers between devices: 46.7 us -> 46.6 us  [swap(): return lax.ppermute(values, axis, [(i, i ^ offset) for i in range(size)])]
  transfers between devices with their start and end apart: 73 -> 75, of which waited for: 27 -> 26; matrix products, arithmetic and copies ran while one was open for 30% -> 31% of each run, Pallas kernels for 18% -> 20%
where the time goes in v4:
time: 722 us; the launch traced here: 711 us
  waiting for transfers between devices  189 us (26%)
  Pallas kernels  144 us (20%)
  matrix products  112 us (16%)
  starting transfers between devices  98.6 us (14%)
  local copies, waits for them, and re-layouts  87.8 us (12%)
  other arithmetic  62.9 us (9%)
  between operations  16.4 us (2%)
    ppermute x52, waiting for transfers between devices, swap(): return lax.ppermute(values, axis, [(i, i ^ offset) for i in range(size)])  81.1 us
    ppermute x3, waiting for transfers between devices, shift(): lax.ppermute(values, 'line', [(i, (i + 1) % line) for i in range(line)])  62.7 us
    pallas_call x2, Pallas kernels, self_backward(): pl.pallas_call(functools.partial(self_backward_kernel, tok, width, group...  62.5 us
    ppermute x52, starting transfers between devices, swap(): return lax.ppermute(values, axis, [(i, i ^ offset) for i in range(size)])  46.6 us
    pallas_call x2, Pallas kernels, self_forward(): pl.pallas_call(functools.partial(self_forward_kernel, tok, width, group /...  44.2 us
    dot_general x12, matrix products, product(): return jnp.dot(former, latter, preferred_element_type=jnp.float32)  37.9 us
    all_to_all x8, starting transfers between devices, exchange(): lax.all_to_all(values, SHARD, split_axis=0, concat_axis=0, tiled=True)  37.8 us
    dot_general x12, matrix products, product_right(): lax.dot_general(former, latter, (((1,), (1,)), ((), ())), preferred_eleme...  37.4 us
  transfers between devices with their start and end apart: 75, of which 26 were waited for; matrix products, arithmetic and copies ran while one was open for 31% of the time, Pallas kernels for 20%

profile of v4, /device:TPU:0, one launch (start us, length us, event | category | flops | bytes accessed | tf_op | source)
XLA Modules:
  0.0 710.8 jit_solution(17453767050355054680)
XLA Ops:
  33.8 8.9 %all-to-all-done = bf16[8,32,640]{2,1,0:T(8,128)(2,1)S(1)} async-done(((bf16[8,32,640]{2,1,0:T(8,128)(2,1)}), bf16[8,32,640]{2,1,0:T(8,128)(2,1)S(1)}, u32[]{:S(2)}, u32[]{:S(2)}) %all-to-all-start) | async-done | bytes 327712 | tf_op jit(solution)/shard_map/all_to_all | solution.py:495
  48.8 7.0 collective-permute-done.4
  55.9 7.8 %collective-permute-done.5 = bf16[8,32,640]{2,1,0:T(8,128)(2,1)S(1)} collective-permute-done((bf16[8,32,640]{2,1,0:T(8,128)(2,1)S(1)}, bf16[8,32,640]{2,1,0:T(8,128)(2,1)S(1)}, u32[]{:S(2)}, u32[]{:S(2)}) %collective-permute-start.5) | collective-permute-done | bytes 327712 | tf_op jit(solution)/shard_map/ppermute | solution.py:391
  63.6 24.9 %collective-permute-done.3.refs_4_ = bf16[512,1024]{1,0:T(8,128)(2,1)} collective-permute-done((bf16[512,1024]{1,0:T(8,128)(2,1)S(1)}, bf16[512,1024]{1,0:T(8,128)(2,1)}, u32[]{:S(2)}, u32[]{:S(2)}) %collective-permute-start.3) | collective-permute-done | bytes 1048608 | tf_op jit(solution)/shard_map/ppermute | solution.py:483
  93.5 37.8 %collective-permute-done.8.refs_6_ = bf16[512,1024]{1,0:T(8,128)(2,1)} collective-permute-done((bf16[512,1024]{1,0:T(8,128)(2,1)}, bf16[512,1024]{1,0:T(8,128)(2,1)}, u32[]{:S(2)}, u32[]{:S(2)}) %collective-permute-start.8) | collective-permute-done | bytes 1048608 | tf_op jit(solution)/shard_map/ppermute | solution.py:483
  143.7 25.9 %self_forward.2 = (bf16[4096,384]{1,0:T(8,128)(2,1)}, bf16[8,64,512]{2,1,0:T(8,128)(2,1)}, f32[8,1,512]{2,1,0:T(1,128)S(1)}) custom-call(s32[8]{0:T(128)S(1)} %select_reduce_fusion.1.owner, s32[8]{0:T(128)S(1)} %select_reduce_fusion.slot_of, bf16[512,1024]{1,0:T(8,128)(2,1)} %refs_0_.2, bf16[512,1024]{1,0:T(8,128)(2,1)} %copy-done.21, ...), custom_call_target="tpu_custom_call" | custom-call | flops 1048576 | bytes 65536 | tf_op jit(solution)/shard_map/self_forward/pallas_call | solution.py:266
  186.0 18.4 %self_forward.3 = (bf16[8,64,512]{2,1,0:T(8,128)(2,1)}, f32[8,1,512]{2,1,0:T(1,128)S(1)}) custom-call(s32[8]{0:T(128)S(1)} %select_reduce_fusion.1.owner, s32[8]{0:T(128)S(1)} %select_reduce_fusion.slot_of, bf16[4096,384]{1,0:T(8,128)(2,1)} %get-tuple-element.196.refs_0_.refs_8_), custom_call_target="tpu_custom_call" | custom-call | flops 1048576 | bytes 65536 | tf_op jit(solution)/shard_map/self_forward/pallas_call | solution.py:266
  206.8 7.4 %all-to-all-done.1 = bf16[8,64,512]{2,1,0:T(8,128)(2,1)S(1)} async-done(((bf16[8,64,512]{2,1,0:T(8,128)(2,1)}), bf16[8,64,512]{2,1,0:T(8,128)(2,1)S(1)}, u32[]{:S(2)}, u32[]{:S(2)}) %all-to-all-start.1) | async-done | bytes 524320 | tf_op jit(solution)/shard_map/all_to_all | solution.py:495
  248.6 23.4 %cross_forward.1 = (bf16[512,1024]{1,0:T(8,128)(2,1)S(1)}, f32[8,8,512]{2,1,0:T(8,128)S(1)}) custom-call(bf16[512,1024]{1,0:T(8,128)(2,1)S(1)} %multiply_convert_fusion.8.query, bf16[8,2,512,128]{3,2,1,0:T(8,128)(2,1)S(1)} %bitcast.357), custom_call_target="tpu_custom_call" | custom-call | flops 1048576 | bytes 65536 | tf_op jit(solution)/shard_map/cross_forward/pallas_call | solution.py:351
  277.1 6.2 multiply_convert_fusion.7
  284.9 4.6 multiply_convert_fusion.5
  292.4 5.9 multiply_convert_fusion.6
  301.2 5.8 multiply_convert_fusion.4
  372.5 4.5 add_add_fusion
  376.9 5.6 collective-permute-done.26
  402.8 13.9 %cross_backward.1 = (bf16[512,1024]{1,0:T(8,128)(2,1)S(1)}, bf16[8,2,512,128]{3,2,1,0:T(8,128)(2,1)}) custom-call(bf16[512,1024]{1,0:T(8,128)(2,1)S(1)} %copy-done.5, bf16[8,2,512,128]{3,2,1,0:T(8,128)(2,1)S(1)} %bitcast.358, bf16[512,1024]{1,0:T(8,128)(2,1)S(1)} %convolution_convert_fusion.5.mixed_grad, bf16[512,1024]{1,0:T(8,128)(2,1)S(1)} %copy-done.9, ...), custom_call_target="tpu_custom_call" | custom-call | flops 1048576 | bytes 65536 | tf_op jit(solution)/shard_map/cross_backward/pallas_call | solution.py:373
  417.7 5.1 multiply_reduce_fusion.1
  447.0 5.0 all-to-all-start.3
  460.9 4.5 fusion
  466.9 9.3 %all-to-all-done.3.refs_9_ = bf16[8,64,512]{2,1,0:T(8,128)(2,1)S(1)} async-done(((bf16[8,64,512]{2,1,0:T(8,128)(2,1)}), bf16[8,64,512]{2,1,0:T(8,128)(2,1)S(1)}, u32[]{:S(2)}, u32[]{:S(2)}) %all-to-all-start.3) | async-done | bytes 524320 | tf_op jit(solution)/shard_map/all_to_all | solution.py:495
  476.2 4.4 collective-permute-done.33
  486.8 4.9 all-to-all-start.4
  497.2 31.1 %self_backward.2 = (bf16[8,192,512]{2,1,0:T(8,128)(2,1)}, f32[1152,192]{1,0:T(8,128)}) custom-call(s32[8]{0:T(128)S(1)} %copy-done.12, s32[8]{0:T(128)S(1)} %copy-done.14, bf16[512,1024]{1,0:T(8,128)(2,1)} %refs_0_.2, bf16[512,1024]{1,0:T(8,128)(2,1)} %copy-done.21, bf16[512,1024]{1,0:T(8,128)(2,1)} %copy-done.20, ...), custom_call_target="tpu_custom_call" | custom-call | flops 1048576 | bytes 65536 | tf_op jit(solution)/shard_map/self_backward/pallas_call | solution.py:290
  528.4 7.4 %collective-permute-done.39 = f32[14,1024]{1,0:T(8,128)S(1)} collective-permute-done((f32[14,1024]{1,0:T(8,128)S(1)}, f32[14,1024]{1,0:T(8,128)S(1)}, u32[]{:S(2)}, u32[]{:S(2)}) %collective-permute-start.39) | collective-permute-done | bytes 57376 | tf_op jit(solution)/shard_map/ppermute | solution.py:391
  536.7 4.9 all-to-all-start.5
  554.4 31.4 %self_backward.3 = (bf16[8,192,512]{2,1,0:T(8,128)(2,1)}, f32[1152,192]{1,0:T(8,128)}) custom-call(s32[8]{0:T(128)S(1)} %copy-done.12, s32[8]{0:T(128)S(1)} %copy-done.14, bf16[512,1024]{1,0:T(8,128)(2,1)} %refs_0_.2, bf16[512,1024]{1,0:T(8,128)(2,1)} %copy-done.21, bf16[512,1024]{1,0:T(8,128)(2,1)} %copy-done.20, ...), custom_call_target="tpu_custom_call" | custom-call | flops 1048576 | bytes 65536 | tf_op jit(solution)/shard_map/self_backward/pallas_call | solution.py:290
  587.0 15.4 %collective-permute-done.43 = bf16[3,32,1024]{2,1,0:T(8,128)(2,1)S(1)} collective-permute-done((bf16[3,32,1024]{2,1,0:T(8,128)(2,1)S(1)}, bf16[3,32,1024]{2,1,0:T(8,128)(2,1)S(1)}, u32[]{:S(2)}, u32[]{:S(2)}) %collective-permute-start.43) | collective-permute-done | bytes 196640 | tf_op jit(solution)/shard_map/ppermute | solution.py:463
  603.1 6.3 all-to-all-start.6
  625.1 18.3 %collective-permute-done.49 = bf16[1,3,32,1024]{3,2,1,0:T(8,128)(2,1)S(1)} collective-permute-done((bf16[1,3,32,1024]{3,2,1,0:T(8,128)(2,1)S(1)}, bf16[1,3,32,1024]{3,2,1,0:T(8,128)(2,1)S(1)}, u32[]{:S(2)}, u32[]{:S(2)}) %collective-permute-start.49) | collective-permute-done | bytes 196640 | tf_op jit(solution)/shard_map/ppermute | solution.py:391
  643.5 7.7 %collective-permute-done.48 = bf16[2,128,1024]{2,1,0:T(8,128)(2,1)S(1)} collective-permute-done((bf16[2,128,1024]{2,1,0:T(8,128)(2,1)S(1)}, bf16[2,128,1024]{2,1,0:T(8,128)(2,1)S(1)}, u32[]{:S(2)}, u32[]{:S(2)}) %collective-permute-start.48) | collective-permute-done | bytes 524320 | tf_op jit(solution)/shard_map/ppermute | solution.py:391
  654.6 4.9 all-to-all-start.7
  662.8 8.5 %bitcast_add_fusion = f32[512,1024]{1,0:T(8,128)} fusion(f32[512,1024]{1,0:T(8,128)S(1)} %copy-done.24, bf16[8,2,192,1024]{3,2,1,0:T(8,128)(2,1)} %bitcast.468, f32[512]{0:T(512)S(1)} %copy-done.78, bf16[8,1,192,512]{3,2,0,1:T(8,128)(2,1)} %bitcast.113, bf16[8,1,192,512]{3,2,0,1:T(8,128)(2,1)} %bitcast.112), kind=kOutput, calls=%fused_computation.38 | convolution fusion | flops 3223846912 | bytes 13633536 | tf_op jit(solution)/shard_map/dot_general | solution.py:33
  (571 shorter events, 317.5 us)
Async XLA Ops:
  7.2 35.5 %collective-permute-start = (bf16[512,1024]{1,0:T(8,128)(2,1)}, bf16[512,1024]{1,0:T(8,128)(2,1)S(1)}, u32[]{:S(2)}, u32[]{:S(2)}) collective-permute-start(bf16[512,1024]{1,0:T(8,128)(2,1)} %refs_0_.2), channel_id=1, source_target_pairs={{0,2},{2,4},{4,6},{6,0},{1,3},{3,5},{5,7},{7,1},{8,10},{10,12},{12... | collective-permute-start | bytes 3145736 | tf_op jit(solution)/shard_map/ppermute | solution.py:483
  22.5 108.9 %all-gather.7.cloned.1.call-start = ((), (), s32[]{:S(2)}) async-start(), calls=%async_computation.12 | async-start | bytes 2293760 | tf_op jit(solution)/shard_map/all_gather | solution.py:597
  45.1 89.2 %all-gather.9.cloned.1.call-start = ((), (), s32[]{:S(2)}) async-start(), calls=%async_computation.13 | async-start | bytes 1179648 | tf_op jit(solution)/shard_map/all_gather | solution.py:487
  45.1 43.4 %collective-permute-start.3 = (bf16[512,1024]{1,0:T(8,128)(2,1)S(1)}, bf16[512,1024]{1,0:T(8,128)(2,1)}, u32[]{:S(2)}, u32[]{:S(2)}) collective-permute-start(bf16[512,1024]{1,0:T(8,128)(2,1)S(1)} %collective-permute-done.refs_2_), channel_id=1, source_target_pairs={{0,2},{2,4},{4,6},{6,0},{1,3},{3,5},{5,7},{7,1},{8,10},{10,12},{12... | collective-permute-start | bytes 3145736 | tf_op jit(solution)/shard_map/ppermute | solution.py:483
  45.2 43.3 %collective-permute-start.7 = (bf16[512,1024]{1,0:T(8,128)(2,1)S(1)}, bf16[512,1024]{1,0:T(8,128)(2,1)}, u32[]{:S(2)}, u32[]{:S(2)}) collective-permute-start(bf16[512,1024]{1,0:T(8,128)(2,1)S(1)} %collective-permute-done.refs_2_), channel_id=1, source_target_pairs={{0,1},{1,0},{2,3},{3,2},{4,5},{5,4},{6,7},{7,6},{8,9},{9,8},{10,11... | collective-permute-start | bytes 3145736 | tf_op jit(solution)/shard_map/ppermute | solution.py:391
  88.5 118.3 %all-gather.11.cloned.1.call-start = ((), (), s32[]{:S(2)}) async-start(), calls=%async_computation.14 | async-start | bytes 1310720 | tf_op jit(solution)/shard_map/all_gather | solution.py:617
  88.6 42.7 %collective-permute-start.8 = (bf16[512,1024]{1,0:T(8,128)(2,1)}, bf16[512,1024]{1,0:T(8,128)(2,1)}, u32[]{:S(2)}, u32[]{:S(2)}) collective-permute-start(bf16[512,1024]{1,0:T(8,128)(2,1)} %collective-permute-done.3.refs_4_), channel_id=1, source_target_pairs={{0,2},{2,4},{4,6},{6,0},{1,3},{3,5},{5,7},{7,1},{8,10},{10,12},{12... | collective-permute-start | bytes 3145736 | tf_op jit(solution)/shard_map/ppermute | solution.py:483
  92.7 38.6 %collective-permute-start.9 = (bf16[512,1024]{1,0:T(8,128)(2,1)}, bf16[512,1024]{1,0:T(8,128)(2,1)}, u32[]{:S(2)}, u32[]{:S(2)}) collective-permute-start(bf16[512,1024]{1,0:T(8,128)(2,1)} %collective-permute-done.3.refs_4_), channel_id=1, source_target_pairs={{0,1},{1,0},{2,3},{3,2},{4,5},{5,4},{6,7},{7,6},{8,9},{9,8},{10,11... | collective-permute-start | bytes 3145736 | tf_op jit(solution)/shard_map/ppermute | solution.py:391
  137.3 36.4 %collective-permute-start.12 = (bf16[4,192,512]{2,1,0:T(8,128)(2,1)S(1)}, bf16[4,192,512]{2,1,0:T(8,128)(2,1)}, u32[]{:S(2)}, u32[]{:S(2)}) collective-permute-start(bf16[4,192,512]{2,1,0:T(8,128)(2,1)S(1)} %slice.251), channel_id=1, source_target_pairs={{0,16},{8,24},{16,0},{24,8},{1,17},{9,25},{17,1},{25,9},{2,18},{10... | collective-permute-start | bytes 2359304 | tf_op jit(solution)/shard_map/ppermute | solution.py:391
  140.1 100.5 %all-gather.15.cloned.1.call-start = ((), (), s32[]{:S(2)}) async-start(), calls=%async_computation.20 | async-start | bytes 2359296 | tf_op jit(solution)/shard_map/all_gather | solution.py:655
  177.8 36.4 %collective-permute-start.16 = (bf16[4,4,192,512]{3,2,0,1:T(8,128)(2,1)}, bf16[4,4,192,512]{3,2,0,1:T(8,128)(2,1)}, u32[]{:S(2)}, u32[]{:S(2)}) collective-permute-start(bf16[4,4,192,512]{3,2,0,1:T(8,128)(2,1)} %pad_maximum_fusion.1), channel_id=1, source_target_pairs={{0,1},{1,0},{2,3},{3,2},{4,5},{5,4},{6,7},{7,6},{8,9},{9,8},{10,11... | collective-permute-start | bytes 9437192 | tf_op jit(solution)/shard_map/ppermute | solution.py:391
  214.2 57.8 %collective-permute-start.18 = (bf16[512,1024]{1,0:T(8,128)(2,1)}, bf16[512,1024]{1,0:T(8,128)(2,1)}, u32[]{:S(2)}, u32[]{:S(2)}) collective-permute-start(bf16[512,1024]{1,0:T(8,128)(2,1)} %all-gather.11.cloned.1.call-done), channel_id=1, source_target_pairs={{0,8},{8,0},{16,24},{24,16},{1,9},{9,1},{17,25},{25,17},{2,10},{10... | collective-permute-start | bytes 3145736 | tf_op jit(solution)/shard_map/ppermute | solution.py:391
  215.7 56.3 %collective-permute-start.19 = (bf16[512,1024]{1,0:T(8,128)(2,1)}, bf16[512,1024]{1,0:T(8,128)(2,1)}, u32[]{:S(2)}, u32[]{:S(2)}) collective-permute-start(bf16[512,1024]{1,0:T(8,128)(2,1)} %all-gather.11.cloned.1.call-done), channel_id=1, source_target_pairs={{0,16},{8,24},{16,0},{24,8},{1,17},{9,25},{17,1},{25,9},{2,18},{10... | collective-permute-start | bytes 3145736 | tf_op jit(solution)/shard_map/ppermute | solution.py:391
  220.9 196.8 %all-gather.13.cloned.1.call-start = ((), (), s32[]{:S(2)}) async-start(), calls=%async_computation.15 | async-start | bytes 7077888 | tf_op jit(solution)/shard_map/all_gather | solution.py:487
  235.6 36.4 %collective-permute-start.17 = (bf16[1024,512]{1,0:T(8,128)(2,1)}, bf16[1024,512]{1,0:T(8,128)(2,1)}, u32[]{:S(2)}, u32[]{:S(2)}) collective-permute-start(bf16[1024,512]{1,0:T(8,128)(2,1)} %bitcast.25), channel_id=1, source_target_pairs={{0,24},{8,16},{16,8},{24,0},{1,25},{9,17},{17,9},{25,1},{2,26},{10... | collective-permute-start | bytes 3145736 | tf_op jit(solution)/shard_map/ppermute | solution.py:391
  323.1 143.8 %reduce-scatter.5.cloned.1.call-start = ((), (), s32[]{:S(2)}) async-start(), calls=%async_computation.16 | async-start | bytes 1310720 | tf_op jit(solution)/shard_map/reduce_scatter | solution.py:712
  399.3 137.4 %reduce-scatter.9.cloned.1.call-start = ((), (), s32[]{:S(2)}) async-start(), calls=%async_computation.18 | async-start | bytes 2359296 | tf_op jit(solution)/shard_map/reduce_scatter | solution.py:724
  452.0 84.8 %reduce-scatter.7.cloned.1.call-start = ((), (), s32[]{:S(2)}) async-start(), calls=%async_computation.17 | async-start | bytes 1310720 | tf_op jit(solution)/shard_map/reduce_scatter | solution.py:787
  486.8 49.8 %all-to-all-start.4 = ((bf16[8,64,512]{2,1,0:T(8,128)(2,1)}), bf16[8,64,512]{2,1,0:T(8,128)(2,1)S(1)}, u32[]{:S(2)}, u32[]{:S(2)}) async-start(bf16[8,64,512]{2,1,0:T(8,128)(2,1)} %get-tuple-element.435), calls=%async_computation.6 | async-start | bytes 1048576 | tf_op jit(solution)/shard_map/all_to_all | solution.py:495
  491.7 45.0 %collective-permute-start.36 = (bf16[4,3,32,1024]{3,2,0,1:T(8,128)(2,1)}, bf16[4,3,32,1024]{3,2,0,1:T(8,128)(2,1)S(1)}, u32[]{:S(2)}, u32[]{:S(2)}) collective-permute-start(bf16[4,3,32,1024]{3,2,0,1:T(8,128)(2,1)} %get-tuple-element.269), channel_id=1, source_target_pairs={{0,8},{8,0},{16,24},{24,16},{1,9},{9,1},{17,25},{25,17},{2,10},{10... | collective-permute-start | bytes 2359304 | tf_op jit(solution)/shard_map/ppermute | solution.py:391
  492.7 44.0 %collective-permute-start.37 = (bf16[4,3,32,1024]{3,2,0,1:T(8,128)(2,1)}, bf16[4,3,32,1024]{3,2,0,1:T(8,128)(2,1)}, u32[]{:S(2)}, u32[]{:S(2)}) collective-permute-start(bf16[4,3,32,1024]{3,2,0,1:T(8,128)(2,1)} %get-tuple-element.270), channel_id=1, source_target_pairs={{0,16},{8,24},{16,0},{24,8},{1,17},{9,25},{17,1},{25,9},{2,18},{10... | collective-permute-start | bytes 2359304 | tf_op jit(solution)/shard_map/ppermute | solution.py:391
  493.7 42.9 %collective-permute-start.38 = (bf16[4,3,32,1024]{3,2,0,1:T(8,128)(2,1)}, bf16[4,3,32,1024]{3,2,0,1:T(8,128)(2,1)}, u32[]{:S(2)}, u32[]{:S(2)}) collective-permute-start(bf16[4,3,32,1024]{3,2,0,1:T(8,128)(2,1)} %get-tuple-element.271), channel_id=1, source_target_pairs={{0,24},{8,16},{16,8},{24,0},{1,25},{9,17},{17,9},{25,1},{2,26},{10... | collective-permute-start | bytes 2359304 | tf_op jit(solution)/shard_map/ppermute | solution.py:391
  495.2 40.6 %collective-permute-start.35 = (bf16[1,128,1024]{2,1,0:T(8,128)(2,1)S(1)}, bf16[1,128,1024]{2,1,0:T(8,128)(2,1)S(1)}, u32[]{:S(2)}, u32[]{:S(2)}) collective-permute-start(bf16[1,128,1024]{2,1,0:T(8,128)(2,1)S(1)} %bitcast.419), channel_id=1, source_target_pairs={{0,8},{8,0},{16,24},{24,16},{1,9},{9,1},{17,25},{25,17},{2,10},{10... | collective-permute-start | bytes 786440 | tf_op jit(solution)/shard_map/ppermute | solution.py:391
  496.2 39.6 %collective-permute-start.39 = (f32[14,1024]{1,0:T(8,128)S(1)}, f32[14,1024]{1,0:T(8,128)S(1)}, u32[]{:S(2)}, u32[]{:S(2)}) collective-permute-start(f32[14,1024]{1,0:T(8,128)S(1)} %add.522), channel_id=1, source_target_pairs={{0,8},{8,0},{16,24},{24,16},{1,9},{9,1},{17,25},{25,17},{2,10},{10... | collective-permute-start | bytes 172040 | tf_op jit(solution)/shard_map/ppermute | solution.py:391
  536.7 66.3 %all-to-all-start.5 = ((bf16[8,192,512]{2,1,0:T(8,128)(2,1)}), bf16[8,192,512]{2,1,0:T(8,128)(2,1)}, u32[]{:S(2)}, u32[]{:S(2)}) async-start(bf16[8,192,512]{2,1,0:T(8,128)(2,1)} %get-tuple-element.286), calls=%async_computation.9 | async-start | bytes 3145728 | tf_op jit(solution)/shard_map/all_to_all | solution.py:495
  541.6 61.5 %reduce-scatter.11.cloned.1.call-start = ((), (), s32[]{:S(2)}) async-start(), calls=%async_computation.19 | async-start | bytes 1179648 | tf_op jit(solution)/shard_map/reduce_scatter | solution.py:491
  544.0 41.7 %collective-permute-start.40 = (bf16[1,128,1024]{2,1,0:T(8,128)(2,1)S(1)}, bf16[1,128,1024]{2,1,0:T(8,128)(2,1)S(1)}, u32[]{:S(2)}, u32[]{:S(2)}) collective-permute-start(bf16[1,128,1024]{2,1,0:T(8,128)(2,1)S(1)} %reshape.807), channel_id=1, source_target_pairs={{0,8},{8,0},{16,24},{24,16},{1,9},{9,1},{17,25},{25,17},{2,10},{10... | collective-permute-start | bytes 786440 | tf_op jit(solution)/shard_map/ppermute | solution.py:391
  545.1 40.7 %collective-permute-start.41 = (bf16[2,128,1024]{2,1,0:T(8,128)(2,1)}, bf16[2,128,1024]{2,1,0:T(8,128)(2,1)S(1)}, u32[]{:S(2)}, u32[]{:S(2)}) collective-permute-start(bf16[2,128,1024]{2,1,0:T(8,128)(2,1)} %pad_maximum_fusion.25), channel_id=1, source_target_pairs={{0,16},{8,24},{16,0},{24,8},{1,17},{9,25},{17,1},{25,9},{2,18},{10... | collective-permute-start | bytes 1572872 | tf_op jit(solution)/shard_map/ppermute | solution.py:391
  548.5 38.5 %collective-permute-start.42 = (bf16[3,32,1024]{2,1,0:T(8,128)(2,1)S(1)}, bf16[3,32,1024]{2,1,0:T(8,128)(2,1)S(1)}, u32[]{:S(2)}, u32[]{:S(2)}) collective-permute-start(bf16[3,32,1024]{2,1,0:T(8,128)(2,1)S(1)} %get-tuple-element.451), channel_id=1, source_target_pairs={{0,2},{2,4},{4,6},{6,0},{1,3},{3,5},{5,7},{7,1},{8,10},{10,12},{12... | collective-permute-start | bytes 589832 | tf_op jit(solution)/shard_map/ppermute | solution.py:463
  550.5 51.9 %collective-permute-start.43 = (bf16[3,32,1024]{2,1,0:T(8,128)(2,1)S(1)}, bf16[3,32,1024]{2,1,0:T(8,128)(2,1)S(1)}, u32[]{:S(2)}, u32[]{:S(2)}) collective-permute-start(bf16[3,32,1024]{2,1,0:T(8,128)(2,1)S(1)} %get-tuple-element.450), channel_id=1, source_target_pairs={{0,4},{2,6},{4,0},{6,2},{1,5},{3,7},{5,1},{7,3},{8,12},{10,14},{12... | collective-permute-start | bytes 589832 | tf_op jit(solution)/shard_map/ppermute | solution.py:463
  552.9 50.2 %collective-permute-start.44 = (bf16[3,32,1024]{2,1,0:T(8,128)(2,1)S(1)}, bf16[3,32,1024]{2,1,0:T(8,128)(2,1)}, u32[]{:S(2)}, u32[]{:S(2)}) collective-permute-start(bf16[3,32,1024]{2,1,0:T(8,128)(2,1)S(1)} %get-tuple-element.449), channel_id=1, source_target_pairs={{0,6},{2,0},{4,2},{6,4},{1,7},{3,1},{5,3},{7,5},{8,14},{10,8},{12,... | collective-permute-start | bytes 589832 | tf_op jit(solution)/shard_map/ppermute | solution.py:463
  603.1 49.0 %all-to-all-start.6 = ((bf16[8,192,512]{2,1,0:T(8,128)(2,1)}), bf16[8,192,512]{2,1,0:T(8,128)(2,1)}, u32[]{:S(2)}, u32[]{:S(2)}) async-start(bf16[8,192,512]{2,1,0:T(8,128)(2,1)} %get-tuple-element.289), calls=%async_computation.10 | async-start | bytes 3145728 | tf_op jit(solution)/shard_map/all_to_all | solution.py:495
  (143 other events, 1843.3 us)
Sparse Core Ops, SparseCore 0:
  45.2 60.5 all-gather.6
  107.4 26.8 all-gather.8
  140.2 26.7 all-gather.10
  177.9 38.9 all-gather.14
  323.2 66.0 all-gather.12
  399.4 27.3 reduce-scatter.4
  436.4 41.7 reduce-scatter.8
  486.9 37.0 reduce-scatter.6
  545.3 40.8 reduce-scatter.10

commit v5 on v4

--- a/solution.py
+++ b/solution.py
@@ -129,6 +129,7 @@
 
 def self_backward_kernel(tok, width, half, head, scale, count, owner, place, *refs):
     blocks, refs = refs[:count], refs[count:]
+    before, refs = refs[:-12], refs[-12:]
     qkv, mixed_grad, mixed, total, out, slice_grad = refs[:6]
     key_t, key_sum, value_sum, rows, slice_sum, arrived = refs[6:]
     slot = pl.program_id(0)
@@ -193,7 +194,12 @@
             return carry
 
         lax.fori_loop(0, pl.num_programs(0), finish, 0)
-        slice_grad[...] = jnp.transpose(slice_sum[...])
+        if head < heads - 1:
+            slice_grad[...] = slice_sum[...]
+        else:
+            kinds = [slice(k * HEAD_DIM, (k + 1) * HEAD_DIM) for k in range(3)]
+            every = [part[kind, :] for kind in kinds for part in (*before, slice_sum)]
+            slice_grad[...] = jnp.transpose(jnp.concatenate(every, 0))
 
 
 def cross_forward_kernel(width, query, pair, mixed, total):
@@ -282,23 +288,29 @@
     return made if make else [qkv, *made]
 
 
-def self_backward(head, owner, place, blocks, qkv, mixed_grad, mixed, total):
+def self_backward(head, owner, place, blocks, before, qkv, mixed_grad, mixed, total):
     rows, width = qkv.shape[0], qkv.shape[1] // 3
     tok, model = blocks[0].shape
     group = rows // tok
     owned = pl.BlockSpec((None, HEAD_DIM, tok), lambda p, owner, _: (owner[p], 0, 0))
+    slices = (3 * HEAD_DIM, model + LANES)
+    if head == width // HEAD_DIM - 1:
+        slices = (model + LANES, 3 * width)
+    else:
+        before = ()
     return pl.pallas_call(
         functools.partial(
             self_backward_kernel, tok, width, group // 2, head, HEAD_DIM ** (-0.5), group
         ),
         out_shape=(
             jax.ShapeDtypeStruct((group, 3 * HEAD_DIM, tok), low_type),
-            jax.ShapeDtypeStruct((model + LANES, 3 * HEAD_DIM), jnp.float32),
+            jax.ShapeDtypeStruct(slices, jnp.float32),
         ),
         grid_spec=pltpu.PrefetchScalarGridSpec(
             num_scalar_prefetch=2,
             grid=(group,),
             in_specs=[pl.BlockSpec(memory_space=pl.ANY)] * group
+            + [whole_block(each.shape) for each in before]
             + [
                 whole_block(qkv.shape),
                 owned,
@@ -307,7 +319,7 @@
             ],
             out_specs=[
                 pl.BlockSpec((group, 3 * HEAD_DIM, tok), lambda *_: (0, 0, 0)),
-                pl.BlockSpec((model + LANES, 3 * HEAD_DIM), lambda *_: (0, 0)),
+                pl.BlockSpec(slices, lambda *_: (0, 0)),
             ],
             scratch_shapes=[
                 pltpu.VMEM((HEAD_DIM, rows), low_type),
@@ -321,7 +333,7 @@
         compiler_params=kernel_options(52),
         cost_estimate=declared,
         name="self_backward",
-    )(owner, place, *blocks, qkv, mixed_grad, mixed, total)
+    )(owner, place, *blocks, *before, qkv, mixed_grad, mixed, total)
 
 
 def split_columns(values, group):
@@ -546,14 +558,16 @@
     def in_columns(row):
         return lax.dynamic_update_slice(jnp.zeros((model,), jnp.float32), row, (member * width,))
 
+    part_rows = weight_rows // reps
     slices = jnp.concatenate(
         [
-            w_self_qkv.reshape(reps, weight_rows // reps, 3, group, width),
-            w_cross_kv.reshape(reps, weight_rows // reps, 2, group, width),
+            lax.dynamic_slice_in_dim(weight, rep * part_rows, part_rows, 0).reshape(
+                part_rows, -1, group, width
+            )
+            for weight in (w_self_qkv, w_cross_kv)
         ],
-        2,
-    )
-    slices = lax.dynamic_index_in_dim(slices, rep, 0, keepdims=False)
+        1,
+    )
     slices = slices.transpose(2, 0, 1, 3).reshape(group, weight_rows // reps, 5 * width)
     first_cut = w_fc1.reshape(weight_rows, line, 2, reps, unit)
     first_cut = lax.dynamic_index_in_dim(first_cut, rep, 3, keepdims=False)
@@ -575,9 +589,7 @@
 
     square = jnp.stack([w_self_out, w_cross_q, w_cross_out], 0)
     square = square.reshape(3, reps, weight_rows // reps, model)
-    square = lax.dynamic_index_in_dim(square, rep, 1, keepdims=False)
-    square = square.reshape(-1, model // (line * unit), line * unit).transpose(1, 0, 2)
-    square = square.reshape(-1, line * unit)
+    square = lax.dynamic_index_in_dim(square, rep, 1, keepdims=False).reshape(-1, model)
 
     inputs = layer_input.astype(jnp.float32)
     zeros = jnp.zeros((width,), jnp.float32)
@@ -595,8 +607,8 @@
     )
 
     both_cut = lax.all_gather(
-        jnp.concatenate([first_cut, square], 0), "line", axis=0, tiled=True
-    ).reshape(line, -1, line * unit)
+        jnp.concatenate([second_cut, square], 0), "line", axis=0, tiled=True
+    ).reshape(line, -1, model)
     blocks += [block, swap(block, "core", 1)]
     block = shift(block)
     slices = spread_over_rep(slices)
@@ -608,17 +620,16 @@
     slices = jnp.stack(rep_order(slices), 1).reshape(model, 5 * width)
     head_qkv, head_ckv = slices[:, : 3 * width], slices[:, 3 * width :]
     all_states = gather_rows(encoder_states)
-    block, blocks, both_cut, head_qkv, head_ckv, all_states, second_cut = stage(
-        (block, blocks, both_cut, head_qkv, head_ckv, all_states, second_cut)
+    block, blocks, both_cut, head_qkv, head_ckv, all_states, first_cut = stage(
+        (block, blocks, both_cut, head_qkv, head_ckv, all_states, first_cut)
     )
 
     blocks += [block, swap(block, "core", 1)]
-    square = spread_over_rep(both_cut[:, 2 * weight_rows :])
-    second_cut = lax.all_gather(second_cut, "line", axis=0, tiled=True)
-    wfirst = {0: both_cut[:, : 2 * weight_rows].reshape(model, line * unit)}
+    square = spread_over_rep(both_cut[:, unit:])
+    wfirst = {0: lax.all_gather(first_cut, "line", axis=0, tiled=True)}
     head_pair = (product(all_states, head_ckv) + cross_bias).astype(low_type)
     head_pair = split_columns(head_pair, 2)
-    wsecond = {0: second_cut}
+    wsecond = {0: both_cut[:, :unit].reshape(line * unit, model)}
     back = (lax.axis_index("line") - owners // 2) % line
     places = 2 * back + ((owners % 2) ^ core)
     slot_of = jnp.sum(
@@ -632,25 +643,24 @@
         self_totals.append(total)
         if head == 0:
             mixed, turn, square, head_pair = stage((mixed, turn, square, head_pair))
-            wfirst.update({d: swap(wfirst[0], "rep", d) for d in near})
+            wsecond.update({d: swap(wsecond[0], "rep", d) for d in near})
             square = jnp.stack(rep_order(square), 1)
             square_other = swap(square, "core", 1)
         if head == heads - 1:
             held = (mixed, wfirst, square, square_other)
             held, wsecond, self_low = stage((held, wsecond, self_low))
             mixed, wfirst, square, square_other = held
-            wfirst.update({d: swap(wfirst[0], "rep", d) for d in far})
-            wsecond.update({d: swap(wsecond[0], "rep", d) for d in near})
+            wsecond.update({d: swap(wsecond[0], "rep", d) for d in far})
+            wfirst.update({d: swap(wfirst[0], "rep", d) for d in near})
         self_mixed.append(mixed)
         self_low.append(exchange(mixed))
     qkv = made
     square = jnp.where(
         core == 0, jnp.stack([square, square_other], 1), jnp.stack([square_other, square], 1)
     )
-    square = square.reshape(line, 2, reps, -1, 3, weight_rows // reps, line * unit)
+    square = square.reshape(line, 2, reps, 3, weight_rows // reps, model)
     full_out, full_cross_q, full_cross_out = [
-        square[:, :, :, :, i].transpose(0, 1, 2, 4, 3, 5).reshape(model, model)
-        for i in range(3)
+        square[:, :, :, i].reshape(model, model) for i in range(3)
     ]
     pairs = lax.all_gather(head_pair, SHARD, axis=0, tiled=False)
     self_low, pairs = stage((self_low, pairs))
@@ -664,7 +674,7 @@
     )
     cross_low, cross_total = cross_forward(cross_queries, pairs)
     cross_low, wfirst, wsecond = stage((cross_low, wfirst, wsecond))
-    wsecond.update({d: swap(wsecond[0], "rep", d) for d in far})
+    wfirst.update({d: swap(wfirst[0], "rep", d) for d in far})
     second_sum = first_norm + (product(cross_low, full_cross_out) + proj_biases[5])
     second_norm, norm2_back = jax.vjp(norm_rows, second_sum, norm_gains[1], norm_shifts[1])
     second_low = second_norm.astype(low_type)
@@ -821,6 +831,7 @@
             turn,
             places,
             blocks,
+            slice_parts,
             qkv,
             mixed_grad[head],
             self_mixed[head],
@@ -848,13 +859,14 @@
         parts.append(exchange(part))
         slice_parts.append(slice_part)
 
-    slice_parts = trade_slices(
-        jnp.concatenate([slice_parts[0], pair_slices] + slice_parts[1:], 1)
-    )
+    slice_parts = trade_slices(jnp.concatenate([slice_parts[-1], pair_slices], 1))
     for offset in near[1:]:
         first_sums = double(first_sums, offset)
     square = double(sum_of(square_terms).astype(low_type)[None], near[0])
-    parts, slice_parts, first_sums, square = stage((parts, slice_parts, first_sums, square))
+    small = hop(small, 1)
+    held = (first_sums, square, small)
+    parts, slice_parts, held = stage((parts, slice_parts, held))
+    first_sums, square, small = held
 
     slice_parts = exchange_slices(slice_parts)
     for offset in near[1:]:
@@ -888,16 +900,12 @@
     grad_fc1 = grad_fc1.transpose(2, 3, 0, 1, 4).reshape(weight_rows, feed).astype(jnp.float32)
 
     def of_self(values):
-        found, start = [], 0
-        for head in range(heads):
-            found.append(values[..., start : start + 3 * HEAD_DIM])
-            start += 3 * HEAD_DIM + (0 if head else 2 * width)
-        found = [each.reshape(-1, group, 3, HEAD_DIM) for each in found]
-        return jnp.stack(found, 3).transpose(0, 2, 1, 3, 4).reshape(-1, 3, model)
+        values = values[..., : 3 * width].reshape(-1, group, 3, width)
+        return values.transpose(0, 2, 1, 3).reshape(-1, 3, model)
 
     def of_cross(values):
-        values = values[..., 3 * HEAD_DIM : 3 * HEAD_DIM + 2 * width]
-        return values.reshape(-1, group, 2, width).transpose(0, 2, 1, 3).reshape(-1, 2, model)
+        values = values[..., 3 * width :].reshape(-1, group, 2, width)
+        return values.transpose(0, 2, 1, 3).reshape(-1, 2, model)
 
     grad_self_qkv = of_self(slice_parts[0].astype(jnp.float32)).reshape(weight_rows, 3 * model)
     grad_cross_kv = of_cross(slice_parts[0].astype(jnp.float32)).reshape(weight_rows, 2 * model)

time: 722 us -> 717 us (level)
  local copies, waits for them, and re-layouts: 87.8 us -> 67.7 us
  Pallas kernels: 144 us -> 131 us
  waiting for transfers between devices: 189 us -> 202 us
  matrix products: 112 us -> 121 us
    pallas_call x1, Pallas kernels: 23.4 us -> 10.9 us  [cross_forward(): pl.pallas_call(functools.partial(cross_forward_kernel, width), out_shape=...]
    transpose x7 -> x0, local copies, waits for them, and re-layouts: 9.46 us -> none  [the longest x4 7.65 us: local(): square[:, :, :, :, i].transpose(0, 1, 2, 4, 3, 5).reshape(model, model)]
    dot_general x12, matrix products: 37.9 us -> 47.3 us  [product(): return jnp.dot(former, latter, preferred_element_type=jnp.float32)]
    ppermute x52, waiting for transfers between devices: 81.1 us -> 90.2 us  [swap(): return lax.ppermute(values, axis, [(i, i ^ offset) for i in range(size)])]
    unnamed x212 -> x207, local copies, waits for them, and re-layouts: 34.9 us -> 26.5 us
  transfers between devices with their start and end apart: 75 -> 75, of which waited for: 26 -> 28; matrix products, arithmetic and copies ran while one was open for 31% -> 30% of each run, Pallas kernels for 20% -> 19%
where the time goes in v5:
time: 717 us; the launch traced here: 707 us
  waiting for transfers between devices  202 us (28%)
  Pallas kernels  131 us (18%)
  matrix products  121 us (17%)
  starting transfers between devices  98.3 us (14%)
  other arithmetic  69.9 us (10%)
  local copies, waits for them, and re-layouts  67.7 us (9%)
  between operations  16.3 us (2%)
    ppermute x52, waiting for transfers between devices, swap(): return lax.ppermute(values, axis, [(i, i ^ offset) for i in range(size)])  90.2 us
    ppermute x3, waiting for transfers between devices, shift(): lax.ppermute(values, 'line', [(i, (i + 1) % line) for i in range(line)])  62.7 us
    pallas_call x2, Pallas kernels, self_backward(): pl.pallas_call(functools.partial(self_backward_kernel, tok, width, group...  62.2 us
    ppermute x52, starting transfers between devices, swap(): return lax.ppermute(values, axis, [(i, i ^ offset) for i in range(size)])  47.9 us
    dot_general x12, matrix products, product(): return jnp.dot(former, latter, preferred_element_type=jnp.float32)  47.3 us
    pallas_call x2, Pallas kernels, self_forward(): pl.pallas_call(functools.partial(self_forward_kernel, tok, width, group /...  44.2 us
    dot_general x12, matrix products, product_right(): lax.dot_general(former, latter, (((1,), (1,)), ((), ())), preferred_eleme...  37.4 us
    dot_general x13, matrix products, product_left(): lax.dot_general(former, latter, (((0,), (0,)), ((), ())), preferred_eleme...  36.8 us
  transfers between devices with their start and end apart: 75, of which 28 were waited for; matrix products, arithmetic and copies ran while one was open for 30% of the time, Pallas kernels for 19%

profile of v5, /device:TPU:0, one launch (start us, length us, event | category | flops | bytes accessed | tf_op | source)
XLA Modules:
  0.0 706.7 jit_solution(709710992430039260)
XLA Ops:
  27.9 14.8 %all-to-all-done = bf16[8,32,640]{2,1,0:T(8,128)(2,1)S(1)} async-done(((bf16[8,32,640]{2,1,0:T(8,128)(2,1)}), bf16[8,32,640]{2,1,0:T(8,128)(2,1)S(1)}, u32[]{:S(2)}, u32[]{:S(2)}) %all-to-all-start) | async-done | bytes 327712 | tf_op jit(solution)/shard_map/all_to_all | solution.py:507
  48.8 7.0 collective-permute-done.4
  55.8 7.8 %collective-permute-done.5 = bf16[8,32,640]{2,1,0:T(8,128)(2,1)S(1)} collective-permute-done((bf16[8,32,640]{2,1,0:T(8,128)(2,1)S(1)}, bf16[8,32,640]{2,1,0:T(8,128)(2,1)S(1)}, u32[]{:S(2)}, u32[]{:S(2)}) %collective-permute-start.5) | collective-permute-done | bytes 327712 | tf_op jit(solution)/shard_map/ppermute | solution.py:403
  63.6 24.9 %collective-permute-done.3.refs_4_ = bf16[512,1024]{1,0:T(8,128)(2,1)} collective-permute-done((bf16[512,1024]{1,0:T(8,128)(2,1)S(1)}, bf16[512,1024]{1,0:T(8,128)(2,1)}, u32[]{:S(2)}, u32[]{:S(2)}) %collective-permute-start.3) | collective-permute-done | bytes 1048608 | tf_op jit(solution)/shard_map/ppermute | solution.py:495
  93.5 37.8 %collective-permute-done.8.refs_6_ = bf16[512,1024]{1,0:T(8,128)(2,1)} collective-permute-done((bf16[512,1024]{1,0:T(8,128)(2,1)}, bf16[512,1024]{1,0:T(8,128)(2,1)}, u32[]{:S(2)}, u32[]{:S(2)}) %collective-permute-start.8) | collective-permute-done | bytes 1048608 | tf_op jit(solution)/shard_map/ppermute | solution.py:495
  143.7 25.8 %self_forward.2 = (bf16[4096,384]{1,0:T(8,128)(2,1)}, bf16[8,64,512]{2,1,0:T(8,128)(2,1)}, f32[8,1,512]{2,1,0:T(1,128)S(1)}) custom-call(s32[8]{0:T(128)S(1)} %select_reduce_fusion.1.owner, s32[8]{0:T(128)S(1)} %select_reduce_fusion.slot_of, bf16[512,1024]{1,0:T(8,128)(2,1)} %refs_0_.2, bf16[512,1024]{1,0:T(8,128)(2,1)} %copy-done.21, ...), custom_call_target="tpu_custom_call" | custom-call | flops 1048576 | bytes 65536 | tf_op jit(solution)/shard_map/self_forward/pallas_call | solution.py:272
  185.9 18.4 %self_forward.3 = (bf16[8,64,512]{2,1,0:T(8,128)(2,1)}, f32[8,1,512]{2,1,0:T(1,128)S(1)}) custom-call(s32[8]{0:T(128)S(1)} %select_reduce_fusion.1.owner, s32[8]{0:T(128)S(1)} %select_reduce_fusion.slot_of, bf16[4096,384]{1,0:T(8,128)(2,1)} %get-tuple-element.196.refs_0_.refs_8_.refs_9_), custom_call_target="tpu_custom_call" | custom-call | flops 1048576 | bytes 65536 | tf_op jit(solution)/shard_map/self_forward/pallas_call | solution.py:272
  206.8 7.4 %all-to-all-done.1 = bf16[8,64,512]{2,1,0:T(8,128)(2,1)S(1)} async-done(((bf16[8,64,512]{2,1,0:T(8,128)(2,1)}), bf16[8,64,512]{2,1,0:T(8,128)(2,1)S(1)}, u32[]{:S(2)}, u32[]{:S(2)}) %all-to-all-start.1) | async-done | bytes 524320 | tf_op jit(solution)/shard_map/all_to_all | solution.py:507
  220.9 5.4 maximum_select_fusion
  244.1 10.9 %cross_forward.1 = (bf16[512,1024]{1,0:T(8,128)(2,1)S(1)}, f32[8,8,512]{2,1,0:T(8,128)S(1)}) custom-call(bf16[512,1024]{1,0:T(8,128)(2,1)S(1)} %multiply_convert_fusion.8.query, bf16[8,2,512,128]{3,2,1,0:T(8,128)(2,1)S(1)} %bitcast.344), custom_call_target="tpu_custom_call" | custom-call | flops 1048576 | bytes 65536 | tf_op jit(solution)/shard_map/cross_forward/pallas_call | solution.py:363
  255.0 8.1 %collective-permute-done.18 = bf16[1024,512]{0,1:T(8,128)(2,1)} collective-permute-done((bf16[1024,512]{0,1:T(8,128)(2,1)}, bf16[1024,512]{0,1:T(8,128)(2,1)}, u32[]{:S(2)}, u32[]{:S(2)}) %collective-permute-start.18) | collective-permute-done | bytes 1048608 | tf_op jit(solution)/shard_map/ppermute | solution.py:403
  268.2 6.2 multiply_convert_fusion.5
  275.8 13.5 %multiply_convert_fusion.7 = (bf16[1024,512]{1,0:T(8,128)(2,1)S(1)}, f32[1024,512]{1,0:T(8,128)}) fusion(f32[512]{0:T(512)S(1)} %bitcast.442, bf16[1024,512]{0,1:T(8,128)(2,1)S(1)} %copy-done.44, bf16[512,1024]{1,0:T(8,128)(2,1)S(1)} %collective-permute-done.20, bf16[512,1024]{1,0:T(8,128)(2,1)S(1)} %fusion.10), kind=kOutput, calls=%fused_computation.64 | convolution fusion | flops 1090519040 | bytes 6293504 | tf_op jit(solution)/shard_map/dot_general | solution.py:29
  292.1 5.9 multiply_convert_fusion.6
  301.0 4.6 multiply_convert_fusion.4
  378.3 5.3 collective-permute-done.26
  404.0 13.9 %cross_backward.1 = (bf16[512,1024]{1,0:T(8,128)(2,1)S(1)}, bf16[8,2,512,128]{3,2,1,0:T(8,128)(2,1)}) custom-call(bf16[512,1024]{1,0:T(8,128)(2,1)S(1)} %copy-done.5, bf16[8,2,512,128]{3,2,1,0:T(8,128)(2,1)S(1)} %bitcast.345, bf16[512,1024]{1,0:T(8,128)(2,1)S(1)} %convolution_convert_fusion.5.mixed_grad, bf16[512,1024]{1,0:T(8,128)(2,1)S(1)} %copy-done.9, ...), custom_call_target="tpu_custom_call" | custom-call | flops 1048576 | bytes 65536 | tf_op jit(solution)/shard_map/cross_backward/pallas_call | solution.py:385
  418.9 5.1 multiply_reduce_fusion.1
  463.6 4.5 fusion
  469.9 6.8 all-to-all-done.3.refs_9_
  476.7 6.4 collective-permute-done.33
  489.3 4.8 all-to-all-start.4
  499.7 30.4 %self_backward.2 = (bf16[8,192,512]{2,1,0:T(8,128)(2,1)}, f32[192,1152]{1,0:T(8,128)S(1)}) custom-call(s32[8]{0:T(128)S(1)} %copy-done.12, s32[8]{0:T(128)S(1)} %copy-done.14, bf16[512,1024]{1,0:T(8,128)(2,1)} %refs_0_.2, bf16[512,1024]{1,0:T(8,128)(2,1)} %copy-done.21, bf16[512,1024]{1,0:T(8,128)(2,1)} %copy-done.20, ...), custom_call_target="tpu_custom_call" | custom-call | flops 1048576 | bytes 65536 | tf_op jit(solution)/shard_map/self_backward/pallas_call | solution.py:301
  530.1 8.2 %collective-permute-done.39 = f32[14,1024]{1,0:T(8,128)S(1)} collective-permute-done((f32[14,1024]{1,0:T(8,128)S(1)}, f32[14,1024]{1,0:T(8,128)S(1)}, u32[]{:S(2)}, u32[]{:S(2)}) %collective-permute-start.39) | collective-permute-done | bytes 57376 | tf_op jit(solution)/shard_map/ppermute | solution.py:403
  539.2 4.9 all-to-all-start.5
  558.0 31.8 %self_backward.3 = (bf16[8,192,512]{2,1,0:T(8,128)(2,1)}, f32[1152,384]{1,0:T(8,128)}) custom-call(s32[8]{0:T(128)S(1)} %copy-done.12, s32[8]{0:T(128)S(1)} %copy-done.14, bf16[512,1024]{1,0:T(8,128)(2,1)} %refs_0_.2, bf16[512,1024]{1,0:T(8,128)(2,1)} %copy-done.21, bf16[512,1024]{1,0:T(8,128)(2,1)} %copy-done.20, ...), custom_call_target="tpu_custom_call" | custom-call | flops 1048576 | bytes 65536 | tf_op jit(solution)/shard_map/self_backward/pallas_call | solution.py:301
  591.0 13.9 %collective-permute-done.43 = bf16[3,32,1024]{2,1,0:T(8,128)(2,1)S(1)} collective-permute-done((bf16[3,32,1024]{2,1,0:T(8,128)(2,1)S(1)}, bf16[3,32,1024]{2,1,0:T(8,128)(2,1)S(1)}, u32[]{:S(2)}, u32[]{:S(2)}) %collective-permute-start.43) | collective-permute-done | bytes 196640 | tf_op jit(solution)/shard_map/ppermute | solution.py:475
  605.6 6.3 all-to-all-start.6
  627.1 18.3 %collective-permute-done.49 = bf16[1,3,32,1024]{3,2,1,0:T(8,128)(2,1)S(1)} collective-permute-done((bf16[1,3,32,1024]{3,2,1,0:T(8,128)(2,1)S(1)}, bf16[1,3,32,1024]{3,2,1,0:T(8,128)(2,1)S(1)}, u32[]{:S(2)}, u32[]{:S(2)}) %collective-permute-start.49) | collective-permute-done | bytes 196640 | tf_op jit(solution)/shard_map/ppermute | solution.py:403
  645.4 7.4 %collective-permute-done.48 = bf16[2,128,1024]{2,1,0:T(8,128)(2,1)S(1)} collective-permute-done((bf16[2,128,1024]{2,1,0:T(8,128)(2,1)S(1)}, bf16[2,128,1024]{2,1,0:T(8,128)(2,1)S(1)}, u32[]{:S(2)}, u32[]{:S(2)}) %collective-permute-start.48) | collective-permute-done | bytes 524320 | tf_op jit(solution)/shard_map/ppermute | solution.py:403
  656.2 4.9 all-to-all-start.7
  666.5 8.5 %bitcast_add_fusion = f32[512,1024]{1,0:T(8,128)} fusion(f32[512,1024]{1,0:T(8,128)S(1)} %copy-done.24, bf16[8,2,192,1024]{3,2,1,0:T(8,128)(2,1)} %bitcast.447, f32[512]{0:T(512)S(1)} %copy-done.78, bf16[8,1,192,512]{3,2,0,1:T(8,128)(2,1)} %bitcast.111, bf16[8,1,192,512]{3,2,0,1:T(8,128)(2,1)} %bitcast.110), kind=kOutput, calls=%fused_computation.35 | convolution fusion | flops 3223846912 | bytes 13633536 | tf_op jit(solution)/shard_map/dot_general | solution.py:33
  (551 shorter events, 310.6 us)
Async XLA Ops:
  7.2 35.5 %collective-permute-start = (bf16[512,1024]{1,0:T(8,128)(2,1)}, bf16[512,1024]{1,0:T(8,128)(2,1)S(1)}, u32[]{:S(2)}, u32[]{:S(2)}) collective-permute-start(bf16[512,1024]{1,0:T(8,128)(2,1)} %refs_0_.2), channel_id=1, source_target_pairs={{0,2},{2,4},{4,6},{6,0},{1,3},{3,5},{5,7},{7,1},{8,10},{10,12},{12... | collective-permute-start | bytes 3145736 | tf_op jit(solution)/shard_map/ppermute | solution.py:495
  19.3 112.0 %all-gather.7.cloned.1.call-start = ((), (), s32[]{:S(2)}) async-start(), calls=%async_computation.12 | async-start | bytes 2293760 | tf_op jit(solution)/shard_map/all_gather | solution.py:609
  45.0 89.2 %all-gather.9.cloned.1.call-start = ((), (), s32[]{:S(2)}) async-start(), calls=%async_computation.13 | async-start | bytes 1179648 | tf_op jit(solution)/shard_map/all_gather | solution.py:499
  45.1 43.4 %collective-permute-start.3 = (bf16[512,1024]{1,0:T(8,128)(2,1)S(1)}, bf16[512,1024]{1,0:T(8,128)(2,1)}, u32[]{:S(2)}, u32[]{:S(2)}) collective-permute-start(bf16[512,1024]{1,0:T(8,128)(2,1)S(1)} %collective-permute-done.refs_2_), channel_id=1, source_target_pairs={{0,2},{2,4},{4,6},{6,0},{1,3},{3,5},{5,7},{7,1},{8,10},{10,12},{12... | collective-permute-start | bytes 3145736 | tf_op jit(solution)/shard_map/ppermute | solution.py:495
  45.2 43.3 %collective-permute-start.7 = (bf16[512,1024]{1,0:T(8,128)(2,1)S(1)}, bf16[512,1024]{1,0:T(8,128)(2,1)}, u32[]{:S(2)}, u32[]{:S(2)}) collective-permute-start(bf16[512,1024]{1,0:T(8,128)(2,1)S(1)} %collective-permute-done.refs_2_), channel_id=1, source_target_pairs={{0,1},{1,0},{2,3},{3,2},{4,5},{5,4},{6,7},{7,6},{8,9},{9,8},{10,11... | collective-permute-start | bytes 3145736 | tf_op jit(solution)/shard_map/ppermute | solution.py:403
  88.5 118.3 %all-gather.11.cloned.1.call-start = ((), (), s32[]{:S(2)}) async-start(), calls=%async_computation.14 | async-start | bytes 1310720 | tf_op jit(solution)/shard_map/all_gather | solution.py:629
  88.6 42.7 %collective-permute-start.8 = (bf16[512,1024]{1,0:T(8,128)(2,1)}, bf16[512,1024]{1,0:T(8,128)(2,1)}, u32[]{:S(2)}, u32[]{:S(2)}) collective-permute-start(bf16[512,1024]{1,0:T(8,128)(2,1)} %collective-permute-done.3.refs_4_), channel_id=1, source_target_pairs={{0,2},{2,4},{4,6},{6,0},{1,3},{3,5},{5,7},{7,1},{8,10},{10,12},{12... | collective-permute-start | bytes 3145736 | tf_op jit(solution)/shard_map/ppermute | solution.py:495
  92.7 38.6 %collective-permute-start.9 = (bf16[512,1024]{1,0:T(8,128)(2,1)}, bf16[512,1024]{1,0:T(8,128)(2,1)}, u32[]{:S(2)}, u32[]{:S(2)}) collective-permute-start(bf16[512,1024]{1,0:T(8,128)(2,1)} %collective-permute-done.3.refs_4_), channel_id=1, source_target_pairs={{0,1},{1,0},{2,3},{3,2},{4,5},{5,4},{6,7},{7,6},{8,9},{9,8},{10,11... | collective-permute-start | bytes 3145736 | tf_op jit(solution)/shard_map/ppermute | solution.py:403
  137.2 36.4 %collective-permute-start.12 = (bf16[4,96,1024]{2,1,0:T(8,128)(2,1)S(1)}, bf16[4,96,1024]{2,1,0:T(8,128)(2,1)}, u32[]{:S(2)}, u32[]{:S(2)}) collective-permute-start(bf16[4,96,1024]{2,1,0:T(8,128)(2,1)S(1)} %slice.245), channel_id=1, source_target_pairs={{0,16},{8,24},{16,0},{24,8},{1,17},{9,25},{17,1},{25,9},{2,18},{10... | collective-permute-start | bytes 2359304 | tf_op jit(solution)/shard_map/ppermute | solution.py:403
  140.1 93.1 %all-gather.15.cloned.1.call-start = ((), (), s32[]{:S(2)}) async-start(), calls=%async_computation.20 | async-start | bytes 2359296 | tf_op jit(solution)/shard_map/all_gather | solution.py:665
  177.8 36.4 %collective-permute-start.14 = (bf16[4,4,96,1024]{3,2,1,0:T(8,128)(2,1)}, bf16[4,4,96,1024]{3,2,1,0:T(8,128)(2,1)}, u32[]{:S(2)}, u32[]{:S(2)}) collective-permute-start(bf16[4,4,96,1024]{3,2,1,0:T(8,128)(2,1)} %pad_maximum_fusion.1), channel_id=1, source_target_pairs={{0,1},{1,0},{2,3},{3,2},{4,5},{5,4},{6,7},{7,6},{8,9},{9,8},{10,11... | collective-permute-start | bytes 9437192 | tf_op jit(solution)/shard_map/ppermute | solution.py:403
  214.2 40.8 %collective-permute-start.17 = (bf16[1024,512]{0,1:T(8,128)(2,1)}, bf16[1024,512]{0,1:T(8,128)(2,1)}, u32[]{:S(2)}, u32[]{:S(2)}) collective-permute-start(bf16[1024,512]{0,1:T(8,128)(2,1)} %all-gather.11.cloned.1.call-done), channel_id=1, source_target_pairs={{0,8},{8,0},{16,24},{24,16},{1,9},{9,1},{17,25},{25,17},{2,10},{10... | collective-permute-start | bytes 3145736 | tf_op jit(solution)/shard_map/ppermute | solution.py:403
  215.7 47.5 %collective-permute-start.18 = (bf16[1024,512]{0,1:T(8,128)(2,1)}, bf16[1024,512]{0,1:T(8,128)(2,1)}, u32[]{:S(2)}, u32[]{:S(2)}) collective-permute-start(bf16[1024,512]{0,1:T(8,128)(2,1)} %all-gather.11.cloned.1.call-done), channel_id=1, source_target_pairs={{0,16},{8,24},{16,0},{24,8},{1,17},{9,25},{17,1},{25,9},{2,18},{10... | collective-permute-start | bytes 3145736 | tf_op jit(solution)/shard_map/ppermute | solution.py:403
  220.8 198.0 %all-gather.13.cloned.1.call-start = ((), (), s32[]{:S(2)}) async-start(), calls=%async_computation.15 | async-start | bytes 7077888 | tf_op jit(solution)/shard_map/all_gather | solution.py:499
  323.3 146.6 %reduce-scatter.5.cloned.1.call-start = ((), (), s32[]{:S(2)}) async-start(), calls=%async_computation.16 | async-start | bytes 1310720 | tf_op jit(solution)/shard_map/reduce_scatter | solution.py:722
  400.5 138.7 %reduce-scatter.9.cloned.1.call-start = ((), (), s32[]{:S(2)}) async-start(), calls=%async_computation.18 | async-start | bytes 2359296 | tf_op jit(solution)/shard_map/reduce_scatter | solution.py:734
  453.4 85.8 %reduce-scatter.7.cloned.1.call-start = ((), (), s32[]{:S(2)}) async-start(), calls=%async_computation.17 | async-start | bytes 1310720 | tf_op jit(solution)/shard_map/reduce_scatter | solution.py:797
  489.3 49.8 %all-to-all-start.4 = ((bf16[8,64,512]{2,1,0:T(8,128)(2,1)}), bf16[8,64,512]{2,1,0:T(8,128)(2,1)S(1)}, u32[]{:S(2)}, u32[]{:S(2)}) async-start(bf16[8,64,512]{2,1,0:T(8,128)(2,1)} %get-tuple-element.417), calls=%async_computation.6 | async-start | bytes 1048576 | tf_op jit(solution)/shard_map/all_to_all | solution.py:507
  494.2 45.0 %collective-permute-start.36 = (bf16[4,3,32,1024]{3,2,0,1:T(8,128)(2,1)}, bf16[4,3,32,1024]{3,2,0,1:T(8,128)(2,1)S(1)}, u32[]{:S(2)}, u32[]{:S(2)}) collective-permute-start(bf16[4,3,32,1024]{3,2,0,1:T(8,128)(2,1)} %get-tuple-element.269), channel_id=1, source_target_pairs={{0,8},{8,0},{16,24},{24,16},{1,9},{9,1},{17,25},{25,17},{2,10},{10... | collective-permute-start | bytes 2359304 | tf_op jit(solution)/shard_map/ppermute | solution.py:403
  494.9 44.3 %collective-permute-start.37 = (bf16[4,3,32,1024]{3,2,0,1:T(8,128)(2,1)}, bf16[4,3,32,1024]{3,2,0,1:T(8,128)(2,1)}, u32[]{:S(2)}, u32[]{:S(2)}) collective-permute-start(bf16[4,3,32,1024]{3,2,0,1:T(8,128)(2,1)} %get-tuple-element.270), channel_id=1, source_target_pairs={{0,16},{8,24},{16,0},{24,8},{1,17},{9,25},{17,1},{25,9},{2,18},{10... | collective-permute-start | bytes 2359304 | tf_op jit(solution)/shard_map/ppermute | solution.py:403
  496.2 43.0 %collective-permute-start.38 = (bf16[4,3,32,1024]{3,2,0,1:T(8,128)(2,1)}, bf16[4,3,32,1024]{3,2,0,1:T(8,128)(2,1)}, u32[]{:S(2)}, u32[]{:S(2)}) collective-permute-start(bf16[4,3,32,1024]{3,2,0,1:T(8,128)(2,1)} %get-tuple-element.271), channel_id=1, source_target_pairs={{0,24},{8,16},{16,8},{24,0},{1,25},{9,17},{17,9},{25,1},{2,26},{10... | collective-permute-start | bytes 2359304 | tf_op jit(solution)/shard_map/ppermute | solution.py:403
  497.6 40.6 %collective-permute-start.35 = (bf16[1,128,1024]{2,1,0:T(8,128)(2,1)S(1)}, bf16[1,128,1024]{2,1,0:T(8,128)(2,1)S(1)}, u32[]{:S(2)}, u32[]{:S(2)}) collective-permute-start(bf16[1,128,1024]{2,1,0:T(8,128)(2,1)S(1)} %bitcast.397), channel_id=1, source_target_pairs={{0,8},{8,0},{16,24},{24,16},{1,9},{9,1},{17,25},{25,17},{2,10},{10... | collective-permute-start | bytes 786440 | tf_op jit(solution)/shard_map/ppermute | solution.py:403
  498.4 39.9 %collective-permute-start.39 = (f32[14,1024]{1,0:T(8,128)S(1)}, f32[14,1024]{1,0:T(8,128)S(1)}, u32[]{:S(2)}, u32[]{:S(2)}) collective-permute-start(f32[14,1024]{1,0:T(8,128)S(1)} %add.525), channel_id=1, source_target_pairs={{0,8},{8,0},{16,24},{24,16},{1,9},{9,1},{17,25},{25,17},{2,10},{10... | collective-permute-start | bytes 172040 | tf_op jit(solution)/shard_map/ppermute | solution.py:403
  539.2 66.3 %all-to-all-start.5 = ((bf16[8,192,512]{2,1,0:T(8,128)(2,1)}), bf16[8,192,512]{2,1,0:T(8,128)(2,1)}, u32[]{:S(2)}, u32[]{:S(2)}) async-start(bf16[8,192,512]{2,1,0:T(8,128)(2,1)} %get-tuple-element.287), calls=%async_computation.9 | async-start | bytes 3145728 | tf_op jit(solution)/shard_map/all_to_all | solution.py:507
  544.1 61.5 %reduce-scatter.11.cloned.1.call-start = ((), (), s32[]{:S(2)}) async-start(), calls=%async_computation.19 | async-start | bytes 1179648 | tf_op jit(solution)/shard_map/reduce_scatter | solution.py:503
  547.5 42.3 %collective-permute-start.40 = (bf16[1,128,1024]{2,1,0:T(8,128)(2,1)S(1)}, bf16[1,128,1024]{2,1,0:T(8,128)(2,1)S(1)}, u32[]{:S(2)}, u32[]{:S(2)}) collective-permute-start(bf16[1,128,1024]{2,1,0:T(8,128)(2,1)S(1)} %reshape.797), channel_id=1, source_target_pairs={{0,8},{8,0},{16,24},{24,16},{1,9},{9,1},{17,25},{25,17},{2,10},{10... | collective-permute-start | bytes 786440 | tf_op jit(solution)/shard_map/ppermute | solution.py:403
  548.2 41.6 %collective-permute-start.41 = (bf16[2,128,1024]{2,1,0:T(8,128)(2,1)}, bf16[2,128,1024]{2,1,0:T(8,128)(2,1)S(1)}, u32[]{:S(2)}, u32[]{:S(2)}) collective-permute-start(bf16[2,128,1024]{2,1,0:T(8,128)(2,1)} %pad_maximum_fusion.23), channel_id=1, source_target_pairs={{0,16},{8,24},{16,0},{24,8},{1,17},{9,25},{17,1},{25,9},{2,18},{10... | collective-permute-start | bytes 1572872 | tf_op jit(solution)/shard_map/ppermute | solution.py:403
  552.1 38.9 %collective-permute-start.42 = (bf16[3,32,1024]{2,1,0:T(8,128)(2,1)S(1)}, bf16[3,32,1024]{2,1,0:T(8,128)(2,1)S(1)}, u32[]{:S(2)}, u32[]{:S(2)}) collective-permute-start(bf16[3,32,1024]{2,1,0:T(8,128)(2,1)S(1)} %get-tuple-element.433), channel_id=1, source_target_pairs={{0,2},{2,4},{4,6},{6,0},{1,3},{3,5},{5,7},{7,1},{8,10},{10,12},{12... | collective-permute-start | bytes 589832 | tf_op jit(solution)/shard_map/ppermute | solution.py:475
  554.2 50.7 %collective-permute-start.43 = (bf16[3,32,1024]{2,1,0:T(8,128)(2,1)S(1)}, bf16[3,32,1024]{2,1,0:T(8,128)(2,1)S(1)}, u32[]{:S(2)}, u32[]{:S(2)}) collective-permute-start(bf16[3,32,1024]{2,1,0:T(8,128)(2,1)S(1)} %get-tuple-element.432), channel_id=1, source_target_pairs={{0,4},{2,6},{4,0},{6,2},{1,5},{3,7},{5,1},{7,3},{8,12},{10,14},{12... | collective-permute-start | bytes 589832 | tf_op jit(solution)/shard_map/ppermute | solution.py:475
  556.5 49.0 %collective-permute-start.44 = (bf16[3,32,1024]{2,1,0:T(8,128)(2,1)S(1)}, bf16[3,32,1024]{2,1,0:T(8,128)(2,1)}, u32[]{:S(2)}, u32[]{:S(2)}) collective-permute-start(bf16[3,32,1024]{2,1,0:T(8,128)(2,1)S(1)} %get-tuple-element.431), channel_id=1, source_target_pairs={{0,6},{2,0},{4,2},{6,4},{1,7},{3,1},{5,3},{7,5},{8,14},{10,8},{12,... | collective-permute-start | bytes 589832 | tf_op jit(solution)/shard_map/ppermute | solution.py:475
  605.6 48.1 %all-to-all-start.6 = ((bf16[8,192,512]{2,1,0:T(8,128)(2,1)}), bf16[8,192,512]{2,1,0:T(8,128)(2,1)}, u32[]{:S(2)}, u32[]{:S(2)}) async-start(bf16[8,192,512]{2,1,0:T(8,128)(2,1)} %get-tuple-element.289), calls=%async_computation.10 | async-start | bytes 3145728 | tf_op jit(solution)/shard_map/all_to_all | solution.py:507
  617.7 35.2 %collective-permute-start.45 = (bf16[8,48,640]{2,1,0:T(8,128)(2,1)S(1)}, bf16[8,48,640]{2,1,0:T(8,128)(2,1)}, u32[]{:S(2)}, u32[]{:S(2)}) collective-permute-start(bf16[8,48,640]{2,1,0:T(8,128)(2,1)S(1)} %get-tuple-element.438), channel_id=1, source_target_pairs={{0,8},{8,0},{16,24},{24,16},{1,9},{9,1},{17,25},{25,17},{2,10},{10... | collective-permute-start | bytes 1474568 | tf_op jit(solution)/shard_map/ppermute | solution.py:403
  (140 other events, 1842.9 us)
Sparse Core Ops, SparseCore 0:
  45.2 60.5 all-gather.6
  107.3 26.8 all-gather.8
  140.2 29.0 all-gather.10
  177.9 38.9 all-gather.14
  323.4 62.3 all-gather.12
  400.6 25.0 reduce-scatter.4
  437.5 39.2 reduce-scatter.8
  489.5 36.9 reduce-scatter.6
  547.2 38.7 reduce-scatter.10

commit v6 on v5

--- a/solution.py
+++ b/solution.py
@@ -811,12 +811,22 @@
         return values[..., :part_rows, :], one_row(values[..., part_rows:, :])[..., :1, :]
 
     def trade_slices(values):
-        sums = jnp.broadcast_to(values[model : model + 1], (group, 1, values.shape[1]))
-        values = values[:model].reshape(group, reps, part_rows, -1)
-        return trade_over_rep([with_sums(part, sums) for part in parts_of(values, 1)])
+        columns = values.shape[1]
+        sums = two_rows(jnp.broadcast_to(values[model : model + 1], (8, columns)))
+        values = values[:model].reshape(group, reps, part_rows, columns).astype(low_type)
+        return trade_over_rep(
+            [
+                jnp.concatenate([part.reshape(-1, columns), sums], 0)
+                for part in parts_of(values, 1)
+            ]
+        )
 
     def exchange_slices(terms):
-        return exchange(with_sums(*split_sums(sum_of(terms))))
+        values = sum_of(terms)
+        sums = one_row(values[group * part_rows :])[:1]
+        sums = jnp.broadcast_to(sums, (group,) + sums.shape)
+        values = values[: group * part_rows].reshape(group, part_rows, -1)
+        return exchange(with_sums(values, sums))
 
     def join_slices(values):
         values, sums = split_sums(values.astype(jnp.float32))
@@ -843,7 +853,6 @@
             held, mixed_grad, own_pair_grad = stage((held, mixed_grad, own_pair_grad))
             part, slice_part, turn, first_sums, second_sums, square_terms, small = held
             own_pair_grad = join_columns(own_pair_grad)
-            enc_grad = scatter_rows(product_right(own_pair_grad, head_ckv).astype(low_type))
             for offset in near[1:]:
                 second_sums = double(second_sums, offset)
             first_sums = first_sums.reshape(2, weight_rows, line * unit).transpose(1, 0, 2)
@@ -853,9 +862,9 @@
             pair_slices = jnp.concatenate([product_left(all_states, own_pair_grad), pair_sums], 0)
             square_terms = trade_over_line(sum_of(square_terms).astype(low_type))
         if head == heads - 1:
-            held = (part, slice_part, first_sums, second_sums, square_terms, enc_grad)
+            held = (part, slice_part, first_sums, second_sums, square_terms)
             held, parts, slice_parts = stage((held, parts, slice_parts))
-            part, slice_part, first_sums, second_sums, square_terms, enc_grad = held
+            part, slice_part, first_sums, second_sums, square_terms = held
         parts.append(exchange(part))
         slice_parts.append(slice_part)
 
@@ -864,9 +873,11 @@
         first_sums = double(first_sums, offset)
     square = double(sum_of(square_terms).astype(low_type)[None], near[0])
     small = hop(small, 1)
-    held = (first_sums, square, small)
+    enc_terms = product_right(own_pair_grad, head_ckv).astype(low_type)
+    held = (first_sums, square, small, enc_terms)
     parts, slice_parts, held = stage((parts, slice_parts, held))
-    first_sums, square, small = held
+    first_sums, square, small, enc_terms = held
+    enc_grad = scatter_rows(enc_terms)
 
     slice_parts = exchange_slices(slice_parts)
     for offset in near[1:]:

time: 717 us -> 709 us (0.989)
  waiting for transfers between devices: 202 us -> 188 us
    ppermute x52, waiting for transfers between devices: 90.2 us -> 83 us  [swap(): return lax.ppermute(values, axis, [(i, i ^ offset) for i in range(size)])]
    unnamed x207 -> x200, local copies, waits for them, and re-layouts: 26.5 us -> 27.2 us
  transfers between devices with their start and end apart: 75 -> 75, of which waited for: 28 -> 27; matrix products, arithmetic and copies ran while one was open for 30% -> 32% of each run, Pallas kernels for 19% -> 19%
where the time goes in v6:
time: 709 us; the launch traced here: 699 us
  waiting for transfers between devices  188 us (27%)
  Pallas kernels  131 us (18%)
  matrix products  124 us (17%)
  starting transfers between devices  97.5 us (14%)
  other arithmetic  73.6 us (10%)
  local copies, waits for them, and re-layouts  68.6 us (10%)
  between operations  16.2 us (2%)
    ppermute x52, waiting for transfers between devices, swap(): return lax.ppermute(values, axis, [(i, i ^ offset) for i in range(size)])  83 us
    ppermute x3, waiting for transfers between devices, shift(): lax.ppermute(values, 'line', [(i, (i + 1) % line) for i in range(line)])  62.7 us
    pallas_call x2, Pallas kernels, self_backward(): pl.pallas_call(functools.partial(self_backward_kernel, tok, width, group...  62.1 us
    dot_general x12, matrix products, product(): return jnp.dot(former, latter, preferred_element_type=jnp.float32)  47.3 us
    ppermute x52, starting transfers between devices, swap(): return lax.ppermute(values, axis, [(i, i ^ offset) for i in range(size)])  46.9 us
    pallas_call x2, Pallas kernels, self_forward(): pl.pallas_call(functools.partial(self_forward_kernel, tok, width, group /...  44.2 us
    dot_general x12, matrix products, product_right(): lax.dot_general(former, latter, (((1,), (1,)), ((), ())), preferred_eleme...  38.5 us
    dot_general x13, matrix products, product_left(): lax.dot_general(former, latter, (((0,), (0,)), ((), ())), preferred_eleme...  38.1 us
  transfers between devices with their start and end apart: 75, of which 27 were waited for; matrix products, arithmetic and copies ran while one was open for 32% of the time, Pallas kernels for 19%

profile of v6, /device:TPU:0, one launch (start us, length us, event | category | flops | bytes accessed | tf_op | source)
XLA Modules:
  0.0 698.6 jit_solution(7051902344743848208)
XLA Ops:
  27.9 14.8 %all-to-all-done = bf16[8,32,640]{2,1,0:T(8,128)(2,1)S(1)} async-done(((bf16[8,32,640]{2,1,0:T(8,128)(2,1)}), bf16[8,32,640]{2,1,0:T(8,128)(2,1)S(1)}, u32[]{:S(2)}, u32[]{:S(2)}) %all-to-all-start) | async-done | bytes 327712 | tf_op jit(solution)/shard_map/all_to_all | solution.py:507
  48.8 7.0 %collective-permute-done.4 = bf16[8,32,640]{2,1,0:T(8,128)(2,1)S(1)} collective-permute-done((bf16[8,32,640]{2,1,0:T(8,128)(2,1)S(1)}, bf16[8,32,640]{2,1,0:T(8,128)(2,1)S(1)}, u32[]{:S(2)}, u32[]{:S(2)}) %collective-permute-start.4) | collective-permute-done | bytes 327712 | tf_op jit(solution)/shard_map/ppermute | solution.py:403
  55.8 7.8 %collective-permute-done.5 = bf16[8,32,640]{2,1,0:T(8,128)(2,1)S(1)} collective-permute-done((bf16[8,32,640]{2,1,0:T(8,128)(2,1)S(1)}, bf16[8,32,640]{2,1,0:T(8,128)(2,1)S(1)}, u32[]{:S(2)}, u32[]{:S(2)}) %collective-permute-start.5) | collective-permute-done | bytes 327712 | tf_op jit(solution)/shard_map/ppermute | solution.py:403
  63.6 24.9 %collective-permute-done.3.refs_4_ = bf16[512,1024]{1,0:T(8,128)(2,1)} collective-permute-done((bf16[512,1024]{1,0:T(8,128)(2,1)S(1)}, bf16[512,1024]{1,0:T(8,128)(2,1)}, u32[]{:S(2)}, u32[]{:S(2)}) %collective-permute-start.3) | collective-permute-done | bytes 1048608 | tf_op jit(solution)/shard_map/ppermute | solution.py:495
  93.5 37.8 %collective-permute-done.8.refs_6_ = bf16[512,1024]{1,0:T(8,128)(2,1)} collective-permute-done((bf16[512,1024]{1,0:T(8,128)(2,1)}, bf16[512,1024]{1,0:T(8,128)(2,1)}, u32[]{:S(2)}, u32[]{:S(2)}) %collective-permute-start.8) | collective-permute-done | bytes 1048608 | tf_op jit(solution)/shard_map/ppermute | solution.py:495
  143.8 25.8 %self_forward.2 = (bf16[4096,384]{1,0:T(8,128)(2,1)}, bf16[8,64,512]{2,1,0:T(8,128)(2,1)}, f32[8,1,512]{2,1,0:T(1,128)S(1)}) custom-call(s32[8]{0:T(128)S(1)} %select_reduce_fusion.1.owner, s32[8]{0:T(128)S(1)} %select_reduce_fusion.slot_of, bf16[512,1024]{1,0:T(8,128)(2,1)} %refs_0_.2, bf16[512,1024]{1,0:T(8,128)(2,1)} %copy-done.21, ...), custom_call_target="tpu_custom_call" | custom-call | flops 1048576 | bytes 65536 | tf_op jit(solution)/shard_map/self_forward/pallas_call | solution.py:272
  185.9 18.4 %self_forward.3 = (bf16[8,64,512]{2,1,0:T(8,128)(2,1)}, f32[8,1,512]{2,1,0:T(1,128)S(1)}) custom-call(s32[8]{0:T(128)S(1)} %select_reduce_fusion.1.owner, s32[8]{0:T(128)S(1)} %select_reduce_fusion.slot_of, bf16[4096,384]{1,0:T(8,128)(2,1)} %get-tuple-element.196.refs_0_.refs_8_.refs_9_), custom_call_target="tpu_custom_call" | custom-call | flops 1048576 | bytes 65536 | tf_op jit(solution)/shard_map/self_forward/pallas_call | solution.py:272
  206.8 7.4 %all-to-all-done.1 = bf16[8,64,512]{2,1,0:T(8,128)(2,1)S(1)} async-done(((bf16[8,64,512]{2,1,0:T(8,128)(2,1)}), bf16[8,64,512]{2,1,0:T(8,128)(2,1)S(1)}, u32[]{:S(2)}, u32[]{:S(2)}) %all-to-all-start.1) | async-done | bytes 524320 | tf_op jit(solution)/shard_map/all_to_all | solution.py:507
  220.9 5.3 maximum_select_fusion
  244.1 10.9 %cross_forward.1 = (bf16[512,1024]{1,0:T(8,128)(2,1)S(1)}, f32[8,8,512]{2,1,0:T(8,128)S(1)}) custom-call(bf16[512,1024]{1,0:T(8,128)(2,1)S(1)} %multiply_convert_fusion.8.query, bf16[8,2,512,128]{3,2,1,0:T(8,128)(2,1)S(1)} %bitcast.317), custom_call_target="tpu_custom_call" | custom-call | flops 1048576 | bytes 65536 | tf_op jit(solution)/shard_map/cross_forward/pallas_call | solution.py:363
  255.0 8.1 %collective-permute-done.18 = bf16[1024,512]{0,1:T(8,128)(2,1)} collective-permute-done((bf16[1024,512]{0,1:T(8,128)(2,1)}, bf16[1024,512]{0,1:T(8,128)(2,1)}, u32[]{:S(2)}, u32[]{:S(2)}) %collective-permute-start.18) | collective-permute-done | bytes 1048608 | tf_op jit(solution)/shard_map/ppermute | solution.py:403
  268.2 6.2 multiply_convert_fusion.5
  275.7 13.5 %multiply_convert_fusion.7 = (bf16[1024,512]{1,0:T(8,128)(2,1)S(1)}, f32[1024,512]{1,0:T(8,128)}) fusion(f32[512]{0:T(512)S(1)} %bitcast.418, bf16[1024,512]{0,1:T(8,128)(2,1)S(1)} %copy-done.45, bf16[512,1024]{1,0:T(8,128)(2,1)S(1)} %collective-permute-done.20, bf16[512,1024]{1,0:T(8,128)(2,1)S(1)} %fusion.10), kind=kOutput, calls=%fused_computation.65 | convolution fusion | flops 1090519040 | bytes 6293504 | tf_op jit(solution)/shard_map/dot_general | solution.py:29
  292.1 5.9 multiply_convert_fusion.6
  301.0 4.7 multiply_convert_fusion.4
  378.4 5.2 collective-permute-done.26
  404.0 13.9 %cross_backward.1 = (bf16[512,1024]{1,0:T(8,128)(2,1)S(1)}, bf16[8,2,512,128]{3,2,1,0:T(8,128)(2,1)}) custom-call(bf16[512,1024]{1,0:T(8,128)(2,1)S(1)} %copy-done.5, bf16[8,2,512,128]{3,2,1,0:T(8,128)(2,1)S(1)} %bitcast.318, bf16[512,1024]{1,0:T(8,128)(2,1)S(1)} %convolution_convert_fusion.5.mixed_grad, bf16[512,1024]{1,0:T(8,128)(2,1)S(1)} %copy-done.9, ...), custom_call_target="tpu_custom_call" | custom-call | flops 1048576 | bytes 65536 | tf_op jit(solution)/shard_map/cross_backward/pallas_call | solution.py:385
  418.9 5.1 multiply_reduce_fusion.1
  463.5 4.5 fusion
  469.9 6.7 all-to-all-done.3.refs_9_
  476.5 6.5 collective-permute-done.33
  489.3 4.8 all-to-all-start.4
  499.7 30.4 %self_backward.2 = (bf16[8,192,512]{2,1,0:T(8,128)(2,1)}, f32[192,1152]{1,0:T(8,128)S(1)}) custom-call(s32[8]{0:T(128)S(1)} %copy-done.12, s32[8]{0:T(128)S(1)} %copy-done.14, bf16[512,1024]{1,0:T(8,128)(2,1)} %refs_0_.2, bf16[512,1024]{1,0:T(8,128)(2,1)} %copy-done.21, bf16[512,1024]{1,0:T(8,128)(2,1)} %copy-done.20, ...), custom_call_target="tpu_custom_call" | custom-call | flops 1048576 | bytes 65536 | tf_op jit(solution)/shard_map/self_backward/pallas_call | solution.py:301
  530.0 8.2 %collective-permute-done.39 = f32[14,1024]{1,0:T(8,128)S(1)} collective-permute-done((f32[14,1024]{1,0:T(8,128)S(1)}, f32[14,1024]{1,0:T(8,128)S(1)}, u32[]{:S(2)}, u32[]{:S(2)}) %collective-permute-start.39) | collective-permute-done | bytes 57376 | tf_op jit(solution)/shard_map/ppermute | solution.py:403
  539.1 4.9 all-to-all-start.5
  555.1 31.7 %self_backward.3 = (bf16[8,192,512]{2,1,0:T(8,128)(2,1)}, f32[1152,384]{1,0:T(8,128)}) custom-call(s32[8]{0:T(128)S(1)} %copy-done.12, s32[8]{0:T(128)S(1)} %copy-done.14, bf16[512,1024]{1,0:T(8,128)(2,1)} %refs_0_.2, bf16[512,1024]{1,0:T(8,128)(2,1)} %copy-done.21, bf16[512,1024]{1,0:T(8,128)(2,1)} %copy-done.20, ...), custom_call_target="tpu_custom_call" | custom-call | flops 1048576 | bytes 65536 | tf_op jit(solution)/shard_map/self_backward/pallas_call | solution.py:301
  587.8 7.0 %collective-permute-done.43 = bf16[3,32,1024]{2,1,0:T(8,128)(2,1)S(1)} collective-permute-done((bf16[3,32,1024]{2,1,0:T(8,128)(2,1)S(1)}, bf16[3,32,1024]{2,1,0:T(8,128)(2,1)S(1)}, u32[]{:S(2)}, u32[]{:S(2)}) %collective-permute-start.43) | collective-permute-done | bytes 196640 | tf_op jit(solution)/shard_map/ppermute | solution.py:475
  595.5 6.3 all-to-all-start.6
  618.7 13.5 %collective-permute-done.49 = bf16[1,3,32,1024]{3,2,1,0:T(8,128)(2,1)S(1)} collective-permute-done((bf16[1,3,32,1024]{3,2,1,0:T(8,128)(2,1)S(1)}, bf16[1,3,32,1024]{3,2,1,0:T(8,128)(2,1)S(1)}, u32[]{:S(2)}, u32[]{:S(2)}) %collective-permute-start.49) | collective-permute-done | bytes 196640 | tf_op jit(solution)/shard_map/ppermute | solution.py:403
  632.2 7.9 %collective-permute-done.48 = bf16[2,128,1024]{2,1,0:T(8,128)(2,1)S(1)} collective-permute-done((bf16[2,128,1024]{2,1,0:T(8,128)(2,1)S(1)}, bf16[2,128,1024]{2,1,0:T(8,128)(2,1)S(1)}, u32[]{:S(2)}, u32[]{:S(2)}) %collective-permute-start.48) | collective-permute-done | bytes 524320 | tf_op jit(solution)/shard_map/ppermute | solution.py:403
  643.3 4.7 all-to-all-start.7
  653.8 8.5 %bitcast_add_fusion = f32[512,1024]{1,0:T(8,128)} fusion(f32[512,1024]{1,0:T(8,128)S(1)} %copy-done.24, bf16[8,2,192,1024]{3,2,1,0:T(8,128)(2,1)} %bitcast.423, f32[512]{0:T(512)S(1)} %negate_multiply_fusion, bf16[8,1,192,512]{3,2,0,1:T(8,128)(2,1)} %bitcast.112, bf16[8,1,192,512]{3,2,0,1:T(8,128)(2,1)} %bitcast.111), kind=kOutput, calls=%fused_computation.36 | convolution fusion | flops 3223846912 | bytes 13633536 | tf_op jit(solution)/shard_map/dot_general | solution.py:33
  (544 shorter events, 313.9 us)
Async XLA Ops:
  7.2 35.5 %collective-permute-start = (bf16[512,1024]{1,0:T(8,128)(2,1)}, bf16[512,1024]{1,0:T(8,128)(2,1)S(1)}, u32[]{:S(2)}, u32[]{:S(2)}) collective-permute-start(bf16[512,1024]{1,0:T(8,128)(2,1)} %refs_0_.2), channel_id=1, source_target_pairs={{0,2},{2,4},{4,6},{6,0},{1,3},{3,5},{5,7},{7,1},{8,10},{10,12},{12... | collective-permute-start | bytes 3145736 | tf_op jit(solution)/shard_map/ppermute | solution.py:495
  19.3 112.0 %all-gather.7.cloned.1.call-start = ((), (), s32[]{:S(2)}) async-start(), calls=%async_computation.12 | async-start | bytes 2293760 | tf_op jit(solution)/shard_map/all_gather | solution.py:609
  45.0 89.2 %all-gather.9.cloned.1.call-start = ((), (), s32[]{:S(2)}) async-start(), calls=%async_computation.13 | async-start | bytes 1179648 | tf_op jit(solution)/shard_map/all_gather | solution.py:499
  45.1 43.4 %collective-permute-start.3 = (bf16[512,1024]{1,0:T(8,128)(2,1)S(1)}, bf16[512,1024]{1,0:T(8,128)(2,1)}, u32[]{:S(2)}, u32[]{:S(2)}) collective-permute-start(bf16[512,1024]{1,0:T(8,128)(2,1)S(1)} %collective-permute-done.refs_2_), channel_id=1, source_target_pairs={{0,2},{2,4},{4,6},{6,0},{1,3},{3,5},{5,7},{7,1},{8,10},{10,12},{12... | collective-permute-start | bytes 3145736 | tf_op jit(solution)/shard_map/ppermute | solution.py:495
  45.2 43.3 %collective-permute-start.7 = (bf16[512,1024]{1,0:T(8,128)(2,1)S(1)}, bf16[512,1024]{1,0:T(8,128)(2,1)}, u32[]{:S(2)}, u32[]{:S(2)}) collective-permute-start(bf16[512,1024]{1,0:T(8,128)(2,1)S(1)} %collective-permute-done.refs_2_), channel_id=1, source_target_pairs={{0,1},{1,0},{2,3},{3,2},{4,5},{5,4},{6,7},{7,6},{8,9},{9,8},{10,11... | collective-permute-start | bytes 3145736 | tf_op jit(solution)/shard_map/ppermute | solution.py:403
  88.5 118.3 %all-gather.11.cloned.1.call-start = ((), (), s32[]{:S(2)}) async-start(), calls=%async_computation.14 | async-start | bytes 1310720 | tf_op jit(solution)/shard_map/all_gather | solution.py:629
  88.6 42.7 %collective-permute-start.8 = (bf16[512,1024]{1,0:T(8,128)(2,1)}, bf16[512,1024]{1,0:T(8,128)(2,1)}, u32[]{:S(2)}, u32[]{:S(2)}) collective-permute-start(bf16[512,1024]{1,0:T(8,128)(2,1)} %collective-permute-done.3.refs_4_), channel_id=1, source_target_pairs={{0,2},{2,4},{4,6},{6,0},{1,3},{3,5},{5,7},{7,1},{8,10},{10,12},{12... | collective-permute-start | bytes 3145736 | tf_op jit(solution)/shard_map/ppermute | solution.py:495
  92.7 38.6 %collective-permute-start.9 = (bf16[512,1024]{1,0:T(8,128)(2,1)}, bf16[512,1024]{1,0:T(8,128)(2,1)}, u32[]{:S(2)}, u32[]{:S(2)}) collective-permute-start(bf16[512,1024]{1,0:T(8,128)(2,1)} %collective-permute-done.3.refs_4_), channel_id=1, source_target_pairs={{0,1},{1,0},{2,3},{3,2},{4,5},{5,4},{6,7},{7,6},{8,9},{9,8},{10,11... | collective-permute-start | bytes 3145736 | tf_op jit(solution)/shard_map/ppermute | solution.py:403
  137.2 36.4 %collective-permute-start.12 = (bf16[4,96,1024]{2,1,0:T(8,128)(2,1)S(1)}, bf16[4,96,1024]{2,1,0:T(8,128)(2,1)}, u32[]{:S(2)}, u32[]{:S(2)}) collective-permute-start(bf16[4,96,1024]{2,1,0:T(8,128)(2,1)S(1)} %slice.246), channel_id=1, source_target_pairs={{0,16},{8,24},{16,0},{24,8},{1,17},{9,25},{17,1},{25,9},{2,18},{10... | collective-permute-start | bytes 2359304 | tf_op jit(solution)/shard_map/ppermute | solution.py:403
  138.8 34.9 %collective-permute-start.13 = (bf16[4,96,1024]{2,1,0:T(8,128)(2,1)S(1)}, bf16[4,96,1024]{2,1,0:T(8,128)(2,1)}, u32[]{:S(2)}, u32[]{:S(2)}) collective-permute-start(bf16[4,96,1024]{2,1,0:T(8,128)(2,1)S(1)} %slice.246), channel_id=1, source_target_pairs={{0,24},{8,16},{16,8},{24,0},{1,25},{9,17},{17,9},{25,1},{2,26},{10... | collective-permute-start | bytes 2359304 | tf_op jit(solution)/shard_map/ppermute | solution.py:403
  140.1 93.0 %all-gather.15.cloned.1.call-start = ((), (), s32[]{:S(2)}) async-start(), calls=%async_computation.20 | async-start | bytes 2359296 | tf_op jit(solution)/shard_map/all_gather | solution.py:665
  177.7 36.4 %collective-permute-start.14 = (bf16[4,4,96,1024]{3,2,1,0:T(8,128)(2,1)}, bf16[4,4,96,1024]{3,2,1,0:T(8,128)(2,1)}, u32[]{:S(2)}, u32[]{:S(2)}) collective-permute-start(bf16[4,4,96,1024]{3,2,1,0:T(8,128)(2,1)} %pad_maximum_fusion.1), channel_id=1, source_target_pairs={{0,1},{1,0},{2,3},{3,2},{4,5},{5,4},{6,7},{7,6},{8,9},{9,8},{10,11... | collective-permute-start | bytes 9437192 | tf_op jit(solution)/shard_map/ppermute | solution.py:403
  214.2 40.8 %collective-permute-start.17 = (bf16[1024,512]{0,1:T(8,128)(2,1)}, bf16[1024,512]{0,1:T(8,128)(2,1)}, u32[]{:S(2)}, u32[]{:S(2)}) collective-permute-start(bf16[1024,512]{0,1:T(8,128)(2,1)} %all-gather.11.cloned.1.call-done), channel_id=1, source_target_pairs={{0,8},{8,0},{16,24},{24,16},{1,9},{9,1},{17,25},{25,17},{2,10},{10... | collective-permute-start | bytes 3145736 | tf_op jit(solution)/shard_map/ppermute | solution.py:403
  215.6 47.5 %collective-permute-start.18 = (bf16[1024,512]{0,1:T(8,128)(2,1)}, bf16[1024,512]{0,1:T(8,128)(2,1)}, u32[]{:S(2)}, u32[]{:S(2)}) collective-permute-start(bf16[1024,512]{0,1:T(8,128)(2,1)} %all-gather.11.cloned.1.call-done), channel_id=1, source_target_pairs={{0,16},{8,24},{16,0},{24,8},{1,17},{9,25},{17,1},{25,9},{2,18},{10... | collective-permute-start | bytes 3145736 | tf_op jit(solution)/shard_map/ppermute | solution.py:403
  220.8 198.1 %all-gather.13.cloned.1.call-start = ((), (), s32[]{:S(2)}) async-start(), calls=%async_computation.15 | async-start | bytes 7077888 | tf_op jit(solution)/shard_map/all_gather | solution.py:499
  323.3 146.5 %reduce-scatter.5.cloned.1.call-start = ((), (), s32[]{:S(2)}) async-start(), calls=%async_computation.16 | async-start | bytes 1310720 | tf_op jit(solution)/shard_map/reduce_scatter | solution.py:722
  400.5 138.5 %reduce-scatter.9.cloned.1.call-start = ((), (), s32[]{:S(2)}) async-start(), calls=%async_computation.18 | async-start | bytes 2359296 | tf_op jit(solution)/shard_map/reduce_scatter | solution.py:734
  453.4 85.6 %reduce-scatter.7.cloned.1.call-start = ((), (), s32[]{:S(2)}) async-start(), calls=%async_computation.17 | async-start | bytes 1310720 | tf_op jit(solution)/shard_map/reduce_scatter | solution.py:797
  489.3 49.7 %all-to-all-start.4 = ((bf16[8,64,512]{2,1,0:T(8,128)(2,1)}), bf16[8,64,512]{2,1,0:T(8,128)(2,1)S(1)}, u32[]{:S(2)}, u32[]{:S(2)}) async-start(bf16[8,64,512]{2,1,0:T(8,128)(2,1)} %get-tuple-element.419), calls=%async_computation.6 | async-start | bytes 1048576 | tf_op jit(solution)/shard_map/all_to_all | solution.py:507
  494.1 44.8 %collective-permute-start.36 = (bf16[4,3,32,1024]{3,2,0,1:T(8,128)(2,1)}, bf16[4,3,32,1024]{3,2,0,1:T(8,128)(2,1)S(1)}, u32[]{:S(2)}, u32[]{:S(2)}) collective-permute-start(bf16[4,3,32,1024]{3,2,0,1:T(8,128)(2,1)} %get-tuple-element.269), channel_id=1, source_target_pairs={{0,8},{8,0},{16,24},{24,16},{1,9},{9,1},{17,25},{25,17},{2,10},{10... | collective-permute-start | bytes 2359304 | tf_op jit(solution)/shard_map/ppermute | solution.py:403
  494.8 44.1 %collective-permute-start.37 = (bf16[4,3,32,1024]{3,2,0,1:T(8,128)(2,1)}, bf16[4,3,32,1024]{3,2,0,1:T(8,128)(2,1)}, u32[]{:S(2)}, u32[]{:S(2)}) collective-permute-start(bf16[4,3,32,1024]{3,2,0,1:T(8,128)(2,1)} %get-tuple-element.270), channel_id=1, source_target_pairs={{0,16},{8,24},{16,0},{24,8},{1,17},{9,25},{17,1},{25,9},{2,18},{10... | collective-permute-start | bytes 2359304 | tf_op jit(solution)/shard_map/ppermute | solution.py:403
  496.2 42.8 %collective-permute-start.38 = (bf16[4,3,32,1024]{3,2,0,1:T(8,128)(2,1)}, bf16[4,3,32,1024]{3,2,0,1:T(8,128)(2,1)}, u32[]{:S(2)}, u32[]{:S(2)}) collective-permute-start(bf16[4,3,32,1024]{3,2,0,1:T(8,128)(2,1)} %get-tuple-element.271), channel_id=1, source_target_pairs={{0,24},{8,16},{16,8},{24,0},{1,25},{9,17},{17,9},{25,1},{2,26},{10... | collective-permute-start | bytes 2359304 | tf_op jit(solution)/shard_map/ppermute | solution.py:403
  497.6 41.3 %collective-permute-start.35 = (bf16[1,128,1024]{2,1,0:T(8,128)(2,1)S(1)}, bf16[1,128,1024]{2,1,0:T(8,128)(2,1)S(1)}, u32[]{:S(2)}, u32[]{:S(2)}) collective-permute-start(bf16[1,128,1024]{2,1,0:T(8,128)(2,1)S(1)} %bitcast.374), channel_id=1, source_target_pairs={{0,8},{8,0},{16,24},{24,16},{1,9},{9,1},{17,25},{25,17},{2,10},{10... | collective-permute-start | bytes 786440 | tf_op jit(solution)/shard_map/ppermute | solution.py:403
  498.3 39.9 %collective-permute-start.39 = (f32[14,1024]{1,0:T(8,128)S(1)}, f32[14,1024]{1,0:T(8,128)S(1)}, u32[]{:S(2)}, u32[]{:S(2)}) collective-permute-start(f32[14,1024]{1,0:T(8,128)S(1)} %add.525), channel_id=1, source_target_pairs={{0,8},{8,0},{16,24},{24,16},{1,9},{9,1},{17,25},{25,17},{2,10},{10... | collective-permute-start | bytes 172040 | tf_op jit(solution)/shard_map/ppermute | solution.py:403
  539.1 56.5 %all-to-all-start.5 = ((bf16[8,192,512]{2,1,0:T(8,128)(2,1)}), bf16[8,192,512]{2,1,0:T(8,128)(2,1)}, u32[]{:S(2)}, u32[]{:S(2)}) async-start(bf16[8,192,512]{2,1,0:T(8,128)(2,1)} %get-tuple-element.286), calls=%async_computation.8 | async-start | bytes 3145728 | tf_op jit(solution)/shard_map/all_to_all | solution.py:507
  544.4 42.5 %collective-permute-start.40 = (bf16[1,128,1024]{2,1,0:T(8,128)(2,1)S(1)}, bf16[1,128,1024]{2,1,0:T(8,128)(2,1)S(1)}, u32[]{:S(2)}, u32[]{:S(2)}) collective-permute-start(bf16[1,128,1024]{2,1,0:T(8,128)(2,1)S(1)} %reshape.810), channel_id=1, source_target_pairs={{0,8},{8,0},{16,24},{24,16},{1,9},{9,1},{17,25},{25,17},{2,10},{10... | collective-permute-start | bytes 786440 | tf_op jit(solution)/shard_map/ppermute | solution.py:403
  545.2 42.5 %collective-permute-start.41 = (bf16[2,128,1024]{2,1,0:T(8,128)(2,1)S(1)}, bf16[2,128,1024]{2,1,0:T(8,128)(2,1)S(1)}, u32[]{:S(2)}, u32[]{:S(2)}) collective-permute-start(bf16[2,128,1024]{2,1,0:T(8,128)(2,1)S(1)} %pad_maximum_fusion.23), channel_id=1, source_target_pairs={{0,16},{8,24},{16,0},{24,8},{1,17},{9,25},{17,1},{25,9},{2,18},{10... | collective-permute-start | bytes 1572872 | tf_op jit(solution)/shard_map/ppermute | solution.py:403
  549.0 38.8 %collective-permute-start.42 = (bf16[3,32,1024]{2,1,0:T(8,128)(2,1)S(1)}, bf16[3,32,1024]{2,1,0:T(8,128)(2,1)S(1)}, u32[]{:S(2)}, u32[]{:S(2)}) collective-permute-start(bf16[3,32,1024]{2,1,0:T(8,128)(2,1)S(1)} %get-tuple-element.433), channel_id=1, source_target_pairs={{0,2},{2,4},{4,6},{6,0},{1,3},{3,5},{5,7},{7,1},{8,10},{10,12},{12... | collective-permute-start | bytes 589832 | tf_op jit(solution)/shard_map/ppermute | solution.py:475
  551.1 43.7 %collective-permute-start.43 = (bf16[3,32,1024]{2,1,0:T(8,128)(2,1)S(1)}, bf16[3,32,1024]{2,1,0:T(8,128)(2,1)S(1)}, u32[]{:S(2)}, u32[]{:S(2)}) collective-permute-start(bf16[3,32,1024]{2,1,0:T(8,128)(2,1)S(1)} %get-tuple-element.432), channel_id=1, source_target_pairs={{0,4},{2,6},{4,0},{6,2},{1,5},{3,7},{5,1},{7,3},{8,12},{10,14},{12... | collective-permute-start | bytes 589832 | tf_op jit(solution)/shard_map/ppermute | solution.py:475
  553.5 42.1 %collective-permute-start.44 = (bf16[3,32,1024]{2,1,0:T(8,128)(2,1)S(1)}, bf16[3,32,1024]{2,1,0:T(8,128)(2,1)}, u32[]{:S(2)}, u32[]{:S(2)}) collective-permute-start(bf16[3,32,1024]{2,1,0:T(8,128)(2,1)S(1)} %get-tuple-element.431), channel_id=1, source_target_pairs={{0,6},{2,0},{4,2},{6,4},{1,7},{3,1},{5,3},{7,5},{8,14},{10,8},{12,... | collective-permute-start | bytes 589832 | tf_op jit(solution)/shard_map/ppermute | solution.py:475
  595.5 45.5 %all-to-all-start.6 = ((bf16[8,192,512]{2,1,0:T(8,128)(2,1)}), bf16[8,192,512]{2,1,0:T(8,128)(2,1)}, u32[]{:S(2)}, u32[]{:S(2)}) async-start(bf16[8,192,512]{2,1,0:T(8,128)(2,1)} %get-tuple-element.288), calls=%async_computation.9 | async-start | bytes 3145728 | tf_op jit(solution)/shard_map/all_to_all | solution.py:507
  648.1 41.9 %reduce-scatter.11.cloned.1.call-start = ((), (), s32[]{:S(2)}) async-start(), calls=%async_computation.19 | async-start | bytes 1179648 | tf_op jit(solution)/shard_map/reduce_scatter | solution.py:503
  (137 other events, 1817.3 us)
Sparse Core Ops, SparseCore 0:
  45.2 60.5 all-gather.6
  107.3 26.8 all-gather.8
  140.2 29.0 all-gather.10
  177.9 38.9 all-gather.14
  323.5 62.3 all-gather.12
  400.6 25.0 reduce-scatter.4
  437.5 38.8 reduce-scatter.8
  489.4 36.9 reduce-scatter.6
  653.9 32.0 reduce-scatter.10

commit v7 on v6

--- a/solution.py
+++ b/solution.py
@@ -749,10 +749,16 @@
     bias_cross_q = column_sums(cross_q_grad)
     bias_cross_out = column_sums(cross_out_grad)
 
-    square = jnp.stack([part_self_out, part_cross_q, part_cross_out], 0)
-    square = square.reshape(3, line, 2, reps, weight_rows // reps, model)
-    square_own = lax.dynamic_index_in_dim(square, core, 2, keepdims=False)
-    square_other = swap(lax.dynamic_index_in_dim(square, 1 - core, 2, keepdims=False), "core", 1)
+    square = [
+        part.reshape(line, 2, reps, part_rows, model)
+        for part in (part_self_out, part_cross_q, part_cross_out)
+    ]
+
+    def of_core(index):
+        rows = [lax.dynamic_index_in_dim(part, index, 1, keepdims=False) for part in square]
+        return jnp.stack(rows, 0)
+
+    square_own, square_other = of_core(core), swap(of_core(1 - core), "core", 1)
 
     bias_parts = jnp.stack([part.reshape(line, unit) for part in rep_order(bias_parts)], 1)
     bias_fc1 = jnp.where(

time: 709 us -> 706 us (level)
  no operation moved by 1% of the time
where the time goes in v7:
time: 706 us; the launch traced here: 695 us
  waiting for transfers between devices  189 us (27%)
  Pallas kernels  131 us (19%)
  matrix products  120 us (17%)
  starting transfers between devices  97.6 us (14%)
  other arithmetic  73.1 us (10%)
  local copies, waits for them, and re-layouts  68.8 us (10%)
  between operations  16.3 us (2%)
    ppermute x52, waiting for transfers between devices, swap(): return lax.ppermute(values, axis, [(i, i ^ offset) for i in range(size)])  82.7 us
    ppermute x3, waiting for transfers between devices, shift(): lax.ppermute(values, 'line', [(i, (i + 1) % line) for i in range(line)])  62.7 us
    pallas_call x2, Pallas kernels, self_backward(): pl.pallas_call(functools.partial(self_backward_kernel, tok, width, group...  62.1 us
    ppermute x52, starting transfers between devices, swap(): return lax.ppermute(values, axis, [(i, i ^ offset) for i in range(size)])  47 us
    dot_general x12, matrix products, product(): return jnp.dot(former, latter, preferred_element_type=jnp.float32)  46 us
    pallas_call x2, Pallas kernels, self_forward(): pl.pallas_call(functools.partial(self_forward_kernel, tok, width, group /...  44.2 us
    dot_general x12, matrix products, product_right(): lax.dot_general(former, latter, (((1,), (1,)), ((), ())), preferred_eleme...  38.6 us
    all_to_all x8, starting transfers between devices, exchange(): lax.all_to_all(values, SHARD, split_axis=0, concat_axis=0, tiled=True)  36.1 us
  transfers between devices with their start and end apart: 75, of which 27 were waited for; matrix products, arithmetic and copies ran while one was open for 32% of the time, Pallas kernels for 19%

profile of v7, /device:TPU:0, one launch (start us, length us, event | category | flops | bytes accessed | tf_op | source)
XLA Modules:
  0.0 695.5 jit_solution(4841912881460232401)
XLA Ops:
  27.9 14.8 %all-to-all-done = bf16[8,32,640]{2,1,0:T(8,128)(2,1)S(1)} async-done(((bf16[8,32,640]{2,1,0:T(8,128)(2,1)}), bf16[8,32,640]{2,1,0:T(8,128)(2,1)S(1)}, u32[]{:S(2)}, u32[]{:S(2)}) %all-to-all-start) | async-done | bytes 327712 | tf_op jit(solution)/shard_map/all_to_all | solution.py:507
  48.8 7.0 %collective-permute-done.4 = bf16[8,32,640]{2,1,0:T(8,128)(2,1)S(1)} collective-permute-done((bf16[8,32,640]{2,1,0:T(8,128)(2,1)S(1)}, bf16[8,32,640]{2,1,0:T(8,128)(2,1)S(1)}, u32[]{:S(2)}, u32[]{:S(2)}) %collective-permute-start.4) | collective-permute-done | bytes 327712 | tf_op jit(solution)/shard_map/ppermute | solution.py:403
  55.8 7.8 %collective-permute-done.5 = bf16[8,32,640]{2,1,0:T(8,128)(2,1)S(1)} collective-permute-done((bf16[8,32,640]{2,1,0:T(8,128)(2,1)S(1)}, bf16[8,32,640]{2,1,0:T(8,128)(2,1)S(1)}, u32[]{:S(2)}, u32[]{:S(2)}) %collective-permute-start.5) | collective-permute-done | bytes 327712 | tf_op jit(solution)/shard_map/ppermute | solution.py:403
  63.6 24.9 %collective-permute-done.3.refs_4_ = bf16[512,1024]{1,0:T(8,128)(2,1)} collective-permute-done((bf16[512,1024]{1,0:T(8,128)(2,1)S(1)}, bf16[512,1024]{1,0:T(8,128)(2,1)}, u32[]{:S(2)}, u32[]{:S(2)}) %collective-permute-start.3) | collective-permute-done | bytes 1048608 | tf_op jit(solution)/shard_map/ppermute | solution.py:495
  93.5 37.8 %collective-permute-done.8.refs_6_ = bf16[512,1024]{1,0:T(8,128)(2,1)} collective-permute-done((bf16[512,1024]{1,0:T(8,128)(2,1)}, bf16[512,1024]{1,0:T(8,128)(2,1)}, u32[]{:S(2)}, u32[]{:S(2)}) %collective-permute-start.8) | collective-permute-done | bytes 1048608 | tf_op jit(solution)/shard_map/ppermute | solution.py:495
  143.7 25.8 %self_forward.2 = (bf16[4096,384]{1,0:T(8,128)(2,1)}, bf16[8,64,512]{2,1,0:T(8,128)(2,1)}, f32[8,1,512]{2,1,0:T(1,128)S(1)}) custom-call(s32[8]{0:T(128)S(1)} %select_reduce_fusion.1.owner, s32[8]{0:T(128)S(1)} %select_reduce_fusion.slot_of, bf16[512,1024]{1,0:T(8,128)(2,1)} %refs_0_.2, bf16[512,1024]{1,0:T(8,128)(2,1)} %copy-done.20, ...), custom_call_target="tpu_custom_call" | custom-call | flops 1048576 | bytes 65536 | tf_op jit(solution)/shard_map/self_forward/pallas_call | solution.py:272
  185.9 18.4 %self_forward.3 = (bf16[8,64,512]{2,1,0:T(8,128)(2,1)}, f32[8,1,512]{2,1,0:T(1,128)S(1)}) custom-call(s32[8]{0:T(128)S(1)} %select_reduce_fusion.1.owner, s32[8]{0:T(128)S(1)} %select_reduce_fusion.slot_of, bf16[4096,384]{1,0:T(8,128)(2,1)} %get-tuple-element.196.refs_0_.refs_8_.refs_9_), custom_call_target="tpu_custom_call" | custom-call | flops 1048576 | bytes 65536 | tf_op jit(solution)/shard_map/self_forward/pallas_call | solution.py:272
  206.8 7.4 %all-to-all-done.1 = bf16[8,64,512]{2,1,0:T(8,128)(2,1)S(1)} async-done(((bf16[8,64,512]{2,1,0:T(8,128)(2,1)}), bf16[8,64,512]{2,1,0:T(8,128)(2,1)S(1)}, u32[]{:S(2)}, u32[]{:S(2)}) %all-to-all-start.1) | async-done | bytes 524320 | tf_op jit(solution)/shard_map/all_to_all | solution.py:507
  220.9 5.7 maximum_select_fusion
  244.1 10.9 %cross_forward.1 = (bf16[512,1024]{1,0:T(8,128)(2,1)S(1)}, f32[8,8,512]{2,1,0:T(8,128)S(1)}) custom-call(bf16[512,1024]{1,0:T(8,128)(2,1)S(1)} %multiply_convert_fusion.8.query, bf16[8,2,512,128]{3,2,1,0:T(8,128)(2,1)S(1)} %bitcast.336), custom_call_target="tpu_custom_call" | custom-call | flops 1048576 | bytes 65536 | tf_op jit(solution)/shard_map/cross_forward/pallas_call | solution.py:363
  255.0 8.1 %collective-permute-done.18 = bf16[1024,512]{0,1:T(8,128)(2,1)} collective-permute-done((bf16[1024,512]{0,1:T(8,128)(2,1)}, bf16[1024,512]{0,1:T(8,128)(2,1)}, u32[]{:S(2)}, u32[]{:S(2)}) %collective-permute-start.18) | collective-permute-done | bytes 1048608 | tf_op jit(solution)/shard_map/ppermute | solution.py:403
  268.2 6.2 multiply_convert_fusion.5
  275.7 13.5 %multiply_convert_fusion.7 = (bf16[1024,512]{1,0:T(8,128)(2,1)S(1)}, f32[1024,512]{1,0:T(8,128)}) fusion(f32[512]{0:T(512)S(1)} %bitcast.437, bf16[1024,512]{0,1:T(8,128)(2,1)S(1)} %copy-done.45, bf16[512,1024]{1,0:T(8,128)(2,1)S(1)} %collective-permute-done.20, bf16[512,1024]{1,0:T(8,128)(2,1)S(1)} %fusion.9), kind=kOutput, calls=%fused_computation.63 | convolution fusion | flops 1090519040 | bytes 6293504 | tf_op jit(solution)/shard_map/dot_general | solution.py:29
  292.1 5.9 multiply_convert_fusion.6
  301.0 4.7 multiply_convert_fusion.4
  339.7 4.3 convert_reduce_fusion.3
  378.4 5.2 collective-permute-done.26
  404.0 13.9 %cross_backward.1 = (bf16[512,1024]{1,0:T(8,128)(2,1)S(1)}, bf16[8,2,512,128]{3,2,1,0:T(8,128)(2,1)}) custom-call(bf16[512,1024]{1,0:T(8,128)(2,1)S(1)} %copy-done.5, bf16[8,2,512,128]{3,2,1,0:T(8,128)(2,1)S(1)} %bitcast.337, bf16[512,1024]{1,0:T(8,128)(2,1)S(1)} %convolution_convert_fusion.5.mixed_grad, bf16[512,1024]{1,0:T(8,128)(2,1)S(1)} %copy-done.9, ...), custom_call_target="tpu_custom_call" | custom-call | flops 1048576 | bytes 65536 | tf_op jit(solution)/shard_map/cross_backward/pallas_call | solution.py:385
  418.9 5.1 multiply_reduce_fusion.1
  465.4 8.2 %all-to-all-done.3.refs_9_ = bf16[8,64,512]{2,1,0:T(8,128)(2,1)S(1)} async-done(((bf16[8,64,512]{2,1,0:T(8,128)(2,1)}), bf16[8,64,512]{2,1,0:T(8,128)(2,1)S(1)}, u32[]{:S(2)}, u32[]{:S(2)}) %all-to-all-start.3) | async-done | bytes 524320 | tf_op jit(solution)/shard_map/all_to_all | solution.py:507
  473.7 6.3 collective-permute-done.33
  486.1 4.8 all-to-all-start.4
  496.5 30.4 %self_backward.2 = (bf16[8,192,512]{2,1,0:T(8,128)(2,1)}, f32[192,1152]{1,0:T(8,128)S(1)}) custom-call(s32[8]{0:T(128)S(1)} %copy-done.12, s32[8]{0:T(128)S(1)} %copy-done.14, bf16[512,1024]{1,0:T(8,128)(2,1)} %refs_0_.2, bf16[512,1024]{1,0:T(8,128)(2,1)} %copy-done.20, bf16[512,1024]{1,0:T(8,128)(2,1)} %copy-done.19, ...), custom_call_target="tpu_custom_call" | custom-call | flops 1048576 | bytes 65536 | tf_op jit(solution)/shard_map/self_backward/pallas_call | solution.py:301
  526.9 8.2 %collective-permute-done.39 = f32[14,1024]{1,0:T(8,128)S(1)} collective-permute-done((f32[14,1024]{1,0:T(8,128)S(1)}, f32[14,1024]{1,0:T(8,128)S(1)}, u32[]{:S(2)}, u32[]{:S(2)}) %collective-permute-start.39) | collective-permute-done | bytes 57376 | tf_op jit(solution)/shard_map/ppermute | solution.py:403
  535.9 4.9 all-to-all-start.5
  551.9 31.7 %self_backward.3 = (bf16[8,192,512]{2,1,0:T(8,128)(2,1)}, f32[1152,384]{1,0:T(8,128)}) custom-call(s32[8]{0:T(128)S(1)} %copy-done.12, s32[8]{0:T(128)S(1)} %copy-done.14, bf16[512,1024]{1,0:T(8,128)(2,1)} %refs_0_.2, bf16[512,1024]{1,0:T(8,128)(2,1)} %copy-done.20, bf16[512,1024]{1,0:T(8,128)(2,1)} %copy-done.19, ...), custom_call_target="tpu_custom_call" | custom-call | flops 1048576 | bytes 65536 | tf_op jit(solution)/shard_map/self_backward/pallas_call | solution.py:301
  584.6 7.1 %collective-permute-done.43 = bf16[3,32,1024]{2,1,0:T(8,128)(2,1)S(1)} collective-permute-done((bf16[3,32,1024]{2,1,0:T(8,128)(2,1)S(1)}, bf16[3,32,1024]{2,1,0:T(8,128)(2,1)S(1)}, u32[]{:S(2)}, u32[]{:S(2)}) %collective-permute-start.43) | collective-permute-done | bytes 196640 | tf_op jit(solution)/shard_map/ppermute | solution.py:475
  592.4 6.3 all-to-all-start.6
  615.5 13.5 %collective-permute-done.49 = bf16[1,3,32,1024]{3,2,1,0:T(8,128)(2,1)S(1)} collective-permute-done((bf16[1,3,32,1024]{3,2,1,0:T(8,128)(2,1)S(1)}, bf16[1,3,32,1024]{3,2,1,0:T(8,128)(2,1)S(1)}, u32[]{:S(2)}, u32[]{:S(2)}) %collective-permute-start.49) | collective-permute-done | bytes 196640 | tf_op jit(solution)/shard_map/ppermute | solution.py:403
  629.1 7.9 %collective-permute-done.48 = bf16[2,128,1024]{2,1,0:T(8,128)(2,1)S(1)} collective-permute-done((bf16[2,128,1024]{2,1,0:T(8,128)(2,1)S(1)}, bf16[2,128,1024]{2,1,0:T(8,128)(2,1)S(1)}, u32[]{:S(2)}, u32[]{:S(2)}) %collective-permute-start.48) | collective-permute-done | bytes 524320 | tf_op jit(solution)/shard_map/ppermute | solution.py:403
  640.2 4.7 all-to-all-start.7
  650.6 8.5 %bitcast_add_fusion = f32[512,1024]{1,0:T(8,128)} fusion(f32[512,1024]{1,0:T(8,128)S(1)} %copy-done.23, bf16[8,2,192,1024]{3,2,1,0:T(8,128)(2,1)} %bitcast.442, f32[512]{0:T(512)S(1)} %negate_multiply_fusion, bf16[8,1,192,512]{3,2,0,1:T(8,128)(2,1)} %bitcast.116, bf16[8,1,192,512]{3,2,0,1:T(8,128)(2,1)} %bitcast.115), kind=kOutput, calls=%fused_computation.34 | convolution fusion | flops 3223846912 | bytes 13633536 | tf_op jit(solution)/shard_map/dot_general | solution.py:33
  (546 shorter events, 309.3 us)
Async XLA Ops:
  7.2 35.5 %collective-permute-start = (bf16[512,1024]{1,0:T(8,128)(2,1)}, bf16[512,1024]{1,0:T(8,128)(2,1)S(1)}, u32[]{:S(2)}, u32[]{:S(2)}) collective-permute-start(bf16[512,1024]{1,0:T(8,128)(2,1)} %refs_0_.2), channel_id=1, source_target_pairs={{0,2},{2,4},{4,6},{6,0},{1,3},{3,5},{5,7},{7,1},{8,10},{10,12},{12... | collective-permute-start | bytes 3145736 | tf_op jit(solution)/shard_map/ppermute | solution.py:495
  19.3 112.0 %all-gather.7.cloned.1.call-start = ((), (), s32[]{:S(2)}) async-start(), calls=%async_computation.12 | async-start | bytes 2293760 | tf_op jit(solution)/shard_map/all_gather | solution.py:609
  45.0 89.2 %all-gather.9.cloned.1.call-start = ((), (), s32[]{:S(2)}) async-start(), calls=%async_computation.13 | async-start | bytes 1179648 | tf_op jit(solution)/shard_map/all_gather | solution.py:499
  45.1 43.4 %collective-permute-start.3 = (bf16[512,1024]{1,0:T(8,128)(2,1)S(1)}, bf16[512,1024]{1,0:T(8,128)(2,1)}, u32[]{:S(2)}, u32[]{:S(2)}) collective-permute-start(bf16[512,1024]{1,0:T(8,128)(2,1)S(1)} %collective-permute-done.refs_2_), channel_id=1, source_target_pairs={{0,2},{2,4},{4,6},{6,0},{1,3},{3,5},{5,7},{7,1},{8,10},{10,12},{12... | collective-permute-start | bytes 3145736 | tf_op jit(solution)/shard_map/ppermute | solution.py:495
  45.2 43.3 %collective-permute-start.7 = (bf16[512,1024]{1,0:T(8,128)(2,1)S(1)}, bf16[512,1024]{1,0:T(8,128)(2,1)}, u32[]{:S(2)}, u32[]{:S(2)}) collective-permute-start(bf16[512,1024]{1,0:T(8,128)(2,1)S(1)} %collective-permute-done.refs_2_), channel_id=1, source_target_pairs={{0,1},{1,0},{2,3},{3,2},{4,5},{5,4},{6,7},{7,6},{8,9},{9,8},{10,11... | collective-permute-start | bytes 3145736 | tf_op jit(solution)/shard_map/ppermute | solution.py:403
  88.5 118.3 %all-gather.11.cloned.1.call-start = ((), (), s32[]{:S(2)}) async-start(), calls=%async_computation.14 | async-start | bytes 1310720 | tf_op jit(solution)/shard_map/all_gather | solution.py:629
  88.6 42.7 %collective-permute-start.8 = (bf16[512,1024]{1,0:T(8,128)(2,1)}, bf16[512,1024]{1,0:T(8,128)(2,1)}, u32[]{:S(2)}, u32[]{:S(2)}) collective-permute-start(bf16[512,1024]{1,0:T(8,128)(2,1)} %collective-permute-done.3.refs_4_), channel_id=1, source_target_pairs={{0,2},{2,4},{4,6},{6,0},{1,3},{3,5},{5,7},{7,1},{8,10},{10,12},{12... | collective-permute-start | bytes 3145736 | tf_op jit(solution)/shard_map/ppermute | solution.py:495
  92.7 38.6 %collective-permute-start.9 = (bf16[512,1024]{1,0:T(8,128)(2,1)}, bf16[512,1024]{1,0:T(8,128)(2,1)}, u32[]{:S(2)}, u32[]{:S(2)}) collective-permute-start(bf16[512,1024]{1,0:T(8,128)(2,1)} %collective-permute-done.3.refs_4_), channel_id=1, source_target_pairs={{0,1},{1,0},{2,3},{3,2},{4,5},{5,4},{6,7},{7,6},{8,9},{9,8},{10,11... | collective-permute-start | bytes 3145736 | tf_op jit(solution)/shard_map/ppermute | solution.py:403
  137.2 36.4 %collective-permute-start.12 = (bf16[4,96,1024]{2,1,0:T(8,128)(2,1)S(1)}, bf16[4,96,1024]{2,1,0:T(8,128)(2,1)}, u32[]{:S(2)}, u32[]{:S(2)}) collective-permute-start(bf16[4,96,1024]{2,1,0:T(8,128)(2,1)S(1)} %slice.246), channel_id=1, source_target_pairs={{0,16},{8,24},{16,0},{24,8},{1,17},{9,25},{17,1},{25,9},{2,18},{10... | collective-permute-start | bytes 2359304 | tf_op jit(solution)/shard_map/ppermute | solution.py:403
  138.8 34.9 %collective-permute-start.13 = (bf16[4,96,1024]{2,1,0:T(8,128)(2,1)S(1)}, bf16[4,96,1024]{2,1,0:T(8,128)(2,1)}, u32[]{:S(2)}, u32[]{:S(2)}) collective-permute-start(bf16[4,96,1024]{2,1,0:T(8,128)(2,1)S(1)} %slice.246), channel_id=1, source_target_pairs={{0,24},{8,16},{16,8},{24,0},{1,25},{9,17},{17,9},{25,1},{2,26},{10... | collective-permute-start | bytes 2359304 | tf_op jit(solution)/shard_map/ppermute | solution.py:403
  140.0 93.5 %all-gather.15.cloned.1.call-start = ((), (), s32[]{:S(2)}) async-start(), calls=%async_computation.20 | async-start | bytes 2359296 | tf_op jit(solution)/shard_map/all_gather | solution.py:665
  177.7 36.4 %collective-permute-start.14 = (bf16[4,4,96,1024]{3,2,1,0:T(8,128)(2,1)}, bf16[4,4,96,1024]{3,2,1,0:T(8,128)(2,1)}, u32[]{:S(2)}, u32[]{:S(2)}) collective-permute-start(bf16[4,4,96,1024]{3,2,1,0:T(8,128)(2,1)} %pad_maximum_fusion), channel_id=1, source_target_pairs={{0,1},{1,0},{2,3},{3,2},{4,5},{5,4},{6,7},{7,6},{8,9},{9,8},{10,11... | collective-permute-start | bytes 9437192 | tf_op jit(solution)/shard_map/ppermute | solution.py:403
  214.2 40.8 %collective-permute-start.17 = (bf16[1024,512]{0,1:T(8,128)(2,1)}, bf16[1024,512]{0,1:T(8,128)(2,1)}, u32[]{:S(2)}, u32[]{:S(2)}) collective-permute-start(bf16[1024,512]{0,1:T(8,128)(2,1)} %all-gather.11.cloned.1.call-done), channel_id=1, source_target_pairs={{0,8},{8,0},{16,24},{24,16},{1,9},{9,1},{17,25},{25,17},{2,10},{10... | collective-permute-start | bytes 3145736 | tf_op jit(solution)/shard_map/ppermute | solution.py:403
  215.7 47.5 %collective-permute-start.18 = (bf16[1024,512]{0,1:T(8,128)(2,1)}, bf16[1024,512]{0,1:T(8,128)(2,1)}, u32[]{:S(2)}, u32[]{:S(2)}) collective-permute-start(bf16[1024,512]{0,1:T(8,128)(2,1)} %all-gather.11.cloned.1.call-done), channel_id=1, source_target_pairs={{0,16},{8,24},{16,0},{24,8},{1,17},{9,25},{17,1},{25,9},{2,18},{10... | collective-permute-start | bytes 3145736 | tf_op jit(solution)/shard_map/ppermute | solution.py:403
  220.8 198.1 %all-gather.13.cloned.1.call-start = ((), (), s32[]{:S(2)}) async-start(), calls=%async_computation.15 | async-start | bytes 7077888 | tf_op jit(solution)/shard_map/all_gather | solution.py:499
  323.4 142.1 %reduce-scatter.5.cloned.1.call-start = ((), (), s32[]{:S(2)}) async-start(), calls=%async_computation.16 | async-start | bytes 1310720 | tf_op jit(solution)/shard_map/reduce_scatter | solution.py:722
  400.5 135.4 %reduce-scatter.9.cloned.1.call-start = ((), (), s32[]{:S(2)}) async-start(), calls=%async_computation.18 | async-start | bytes 2359296 | tf_op jit(solution)/shard_map/reduce_scatter | solution.py:734
  450.2 85.7 %reduce-scatter.7.cloned.1.call-start = ((), (), s32[]{:S(2)}) async-start(), calls=%async_computation.17 | async-start | bytes 1310720 | tf_op jit(solution)/shard_map/reduce_scatter | solution.py:803
  486.1 49.7 %all-to-all-start.4 = ((bf16[8,64,512]{2,1,0:T(8,128)(2,1)}), bf16[8,64,512]{2,1,0:T(8,128)(2,1)S(1)}, u32[]{:S(2)}, u32[]{:S(2)}) async-start(bf16[8,64,512]{2,1,0:T(8,128)(2,1)} %get-tuple-element.425), calls=%async_computation.6 | async-start | bytes 1048576 | tf_op jit(solution)/shard_map/all_to_all | solution.py:507
  491.0 44.8 %collective-permute-start.36 = (bf16[4,3,32,1024]{3,2,0,1:T(8,128)(2,1)}, bf16[4,3,32,1024]{3,2,0,1:T(8,128)(2,1)S(1)}, u32[]{:S(2)}, u32[]{:S(2)}) collective-permute-start(bf16[4,3,32,1024]{3,2,0,1:T(8,128)(2,1)} %get-tuple-element.269), channel_id=1, source_target_pairs={{0,8},{8,0},{16,24},{24,16},{1,9},{9,1},{17,25},{25,17},{2,10},{10... | collective-permute-start | bytes 2359304 | tf_op jit(solution)/shard_map/ppermute | solution.py:403
  491.7 44.1 %collective-permute-start.37 = (bf16[4,3,32,1024]{3,2,0,1:T(8,128)(2,1)}, bf16[4,3,32,1024]{3,2,0,1:T(8,128)(2,1)}, u32[]{:S(2)}, u32[]{:S(2)}) collective-permute-start(bf16[4,3,32,1024]{3,2,0,1:T(8,128)(2,1)} %get-tuple-element.270), channel_id=1, source_target_pairs={{0,16},{8,24},{16,0},{24,8},{1,17},{9,25},{17,1},{25,9},{2,18},{10... | collective-permute-start | bytes 2359304 | tf_op jit(solution)/shard_map/ppermute | solution.py:403
  493.0 42.8 %collective-permute-start.38 = (bf16[4,3,32,1024]{3,2,0,1:T(8,128)(2,1)}, bf16[4,3,32,1024]{3,2,0,1:T(8,128)(2,1)}, u32[]{:S(2)}, u32[]{:S(2)}) collective-permute-start(bf16[4,3,32,1024]{3,2,0,1:T(8,128)(2,1)} %get-tuple-element.271), channel_id=1, source_target_pairs={{0,24},{8,16},{16,8},{24,0},{1,25},{9,17},{17,9},{25,1},{2,26},{10... | collective-permute-start | bytes 2359304 | tf_op jit(solution)/shard_map/ppermute | solution.py:403
  494.5 41.3 %collective-permute-start.35 = (bf16[1,128,1024]{2,1,0:T(8,128)(2,1)S(1)}, bf16[1,128,1024]{2,1,0:T(8,128)(2,1)S(1)}, u32[]{:S(2)}, u32[]{:S(2)}) collective-permute-start(bf16[1,128,1024]{2,1,0:T(8,128)(2,1)S(1)} %bitcast.393), channel_id=1, source_target_pairs={{0,8},{8,0},{16,24},{24,16},{1,9},{9,1},{17,25},{25,17},{2,10},{10... | collective-permute-start | bytes 786440 | tf_op jit(solution)/shard_map/ppermute | solution.py:403
  495.2 39.9 %collective-permute-start.39 = (f32[14,1024]{1,0:T(8,128)S(1)}, f32[14,1024]{1,0:T(8,128)S(1)}, u32[]{:S(2)}, u32[]{:S(2)}) collective-permute-start(f32[14,1024]{1,0:T(8,128)S(1)} %add.529), channel_id=1, source_target_pairs={{0,8},{8,0},{16,24},{24,16},{1,9},{9,1},{17,25},{25,17},{2,10},{10... | collective-permute-start | bytes 172040 | tf_op jit(solution)/shard_map/ppermute | solution.py:403
  535.9 56.5 %all-to-all-start.5 = ((bf16[8,192,512]{2,1,0:T(8,128)(2,1)}), bf16[8,192,512]{2,1,0:T(8,128)(2,1)}, u32[]{:S(2)}, u32[]{:S(2)}) async-start(bf16[8,192,512]{2,1,0:T(8,128)(2,1)} %get-tuple-element.286), calls=%async_computation.8 | async-start | bytes 3145728 | tf_op jit(solution)/shard_map/all_to_all | solution.py:507
  541.2 42.4 %collective-permute-start.40 = (bf16[1,128,1024]{2,1,0:T(8,128)(2,1)S(1)}, bf16[1,128,1024]{2,1,0:T(8,128)(2,1)S(1)}, u32[]{:S(2)}, u32[]{:S(2)}) collective-permute-start(bf16[1,128,1024]{2,1,0:T(8,128)(2,1)S(1)} %reshape.819), channel_id=1, source_target_pairs={{0,8},{8,0},{16,24},{24,16},{1,9},{9,1},{17,25},{25,17},{2,10},{10... | collective-permute-start | bytes 786440 | tf_op jit(solution)/shard_map/ppermute | solution.py:403
  542.0 42.5 %collective-permute-start.41 = (bf16[2,128,1024]{2,1,0:T(8,128)(2,1)S(1)}, bf16[2,128,1024]{2,1,0:T(8,128)(2,1)S(1)}, u32[]{:S(2)}, u32[]{:S(2)}) collective-permute-start(bf16[2,128,1024]{2,1,0:T(8,128)(2,1)S(1)} %pad_maximum_fusion.23), channel_id=1, source_target_pairs={{0,16},{8,24},{16,0},{24,8},{1,17},{9,25},{17,1},{25,9},{2,18},{10... | collective-permute-start | bytes 1572872 | tf_op jit(solution)/shard_map/ppermute | solution.py:403
  545.9 38.8 %collective-permute-start.42 = (bf16[3,32,1024]{2,1,0:T(8,128)(2,1)S(1)}, bf16[3,32,1024]{2,1,0:T(8,128)(2,1)S(1)}, u32[]{:S(2)}, u32[]{:S(2)}) collective-permute-start(bf16[3,32,1024]{2,1,0:T(8,128)(2,1)S(1)} %get-tuple-element.439), channel_id=1, source_target_pairs={{0,2},{2,4},{4,6},{6,0},{1,3},{3,5},{5,7},{7,1},{8,10},{10,12},{12... | collective-permute-start | bytes 589832 | tf_op jit(solution)/shard_map/ppermute | solution.py:475
  547.9 43.8 %collective-permute-start.43 = (bf16[3,32,1024]{2,1,0:T(8,128)(2,1)S(1)}, bf16[3,32,1024]{2,1,0:T(8,128)(2,1)S(1)}, u32[]{:S(2)}, u32[]{:S(2)}) collective-permute-start(bf16[3,32,1024]{2,1,0:T(8,128)(2,1)S(1)} %get-tuple-element.438), channel_id=1, source_target_pairs={{0,4},{2,6},{4,0},{6,2},{1,5},{3,7},{5,1},{7,3},{8,12},{10,14},{12... | collective-permute-start | bytes 589832 | tf_op jit(solution)/shard_map/ppermute | solution.py:475
  550.3 42.1 %collective-permute-start.44 = (bf16[3,32,1024]{2,1,0:T(8,128)(2,1)S(1)}, bf16[3,32,1024]{2,1,0:T(8,128)(2,1)}, u32[]{:S(2)}, u32[]{:S(2)}) collective-permute-start(bf16[3,32,1024]{2,1,0:T(8,128)(2,1)S(1)} %get-tuple-element.437), channel_id=1, source_target_pairs={{0,6},{2,0},{4,2},{6,4},{1,7},{3,1},{5,3},{7,5},{8,14},{10,8},{12,... | collective-permute-start | bytes 589832 | tf_op jit(solution)/shard_map/ppermute | solution.py:475
  592.4 45.5 %all-to-all-start.6 = ((bf16[8,192,512]{2,1,0:T(8,128)(2,1)}), bf16[8,192,512]{2,1,0:T(8,128)(2,1)}, u32[]{:S(2)}, u32[]{:S(2)}) async-start(bf16[8,192,512]{2,1,0:T(8,128)(2,1)} %get-tuple-element.288), calls=%async_computation.9 | async-start | bytes 3145728 | tf_op jit(solution)/shard_map/all_to_all | solution.py:507
  644.9 42.0 %reduce-scatter.11.cloned.1.call-start = ((), (), s32[]{:S(2)}) async-start(), calls=%async_computation.19 | async-start | bytes 1179648 | tf_op jit(solution)/shard_map/reduce_scatter | solution.py:503
  (137 other events, 1815.7 us)
Sparse Core Ops, SparseCore 0:
  45.2 60.5 all-gather.6
  107.3 26.8 all-gather.8
  140.2 29.0 all-gather.10
  177.9 38.9 all-gather.14
  323.5 62.3 all-gather.12
  400.6 25.0 reduce-scatter.4
  438.6 39.0 reduce-scatter.8
  486.2 36.9 reduce-scatter.6
  650.7 32.1 reduce-scatter.10
